TPU v7x, 32 devices: a whole 2x2x4 slice. The times are simulated.
32 devices in a mesh: group: 2 (over y), chan: 4 (over z), stat: 2 (over x), pol: 2 (over core).
Axes of the slice: x: 2, y: 2, z: 4, core: 2. Of those that a mesh axis runs over, the one named last changes fastest.
Arguments:
- voltages: bfloat16 [4, 16, 2, 19, 2, 4096], P(('group', 'stat'), 'chan', 'pol'), parts along dimension 0, may hold values from -6 to 6
- filter_taps: float32 [12, 4096], replicated, may hold values from -1.5 to 1.5
- beam_table: float32 [2, 16], replicated, may hold values from -4 to 4
- beam_index: int32 [500, 32], replicated, may hold values from 0 to 15
- block_owner: int32 [32], replicated, may hold values from 0 to 31, each once
Outputs:
- visibilities: float32 [64, 2, 64, 64], P(('group', 'chan'), None, ('stat', 'pol')), parts along dimension 0
- beams: float32 [1000, 2, 2, 8, 4096], P(('group', 'stat'), 'pol', None, None, 'chan'), parts along dimension 0
There are 2 independent parts, one for each index of `group`. A program takes and returns all parts, laid end to end along the dimension named above; an argument that names none is the same for every part. Nothing has to cross between parts.
Inputs may be any that keep to these rules, and one draw needn't show every extreme that they name: `block_owner`: each of the 32 channel groups appears at exactly one position.
All inputs are finite; a program needn't handle non-finite values.
Results may differ from a plain program's by a relative error of at most 0.0095.
Values may be sent and summed in bfloat16 or wider, within the bound.
No kernel may reach another device: no remote copies, remote signals or barrier semaphores. Data moves between devices by JAX's collectives and lax.ppermute only.
A program may use at most 64 MiB of HBM per device.

v0:
```python
import math

import jax
import jax.numpy as jnp
from jax import lax
from jax.sharding import PartitionSpec as P

ROOT = 64
AVG = 128


def fourier_segment(length):
    counter = jnp.arange(length, dtype=jnp.int32)
    phase = (counter[:, None] * counter[None, :] % length).astype(jnp.float32) * (
        2.0 * math.pi / length
    )
    cosine = jnp.cos(phase)
    sine = jnp.sin(phase)
    upper_half = jnp.stack([cosine, -sine], axis=1)
    lower_half = jnp.stack([sine, cosine], axis=1)
    return jnp.stack([upper_half, lower_half], axis=0)


def channelise(voltages, filter_taps):
    samples = voltages[0, :, 0].astype(jnp.float32)
    taps_count = filter_taps.shape[0]
    frames = samples.shape[1] - taps_count + 1
    filtered = filter_taps[0] * samples[:, 0:frames]
    for tap_index in range(1, taps_count):
        filtered = filtered + filter_taps[tap_index] * samples[:, tap_index : tap_index + frames]
    stations = samples.shape[0]
    shaped = filtered.reshape(stations, frames, 2, ROOT, ROOT)
    matrix = fourier_segment(ROOT)
    segment_one = jnp.einsum("sfcxy,cxdk->sfdky", shaped, matrix, precision=lax.Precision.HIGHEST)
    counter = jnp.arange(ROOT, dtype=jnp.int32)
    twiddle = (counter[:, None] * counter[None, :]).astype(jnp.float32) * (
        2.0 * math.pi / (ROOT * ROOT)
    )
    twiddle_cos = jnp.cos(twiddle)
    twiddle_sin = jnp.sin(twiddle)
    turned_real = segment_one[:, :, 0] * twiddle_cos + segment_one[:, :, 1] * twiddle_sin
    turned_imag = segment_one[:, :, 1] * twiddle_cos - segment_one[:, :, 0] * twiddle_sin
    turned = jnp.stack([turned_real, turned_imag], axis=2)
    segment_two = jnp.einsum("sfcky,cydz->sdfzk", turned, matrix, precision=lax.Precision.HIGHEST)
    return (segment_two.reshape(stations, 2, frames, ROOT * ROOT) * (1.0 / ROOT)).astype(
        jnp.bfloat16
    )


def beam_weights(indices, beam_table, factor):
    levels = jnp.arange(beam_table.shape[1], dtype=jnp.int32)
    selected = indices[..., None] == levels
    w_real = jnp.sum(jnp.where(selected, beam_table[0], 0.0), axis=-1) * factor
    w_imag = jnp.sum(jnp.where(selected, beam_table[1], 0.0), axis=-1) * factor
    upper_half = jnp.stack([w_real, -w_imag], axis=1)
    lower_half = jnp.stack([w_imag, w_real], axis=1)
    return jnp.stack([upper_half, lower_half], axis=1).astype(jnp.bfloat16)


def on_device(voltages, filter_taps, beam_table, beam_index, block_owner):
    spectra = channelise(voltages, filter_taps)
    stations = spectra.shape[0]
    frames = spectra.shape[2]
    nfft_total = spectra.shape[3]
    owners = lax.axis_size("chan")
    chan_width = nfft_total // owners
    group_count = block_owner.shape[0]
    grouped = spectra.reshape(stations, 2, frames, group_count, nfft_total // group_count)
    regrouped = jnp.take(grouped, block_owner, axis=3)
    ordered = regrouped.reshape(stations, 2, frames, owners, chan_width)
    exchanged = lax.all_to_all(ordered, "chan", split_axis=3, concat_axis=0, tiled=True)
    local_spectra = exchanged.reshape(-1, 2, frames, chan_width)
    section_rows = local_spectra.shape[0]
    sections = lax.axis_size("stat")
    input_count = section_rows * 2 * sections
    groups = chan_width // AVG
    mean_factor = 1.0 / (frames * AVG)
    own_rows = local_spectra.reshape(section_rows, 2, frames, groups, AVG)
    section = lax.axis_index("stat")
    polarity = lax.axis_index("pol")
    station_count = beam_index.shape[1]
    beam_count = beam_index.shape[0]
    owned_beams = beam_count // sections
    norm_factor = 1.0 / math.sqrt(station_count)
    own_index = lax.dynamic_slice_in_dim(beam_index, section * owned_beams, owned_beams, 0)
    own_weights = beam_weights(own_index, beam_table, norm_factor)
    spread = own_weights.reshape(owned_beams, 2, 2, sections, 1, section_rows)
    chosen = (jnp.arange(2, dtype=jnp.int32) == polarity).reshape(1, 1, 1, 1, 2, 1)
    spread = jnp.where(chosen, spread, jnp.zeros((), jnp.bfloat16))
    wide_weights = spread.reshape(owned_beams, 2, 2, input_count)
    shard_rows = lax.all_gather(local_spectra, ("stat", "pol"), axis=0, tiled=True)
    piece_rows = shard_rows.shape[0]
    beam_term = jnp.einsum(
        "bocj,jcq->boq",
        wide_weights,
        shard_rows.reshape(piece_rows, 2, -1),
        preferred_element_type=jnp.float32,
    )
    piece_rows = shard_rows.shape[0]
    rotated = jnp.concatenate([-shard_rows[:, 1:2], shard_rows[:, 0:1]], axis=1)
    their_rows = shard_rows.reshape(piece_rows, 2, frames, groups, AVG)
    their_turned = rotated.reshape(piece_rows, 2, frames, groups, AVG)
    real_part = jnp.einsum(
        "icfam,jcfam->aij", own_rows, their_rows, preferred_element_type=jnp.float32
    )
    imag_part = jnp.einsum(
        "icfam,jcfam->aij", own_rows, their_turned, preferred_element_type=jnp.float32
    )
    vis_block = jnp.stack([real_part, imag_part], axis=1) * mean_factor
    return (vis_block, beam_term.reshape(owned_beams, 1, 2, frames, chan_width))


def solution(mesh):
    return jax.shard_map(
        on_device,
        mesh=mesh,
        in_specs=(P(("group", "stat"), "chan", "pol", None, None, None), P(), P(), P(), P()),
        out_specs=(
            P(("group", "chan"), None, ("stat", "pol"), None),
            P(("group", "stat"), "pol", None, None, "chan"),
        ),
        check_vma=False,
    )
```

profile of v0, /device:TPU:0, one launch (start us, length us, event | category | flops | bytes accessed | tf_op | source)
XLA Modules:
  0.0 116.7 jit_solution(14907172509124150411)
XLA Ops:
  7.2 0.7 compare_and_fusion
  7.9 0.7 compare_select_fusion
  9.2 2.1 %fusion.46 = (f32[1,4096]{1,0:T(1,128)S(1)}, f32[1,4096]{1,0:T(1,128)S(1)}, f32[1,4096]{1,0:T(1,128)S(1)}, f32[1,4096]{1,0:T(1,128)S(1)}, f32[1,4096]{1,0:T(1,12...) fusion(f32[12,4096]{1,0:T(8,128)} %param.6), kind=kLoop, calls=%fused_computation.89 | loop fusion | bytes 393216 | tf_op jit(solution)/shard_map/slice | solution.py:28
  11.3 2.4 %bitcast_convert_fusion = f32[4,19,2,4096]{3,2,1,0:T(2,128)S(1)} fusion(bf16[1,4,1,19,2,4096]{5,4,3,2,1,0:T(2,128)(2,1)} %param.5), kind=kLoop, calls=%fused_computation.17 | loop fusion | flops 622592 | bytes 3735552 | tf_op jit(solution)/shard_map/convert_element_type | solution.py:25
  13.6 6.6 %fusion.20 = f32[4,8,2,4096]{3,2,1,0:T(2,128)S(1)} fusion(f32[4,19,2,4096]{3,2,1,0:T(2,128)S(1)} %bitcast_convert_fusion, f32[4096]{0:T(1024)S(1)} %bitcast.152, f32[4096]{0:T(1024)S(1)} %bitcast.153, f32[4096]{0:T(1024)S(1)} %bitcast.143, f32[4096]{0:T(1024)S(1)} %bitcast.144, f32[4096]{0:T(1024)S(1)} %bitcast.145, f32[4096]{0:T(1024)S(1)} %bitcast.146, ...), kind=kLoop, calls=%fused_computation.22 | loop fusion | flops 6029312 | bytes 13828096 | tf_op jit(solution)/shard_map/add | solution.py:30
  20.3 1.2 %reshape.261 = f32[4,8,2,64,64,1]{4,3,2,1,0,5:T(8,128)S(1)} reshape(f32[4,8,2,4096]{3,2,1,0:T(2,128)S(1)} %fusion.20) | data formatting | bytes 2097152 | tf_op jit(solution)/shard_map/reshape | solution.py:32
  21.5 2.0 %convolution_bitcast_fusion.1 = f32[4,8,2,64,64]{4,3,1,0,2:T(8,128)S(1)} fusion(f32[4,8,2,64,64,1]{4,3,2,1,0,5:T(8,128)S(1)} %reshape.261, f32[1,64,2,64]{1,3,0,2:T(8,128)S(1)} %get-tuple-element.33, f32[1,64,2,64]{1,3,0,2:T(8,128)S(1)} %get-tuple-element.32), kind=kOutput, calls=%fused_computation.15 | convolution fusion | flops 402669568 | bytes 2162688 | tf_op jit(solution)/shard_map/sfcxy,cxdk->sfdky/dot_general | solution.py:34
  23.4 0.4 multiply_add_fusion
  23.9 3.1 %fusion.11 = bf16[4,2,8,64,64]{4,3,2,0,1:T(8,128)(2,1)S(1)} fusion(f32[1,64,2,64]{1,3,0,2:T(8,128)S(1)} %get-tuple-element.33, f32[1,64,2,64]{1,3,0,2:T(8,128)S(1)} %get-tuple-element.32, f32[4,8,1,64,64]{4,3,1,0,2:T(8,128)S(1)} %get-tuple-element.15, f32[4,8,1,64,64]{4,3,1,0,2:T(8,128)S(1)} %get-tuple-element.14), kind=kOutput, calls=%fused_computation.16 | convolution fusion | flops 403456000 | bytes 1638400 | tf_op jit(solution)/shard_map/sfcky,cydz->sdfzk/dot_general | solution.py:44
  27.0 0.5 convert_element_type.67
  27.7 0.8 gather_fusion
  29.4 20.7 %all_to_all.15 = bf16[4,2,8,4,1024]{4,2,1,0,3:T(8,128)(2,1)} all-to-all(bf16[4,2,8,4,1024]{4,2,1,0,3:T(8,128)(2,1)S(1)} %copy.57), channel_id=1, replica_groups=mesh['group'=2,'chan'=4,'stat'=2,'pol'=2] {'chan'}, dimensions={3} | all-to-all | bytes 1048576 | tf_op jit(solution)/shard_map/all_to_all | solution.py:71
  50.7 1.1 copy.77
  51.9 20.1 %all-gather.2.cloned.1.call-done = bf16[64,2,8,1024]{3,2,1,0:T(8,128)(2,1)} async-done(((bf16[16,2,8,1024]{3,2,1,0:T(8,128)(2,1)}), bf16[64,2,8,1024]{3,2,1,0:T(8,128)(2,1)}) %all-gather.2.cloned.1.call-update) | async-done | bytes 2097168 | tf_op jit(solution)/shard_map/all_gather | solution.py:91
  72.0 3.7 %copy.78 = bf16[128,8,8,128]{3,2,1,0:T(8,128)(2,1)} copy(bf16[128,8,8,128]{3,1,2,0:T(8,128)(2,1)} %bitcast.129) | data formatting | bytes 4194304
  75.7 2.7 %reshape.245 = bf16[64,2,8192]{2,1,0:T(2,128)(2,1)} reshape(bf16[64,2,8,1024]{3,2,1,0:T(8,128)(2,1)S(1)} %copy-done.1) | data formatting | bytes 4194304 | tf_op jit(solution)/shard_map/reshape | solution.py:96
  78.4 2.7 %copy.64 = bf16[64,2,8192]{2,0,1:T(8,128)(2,1)S(1)} copy(bf16[64,2,8192]{2,1,0:T(2,128)(2,1)} %reshape.245) | data formatting | bytes 4194304 | tf_op jit(solution)/shard_map/reshape | solution.py:96
  81.5 0.6 copy.79
  82.2 0.9 copy-done.2
  83.1 1.5 %fusion.14 = f32[8,1,16,64]{3,2,0,1:T(8,128)S(1)} fusion(bf16[64,2,8,8,128]{4,3,2,1,0:T(8,128)(2,1)S(1)} %bitcast.134, bf16[16,2,8,8,128]{4,3,2,1,0:T(8,128)(2,1)S(1)} %bitcast.138), kind=kOutput, calls=%fused_computation.18 | convolution fusion | flops 33554432 | bytes 2654208 | tf_op jit(solution)/shard_map/icfam,jcfam->aij/dot_general | solution.py:103
  84.6 1.5 %fusion.17 = f32[8,1,16,64]{3,2,0,1:T(8,128)S(1)} fusion(bf16[64,2,8,8,128]{4,3,2,1,0:T(8,128)(2,1)S(1)} %bitcast.135, bf16[16,2,8,8,128]{4,3,2,1,0:T(8,128)(2,1)S(1)} %bitcast.139), kind=kOutput, calls=%fused_computation.19 | convolution fusion | flops 33554432 | bytes 2654208 | tf_op jit(solution)/shard_map/icfam,jcfam->aij/dot_general | solution.py:106
  86.1 0.7 copy.66
  86.7 2.4 %convolution_bitcast_fusion = f32[250,1,2,8,1024]{4,0,3,2,1:T(8,128)S(1)} fusion(bf16[250,2,2,64,1]{0,3,2,4,1:T(8,128)(2,1)S(1)} %bitcast.137, bf16[2,8,8,8,1024]{4,3,2,1,0:T(8,128)(2,1)S(1)} %bitcast.130), kind=kOutput, calls=%fused_computation.1 | convolution fusion | flops 1048576000 | bytes 18609152 | tf_op jit(solution)/shard_map/bocj,jcq->boq/dot_general | solution.py:93
  89.1 20.8 %copy.67 = f32[250,1,2,8,1024]{4,3,2,1,0:T(8,128)} copy(f32[250,1,2,8,1024]{4,0,3,2,1:T(8,128)S(1)} %convolution_bitcast_fusion) | data formatting | bytes 32768000
  (34 shorter events, 2.6 us)
Async XLA Ops:
  7.2 43.0 %copy-start = (s32[500,32]{0,1:T(8,128)S(1)}, s32[500,32]{0,1:T(8,128)}, u32[]{:S(2)}) copy-start(s32[500,32]{0,1:T(8,128)} %param.8) | copy-start | bytes 192004
  7.2 64.8 %all-gather.2.cloned.1.call-start = ((), (), s32[]{:S(2)}) async-start(), calls=%async_computation.1 | async-start | bytes 2621440 | tf_op jit(solution)/shard_map/all_gather | solution.py:91
  29.0 21.3 %copy-start.3 = (f32[2,16]{1,0:T(2,128)S(1)}, f32[2,16]{1,0:T(2,128)}, u32[]{:S(2)}) copy-start(f32[2,16]{1,0:T(2,128)} %param.7) | copy-start | bytes 388
  72.0 3.7 %copy-start.1 = (bf16[64,2,8,1024]{3,2,1,0:T(8,128)(2,1)S(1)}, bf16[64,2,8,1024]{3,2,1,0:T(8,128)(2,1)}, u32[]{:S(2)}) copy-start(bf16[64,2,8,1024]{3,2,1,0:T(8,128)(2,1)} %all-gather.2.cloned.1.call-done) | copy-start | bytes 6291460
  81.5 1.6 %copy-start.2 = (bf16[128,8,8,128]{3,2,1,0:T(8,128)(2,1)S(1)}, bf16[128,8,8,128]{3,2,1,0:T(8,128)(2,1)}, u32[]{:S(2)}) copy-start(bf16[128,8,8,128]{3,2,1,0:T(8,128)(2,1)} %copy.78) | copy-start | bytes 6291460
Sparse Core Ops, SparseCore 0:
  50.3 21.6 all-gather.1
where the time goes:
time: 117 us
  local copies, waits for them, and re-layouts  39 us (33%)
  blocking collectives  20.7 us (18%)
  waiting for transfers between devices  20.1 us (17%)
  between operations  14.3 us (12%)
  other arithmetic  12.2 us (10%)
  matrix products  10.4 us (9%)
    unnamed x15, local copies, waits for them, and re-layouts  27.9 us
    all_to_all x1, blocking collectives, on_device(): lax.all_to_all(ordered, 'chan', split_axis=3, concat_axis=0, tiled=True)  20.7 us
    all_gather x1, waiting for transfers between devices, on_device(): lax.all_gather(local_spectra, ('stat', 'pol'), axis=0, tiled=True)  20.1 us
    add x1, other arithmetic, channelise(): filtered + filter_taps[tap_index] * samples[:, tap_index:tap_index + frames]  6.62 us
    reshape x2, local copies, waits for them, and re-layouts, on_device(): shard_rows.reshape(piece_rows, 2, -1)  5.49 us
    dot_general x1, matrix products, channelise(): jnp.einsum('sfcky,cydz->sdfzk', turned, matrix, precision=lax.Precision.H...  3.13 us
    dot_general x1, matrix products, on_device(): jnp.einsum('bocj,jcq->boq', wide_weights, shard_rows.reshape(piece_rows,...  2.37 us
    convert_element_type x1, other arithmetic, channelise(): samples = voltages[0, :, 0].astype(jnp.float32)  2.36 us
  transfers between devices with their start and end apart: 1, of which 1 were waited for; matrix products, arithmetic and copies ran while one was open for 1% of the time, Pallas kernels for 0%

commit v1 on v0

v1 whole, which is shorter than its diff:
```python
import functools, math
import jax, jax.numpy as jnp, numpy as np
from jax import lax
from jax.experimental import pallas as pl
from jax.experimental.pallas import tpu as pltpu
from jax.sharding import PartitionSpec as P

LANES = 128
HALF = 4

def dft_parts(rows, cols, length):
    phase = np.outer(np.arange(rows), np.arange(cols)) % length * (2.0 * np.pi / length)
    return np.cos(phase), np.sin(phase)


def channel_tables(nfft, frames, groups):
    depth = nfft // LANES
    per_group = LANES // depth
    cosine, sine = dft_parts(depth, depth, depth)
    pair = np.stack([np.stack([cosine, sine], -1), np.stack([-sine, cosine], -1)])
    first = np.einsum("akrc,fg->afkgrc", pair, np.eye(HALF))
    first = first.reshape(2 * HALF * depth, HALF * depth * 2)
    turn_cos, turn_sin = dft_parts(depth, LANES, nfft)
    cosine, sine = dft_parts(LANES, LANES, LANES)
    order = (np.arange(groups)[None, :] * per_group + np.arange(per_group)[:, None]).reshape(-1)
    cosine, sine = cosine[order] / math.sqrt(nfft), sine[order] / math.sqrt(nfft)
    second = np.concatenate([np.concatenate([cosine, sine], 1), np.concatenate([-sine, cosine], 1)], 0)
    spread = np.einsum("qr,fg,kl->qfkgrl", np.eye(per_group), np.eye(HALF), np.eye(depth))
    spread = spread.reshape(per_group * HALF * depth, HALF * per_group * depth)
    bf = lambda x: jnp.asarray(x, jnp.bfloat16)
    return bf(first), jnp.asarray(np.stack([turn_cos, turn_sin]), jnp.float32), bf(second), bf(spread)


def channel_kernel(owners, owner_ref, volt_ref, taps_ref, first_ref, turn_ref, second_ref, spread_ref, *rest):
    outs = rest[:owners]
    volts, tap_rows, first, turn, second, spread, filt, wide, pick, sems = rest[owners:]
    stations, blocks, rows, _ = volt_ref.shape
    taps = taps_ref.shape[0]
    frames = blocks - taps + 1
    halves = frames // HALF
    depth = rows // 2
    groups = owner_ref.shape[0]
    width = groups // owners
    quads = LANES // depth
    span = HALF * depth
    here = lax.axis_index("chan")
    copies = []
    for s in range(stations):
        copies.append(pltpu.make_async_copy(volt_ref.at[s], volts.at[s], sems.at[s]))
    consts = []
    for i, (src, dst) in enumerate([(first_ref, first), (turn_ref, turn), (second_ref, second), (spread_ref, spread)]):
        consts.append(pltpu.make_async_copy(src, dst, sems.at[stations + i]))
    for c in copies + consts:
        c.start()

    sub = lax.broadcasted_iota(jnp.int32, (8, LANES), 0)
    for t in range(taps):
        for m in range(rows // 8):
            parts = [jnp.broadcast_to(taps_ref[t : t + 1, pl.ds((4 * m + i) * LANES, LANES)], (8, LANES)) for i in range(4)]
            low = jnp.where(sub < 2, parts[0], parts[1])
            high = jnp.where(sub < 6, parts[2], parts[3])
            tap_rows[t, pl.ds(8 * m, 8), :] = jnp.where(sub < 4, low, high)

    sc = 2 * stations
    lane = lax.broadcasted_iota(jnp.int32, (sc, sc * groups), 1)
    base = lax.broadcasted_iota(jnp.int32, (sc, sc * groups), 0) * groups
    for k in range(owners):
        for j in range(width):
            g = owner_ref[(here ^ k) * width + j]
            p = (k * width + j) * sc
            pick[pl.ds(p, sc), :] = jnp.where(lane == base + g, 1.0, 0.0).astype(jnp.bfloat16)

    step = 16
    for s in range(stations):
        copies[s].wait()

        def fir(m, carry, s=s):
            at = pl.multiple_of(m * step, step)
            x = [volts[s, b, pl.ds(at, step), :].astype(jnp.float32) for b in range(blocks)]
            w = [tap_rows[t, pl.ds(at, step), :] for t in range(taps)]
            for f in range(frames):
                total = w[0] * x[f]
                for t in range(1, taps):
                    total = total + w[t] * x[f + t]
                row = pl.multiple_of((f % HALF) * rows + at, step)
                filt[s, pl.ds(row, step), pl.ds((f // HALF) * LANES, LANES)] = total.astype(jnp.bfloat16)
            return carry

        lax.fori_loop(0, rows // step, fir, 0)

    for c in consts:
        c.wait()
    f32 = jnp.float32
    cosine = jnp.concatenate([turn[0]] * HALF, 0)
    sine = jnp.concatenate([turn[1]] * HALF, 0)
    for s in range(stations):
        y = jnp.dot(first[...], filt[s], preferred_element_type=f32)
        re, im = y[:span], y[span:]
        turned = []
        for h in range(halves):
            a, b = re[:, h * LANES : (h + 1) * LANES], im[:, h * LANES : (h + 1) * LANES]
            turned.append(jnp.concatenate([a * cosine + b * sine, b * cosine - a * sine], 1))
        turned = jnp.concatenate(turned, 0).astype(jnp.bfloat16)
        z = lax.dot_general(second[...], turned, (((1,), (1,)), ((), ())), preferred_element_type=f32).astype(jnp.bfloat16)
        for c in range(2):
            for q in range(quads):
                for h in range(halves):
                    wide[h, pl.ds((s * 2 + c) * groups, groups), pl.ds(q * LANES, LANES)] = z[
                        c * quads * groups + q * groups : c * quads * groups + (q + 1) * groups, h * LANES : (h + 1) * LANES
                    ]
    for h in range(halves):
        y = jnp.dot(wide[h], spread[...], preferred_element_type=f32).astype(jnp.bfloat16)
        z = jnp.dot(pick[...], y, preferred_element_type=f32)
        for k in range(owners):
            for j in range(width):
                for f in range(HALF):
                    p = (k * width + j) * sc
                    outs[k][pl.ds((h * HALF + f) * sc, sc), pl.ds(j * LANES, LANES)] = z[
                        p : p + sc, f * LANES : (f + 1) * LANES
                    ].astype(jnp.bfloat16)


def channelise(voltages, filter_taps, block_owner, owners):
    _, stations, _, blocks, _, nfft = voltages.shape
    taps = filter_taps.shape[0]
    frames = blocks - taps + 1
    groups = block_owner.shape[0]
    depth = nfft // LANES
    volts = voltages.reshape(stations, blocks, 2, depth, LANES).transpose(0, 1, 3, 2, 4).reshape(stations, blocks, 2 * depth, LANES)
    first, turn, second, spread = channel_tables(nfft, frames, groups)
    sc = 2 * stations
    width = groups // owners
    anyspec = pl.BlockSpec(memory_space=pl.ANY)
    bf = jnp.bfloat16
    return pl.pallas_call(
        functools.partial(channel_kernel, owners),
        out_shape=[jax.ShapeDtypeStruct((frames * sc, width * LANES), bf)] * owners,
        in_specs=[pl.BlockSpec(memory_space=pltpu.SMEM), anyspec, pl.BlockSpec(memory_space=pltpu.VMEM)] + [anyspec] * 4,
        out_specs=[pl.BlockSpec(memory_space=pltpu.VMEM)] * owners,
        scratch_shapes=[
            pltpu.VMEM(volts.shape, bf),
            pltpu.VMEM((taps, 2 * depth, LANES), jnp.float32),
            pltpu.VMEM(first.shape, bf),
            pltpu.VMEM(turn.shape, jnp.float32),
            pltpu.VMEM(second.shape, bf),
            pltpu.VMEM(spread.shape, bf),
            pltpu.VMEM((stations, HALF * 2 * depth, frames // HALF * LANES), bf),
            pltpu.VMEM((frames // HALF, sc * groups, spread.shape[0]), bf),
            pltpu.VMEM((groups * sc, sc * groups), bf),
            pltpu.SemaphoreType.DMA((stations + 4,)),
        ],
        name="channelise",
    )(block_owner, volts, filter_taps, first, turn, second, spread)


def pieces(total, most):
    return max(d for d in range(1, most + 1) if total % d == 0)


def weights_kernel(pairs, weight_ref, copy_ref, out_ref, rows_ref):
    count, columns = weight_ref.shape
    tile, spread = copy_ref.shape
    frames = spread // tile

    @pl.when(pl.program_id(0) == 0)
    def _():
        for i in range(columns // tile):
            rows_ref[:, i * spread : (i + 1) * spread] = jnp.dot(
                weight_ref[:, i * tile : (i + 1) * tile], copy_ref[...], preferred_element_type=jnp.float32
            )

    width = out_ref.shape[1]
    owned = lax.broadcasted_iota(jnp.int32, (frames, width), 1) // pairs % frames == lax.broadcasted_iota(
        jnp.int32, (frames, width), 0
    )
    share = out_ref.shape[0] // frames

    def fill(i, carry):
        row = rows_ref[pl.ds(pl.program_id(0) * share + i, 1), :]
        out_ref[pl.ds(pl.multiple_of(i * frames, frames), frames), :] = jnp.where(
            owned, jnp.broadcast_to(row, (frames, width)), 0.0
        ).astype(jnp.bfloat16)
        return carry

    lax.fori_loop(0, share, fill, 0, unroll=pieces(share, 10))


def framed_weights(weights, frames, pairs):
    count, columns = weights.shape
    tile = min(LANES, columns)
    copies = np.einsum("bc,pq,f->bpcfq", np.eye(tile // pairs), np.eye(pairs), np.ones(frames)).reshape(tile, tile * frames)
    share = pieces(count, 100)
    return pl.pallas_call(
        functools.partial(weights_kernel, pairs),
        grid=(count // share,),
        out_shape=jax.ShapeDtypeStruct((count * frames, columns * frames), jnp.bfloat16),
        in_specs=[
            pl.BlockSpec((count, columns), lambda i: (0, 0)),
            pl.BlockSpec((tile, tile * frames), lambda i: (0, 0)),
        ],
        out_specs=pl.BlockSpec((share * frames, columns * frames), lambda i: (i, 0)),
        scratch_shapes=[pltpu.VMEM((count, columns * frames), jnp.float32)],
        name="framed_weights",
    )(weights, jnp.asarray(copies, jnp.bfloat16))


def correlate_kernel(owners, sections, frames, *refs):
    per = owners
    mine = refs[:per]
    twin_ref = refs[per]
    others = refs[per + 1 : per + 1 + per * (sections - 1)]
    out_ref, cross_ref, packed = refs[per + 1 + per * (sections - 1) :]
    rows, lanes = mine[0].shape
    pairs = rows // frames
    width = lanes // LANES
    block = owners * pairs
    here, section, pol = lax.axis_index("chan"), lax.axis_index("stat"), lax.axis_index("pol")
    f32 = jnp.float32

    def put(slot, k, ref, first):
        for j in range(width):
            for f in range(frames):
                packed[j, pl.ds(slot * block + k * pairs, pairs), pl.ds(f * LANES, LANES)] = ref[
                    pl.ds(first + f * pairs, pairs), pl.ds(j * LANES, LANES)
                ]

    for k in range(owners):
        put(0, k, mine[k], 0)
        put(1, k, twin_ref, k * rows)
        for x in range(1, sections):
            put(1 + x, k, others[(x - 1) * owners + k], 0)
    slots = 1 + sections
    products = []
    for j in range(width):
        x = packed[j]
        products.append(
            lax.dot_general(x[: 2 * block], x, (((1,), (1,)), ((), ())), preferred_element_type=f32)
        )
    members = block // 2
    inputs = out_ref.shape[1]
    col = lax.broadcasted_iota(jnp.int32, (slots * block, 1), 0)
    slot, inner = col // block, col % block
    k, station, part = inner // pairs, inner % pairs // 2, inner % 2
    there = jnp.where(slot == 1, 1 - pol, pol)
    source = section ^ jnp.where(slot > 1, slot - 1, 0)
    target = (source * 2 + there) * members + (here ^ k) * (pairs // 2) + station
    wide = lax.broadcasted_iota(jnp.int32, (slots * block, 2 * inputs), 1)
    pick = jnp.where(wide == target + part * inputs, 1.0, 0.0)
    pick_other = jnp.where(slot > 1, pick, 0.0)
    height = width * block
    left = lax.broadcasted_iota(jnp.int32, (height, height), 0)
    right = lax.broadcasted_iota(jnp.int32, (height, height), 1)
    inner = right % block
    k, station, part = inner // pairs, inner % pairs // 2, inner % 2
    aim = right // block * block + (here ^ k) * (pairs // 2) + station
    plain = jnp.where(left == aim + part * members, 1.0, 0.0)
    turned = jnp.where(left == aim + (1 - part) * members, jnp.where(part == 1, 1.0, -1.0), 0.0)
    factor = 1.0 / (frames * LANES)

    def settle(first, chosen):
        v = jnp.concatenate([p[first * block : (first + 1) * block] for p in products], 0)
        u = jnp.dot(v, chosen, preferred_element_type=f32, precision=lax.Precision.HIGHEST)
        total = jnp.dot(plain, u[:, :inputs], preferred_element_type=f32, precision=lax.Precision.HIGHEST)
        total += jnp.dot(turned, u[:, inputs:], preferred_element_type=f32, precision=lax.Precision.HIGHEST)
        return total * factor

    out_ref[...] = settle(0, pick)
    cross_ref[...] = settle(1, pick_other)


def correlate(mine, twin, others, frames, sections):
    owners = len(mine)
    rows, lanes = mine[0].shape
    width = lanes // LANES
    block = owners * rows // frames
    inputs = block // 2 * 2 * sections
    shape = jax.ShapeDtypeStruct((width * block, inputs), jnp.float32)
    vmem = pl.BlockSpec(memory_space=pltpu.VMEM)
    return pl.pallas_call(
        functools.partial(correlate_kernel, owners, sections, frames),
        out_shape=[shape, shape],
        in_specs=[vmem] * (len(mine) + 1 + len(others)),
        out_specs=[vmem, vmem],
        scratch_shapes=[pltpu.VMEM((width, (1 + sections) * block, frames * LANES), jnp.bfloat16)],
        name="correlate",
    )(*mine, twin, *others)


def beams_kernel(owners, sections, weight_ref, *refs):
    blocks, (out_ref, data) = refs[:-2], refs[-2:]
    rows = blocks[0].shape[0]
    here, section = lax.axis_index("chan"), lax.axis_index("stat")

    @pl.when(pl.program_id(0) == 0)
    def _():
        for x in range(sections):
            for k in range(owners):
                at = ((section ^ x) * owners + (here ^ k)) * rows
                data[pl.ds(pl.multiple_of(at, rows), rows), :] = blocks[x * owners + k][...]

    out_ref[...] = jnp.dot(weight_ref[...], data[...], preferred_element_type=jnp.float32)


def beamform(weights, blocks, owners, sections):
    height, depth = weights.shape
    rows, lanes = blocks[0].shape
    share = 8 * pieces(height // 8, max(1, 400 * 512 // depth // 8))
    whole = pl.BlockSpec((rows, lanes), lambda i: (0, 0))
    return pl.pallas_call(
        functools.partial(beams_kernel, owners, sections),
        grid=(height // share,),
        out_shape=jax.ShapeDtypeStruct((height, lanes), jnp.float32),
        in_specs=[pl.BlockSpec((share, depth), lambda i: (i, 0))] + [whole] * len(blocks),
        out_specs=pl.BlockSpec((share, lanes), lambda i: (i, 0)),
        scratch_shapes=[pltpu.VMEM((depth, lanes), jnp.bfloat16)],
        name="beamform",
    )(weights, *blocks)


def beam_weights(indices, beam_table, factor):
    levels = jnp.arange(beam_table.shape[1], dtype=jnp.int32)
    selected = indices[..., None] == levels
    real = jnp.sum(jnp.where(selected, beam_table[0], 0.0), axis=-1) * factor
    imag = jnp.sum(jnp.where(selected, beam_table[1], 0.0), axis=-1) * factor
    upper = jnp.stack([real, -imag], axis=-1)
    lower = jnp.stack([imag, real], axis=-1)
    return jnp.stack([upper, lower], axis=1).astype(jnp.bfloat16)


def partner(x, axis, distance):
    return lax.ppermute(x, axis, [(i, i ^ distance) for i in range(lax.axis_size(axis))])


def on_device(voltages, filter_taps, beam_table, beam_index, block_owner):
    owners, sections = lax.axis_size("chan"), lax.axis_size("stat")
    stations = voltages.shape[1]
    frames = voltages.shape[3] - filter_taps.shape[0] + 1
    pairs = 2 * stations
    groups = block_owner.shape[0]
    own = channelise(voltages, filter_taps, block_owner, owners)
    mine = [own[0]] + [partner(own[k], "chan", k) for k in range(1, owners)]
    lead = max(1, owners // 4)
    others = []
    for x in range(1, sections):
        for first in range(0, owners, lead):
            part = mine[first : first + lead]
            if lead == 1:
                others.append(partner(part[0], "stat", x))
            else:
                moved = partner(jnp.concatenate(part, 0), "stat", x)
                others.extend(jnp.split(moved, lead, 0))
    held = lax.optimization_barrier((jnp.concatenate(mine, 0), others[1]))[0]
    twin = partner(held, "pol", 1)

    beam_count, station_count = beam_index.shape
    owned = beam_count // sections
    index = lax.dynamic_slice_in_dim(beam_index, lax.axis_index("stat") * owned, owned, 0)
    weights = beam_weights(index, beam_table, 1.0 / math.sqrt(station_count)).reshape(2 * owned, 2 * station_count)
    weights = framed_weights(weights, frames, pairs)

    vis, cross = correlate(mine, twin, others, frames, sections)
    crossed = partner(cross, "pol", 1)
    last, _ = lax.optimization_barrier((others[-1], cross))
    beams = beamform(weights, mine + others[:-1] + [last], owners, sections)
    vis = (vis + crossed).reshape(groups // owners, 2, -1, vis.shape[1])
    return vis, beams.reshape(owned, 1, 2, frames, -1)


def solution(mesh):
    return jax.shard_map(
        on_device,
        mesh=mesh,
        in_specs=(P(("group", "stat"), "chan", "pol", None, None, None), P(), P(), P(), P()),
        out_specs=(
            P(("group", "chan"), None, ("stat", "pol"), None),
            P(("group", "stat"), "pol", None, None, "chan"),
        ),
        check_vma=False,
    )
```

time: 117 us -> 70.2 us (0.60)
  Pallas kernels: 0 us -> 26.7 us
  local copies, waits for them, and re-layouts: 39 us -> 15.9 us
  blocking collectives: 20.7 us -> 0 us
  between operations: 14.3 us -> 0.78 us
  starting transfers between devices: 0.04 us -> 11.3 us
  matrix products: 10.4 us -> 0 us
  other arithmetic: 12.2 us -> 2.04 us
  waiting for transfers between devices: 20.1 us -> 12.9 us
    pallas_call x0 -> x4, Pallas kernels: none -> 26.7 us  [the longest x1 12.2 us: beamform(): pl.pallas_call(functools.partial(beams_kernel, owners, sections), grid=(h...]
    unnamed x15 -> x20, local copies, waits for them, and re-layouts: 27.9 us -> 1.43 us
    all_to_all x1 -> x0, blocking collectives: 20.7 us -> none  [on_device(): lax.all_to_all(ordered, 'chan', split_axis=3, concat_axis=0, tiled=True)]
    all_gather x1 -> x0, waiting for transfers between devices: 20.1 us -> none  [on_device(): lax.all_gather(local_spectra, ('stat', 'pol'), axis=0, tiled=True)]
    ppermute x0 -> x9, waiting for transfers between devices: none -> 12.9 us  [partner(): lax.ppermute(x, axis, [(i, i ^ distance) for i in range(lax.axis_size(axi...]
    ppermute x0 -> x9, starting transfers between devices: none -> 11.3 us  [partner(): lax.ppermute(x, axis, [(i, i ^ distance) for i in range(lax.axis_size(axi...]
    dot_general x5 -> x0, matrix products: 10.4 us -> none  [the longest x1 3.13 us: channelise(): jnp.einsum('sfcky,cydz->sdfzk', turned, matrix, precision=lax.Precision.H...]
    convert_element_type x2 -> x1, local copies, waits for them, and re-layouts: 0.69 us -> 8.88 us  [beam_weights(): return jnp.stack([upper, lower], axis=1).astype(jnp.bfloat16)]
  transfers between devices with their start and end apart: 1 -> 9, of which waited for: 1 -> 4; matrix products, arithmetic and copies ran while one was open for 1% -> 23% of each run, Pallas kernels for 0% -> 25%
where the time goes in v1:
time: 70.2 us; the launch traced here: 69.7 us
  Pallas kernels  26.7 us (38%)
  local copies, waits for them, and re-layouts  15.9 us (23%)
  waiting for transfers between devices  12.9 us (18%)
  starting transfers between devices  11.3 us (16%)
  other arithmetic  2.04 us (3%)
  between operations  0.78 us (1%)
    ppermute x9, waiting for transfers between devices, partner(): lax.ppermute(x, axis, [(i, i ^ distance) for i in range(lax.axis_size(axi...  12.9 us
    pallas_call x1, Pallas kernels, beamform(): pl.pallas_call(functools.partial(beams_kernel, owners, sections), grid=(h...  12.2 us
    ppermute x9, starting transfers between devices, partner(): lax.ppermute(x, axis, [(i, i ^ distance) for i in range(lax.axis_size(axi...  11.3 us
    convert_element_type x1, local copies, waits for them, and re-layouts, beam_weights(): return jnp.stack([upper, lower], axis=1).astype(jnp.bfloat16)  8.88 us
    pallas_call x1, Pallas kernels, channelise(): pl.pallas_call(functools.partial(channel_kernel, owners), out_shape=[jax....  5.25 us
    pallas_call x1, Pallas kernels, framed_weights(): pl.pallas_call(functools.partial(weights_kernel, pairs), grid=(count // s...  4.93 us
    another operation x1, local copies, waits for them, and re-layouts, beam_weights(): return jnp.stack([upper, lower], axis=1).astype(jnp.bfloat16)  4.73 us
    pallas_call x1, Pallas kernels, correlate(): pl.pallas_call(functools.partial(correlate_kernel, owners, sections, fram...  4.32 us
  transfers between devices with their start and end apart: 9, of which 4 were waited for; matrix products, arithmetic and copies ran while one was open for 23% of the time, Pallas kernels for 25%

profile of v1, /device:TPU:0, one launch (start us, length us, event | category | flops | bytes accessed | tf_op | source)
XLA Modules:
  0.0 69.7 jit_solution(10267763991536910981)
XLA Ops:
  0.6 5.2 %channelise.1 = (bf16[64,1024]{1,0:T(8,128)(2,1)}, bf16[64,1024]{1,0:T(8,128)(2,1)}, bf16[64,1024]{1,0:T(8,128)(2,1)}, bf16[64,1024]{1,0:T(8,128)(2,1)}) custom-call(s32[32]{0:T(128)} %owner_ref.1, bf16[4,19,64,128]{3,2,1,0:T(8,128)(2,1)} %bitcast.26, f32[12,4096]{1,0:T(8,128)} %taps_ref.1, bf16[256,256]{1,0:T(8,128)(2,1)} %constant.24.clone.first_ref, ...), custom_call_target="tpu_custom_call" | custom-call | tf_op jit(solution)/shard_map/channelise/pallas_call | solution.py:135
  5.9 3.1 %collective-permute-start = (bf16[64,1024]{1,0:T(8,128)(2,1)}, bf16[64,1024]{1,0:T(8,128)(2,1)S(1)}, u32[]{:S(2)}, u32[]{:S(2)}) collective-permute-start(bf16[64,1024]{1,0:T(8,128)(2,1)} %get-tuple-element.11), channel_id=1, source_target_pairs={{0,4},{4,0},{8,12},{12,8},{1,5},{5,1},{9,13},{13,9},{2,6},{6,2},{1... | collective-permute-start | bytes 393224 | tf_op jit(solution)/shard_map/ppermute | solution.py:331
  9.0 2.6 %collective-permute-start.1 = (bf16[64,1024]{1,0:T(8,128)(2,1)}, bf16[64,1024]{1,0:T(8,128)(2,1)S(1)}, u32[]{:S(2)}, u32[]{:S(2)}) collective-permute-start(bf16[64,1024]{1,0:T(8,128)(2,1)} %get-tuple-element.12), channel_id=1, source_target_pairs={{0,8},{4,12},{8,0},{12,4},{1,9},{5,13},{9,1},{13,5},{2,10},{6,14},... | collective-permute-start | bytes 393224 | tf_op jit(solution)/shard_map/ppermute | solution.py:331
  11.6 1.7 %collective-permute-start.5 = (bf16[64,1024]{1,0:T(8,128)(2,1)}, bf16[64,1024]{1,0:T(8,128)(2,1)S(1)}, u32[]{:S(2)}, u32[]{:S(2)}) collective-permute-start(bf16[64,1024]{1,0:T(8,128)(2,1)} %get-tuple-element.10.refs_0_), channel_id=1, source_target_pairs={{0,2},{2,0},{1,3},{3,1},{4,6},{6,4},{5,7},{7,5},{8,10},{10,8},{9,1... | collective-permute-start | bytes 393224 | tf_op jit(solution)/shard_map/ppermute | solution.py:331
  13.3 1.0 %collective-permute-done.refs_1_ = bf16[64,1024]{1,0:T(8,128)(2,1)S(1)} collective-permute-done((bf16[64,1024]{1,0:T(8,128)(2,1)}, bf16[64,1024]{1,0:T(8,128)(2,1)S(1)}, u32[]{:S(2)}, u32[]{:S(2)}) %collective-permute-start) | collective-permute-done | bytes 131104 | tf_op jit(solution)/shard_map/ppermute | solution.py:331
  14.3 1.7 %collective-permute-start.3 = (bf16[64,1024]{1,0:T(8,128)(2,1)S(1)}, bf16[64,1024]{1,0:T(8,128)(2,1)S(1)}, u32[]{:S(2)}, u32[]{:S(2)}) collective-permute-start(bf16[64,1024]{1,0:T(8,128)(2,1)S(1)} %collective-permute-done.refs_1_), channel_id=1, source_target_pairs={{0,2},{2,0},{1,3},{3,1},{4,6},{6,4},{5,7},{7,5},{8,10},{10,8},{9,1... | collective-permute-start | bytes 393224 | tf_op jit(solution)/shard_map/ppermute | solution.py:331
  16.0 0.8 %slice_bitcast_fusion.1 = (f32[16]{0:T(128)S(1)}, f32[16]{0:T(128)S(1)}) fusion(f32[2,16]{1,0:T(2,128)} %param.12), kind=kLoop, calls=%fused_computation.14 | loop fusion | bytes 256 | tf_op jit(solution)/shard_map/squeeze | solution.py:323
  16.8 5.3 %collective-permute-done.1.refs_2_ = bf16[64,1024]{1,0:T(8,128)(2,1)S(1)} collective-permute-done((bf16[64,1024]{1,0:T(8,128)(2,1)}, bf16[64,1024]{1,0:T(8,128)(2,1)S(1)}, u32[]{:S(2)}, u32[]{:S(2)}) %collective-permute-start.1) | collective-permute-done | bytes 131104 | tf_op jit(solution)/shard_map/ppermute | solution.py:331
  22.1 1.0 %pad_maximum_fusion = bf16[256,1024]{1,0:T(8,128)(2,1)S(1)} fusion(bf16[64,1024]{1,0:T(8,128)(2,1)S(1)} %collective-permute-done.2.refs_3_, bf16[64,1024]{1,0:T(8,128)(2,1)S(1)} %collective-permute-done.1.refs_2_, bf16[64,1024]{1,0:T(8,128)(2,1)S(1)} %collective-permute-done.refs_1_, bf16[64,1024]{1,0:T(8,128)(2,1)} %get-tuple-element.10.refs_0_), kind=kLoop, calls=%fused_computation | loop fusion | flops 2097152 | bytes 1048576 | tf_op jit(solution)/shard_map/concatenate | solution.py:352
  23.2 0.1 collective-permute-start.4
  23.3 0.1 constant_dynamic-slice_fusion
  23.4 0.3 select_reduce_fusion
  23.7 1.6 %collective-permute-start.6 = (bf16[64,1024]{1,0:T(8,128)(2,1)S(1)}, bf16[64,1024]{1,0:T(8,128)(2,1)S(1)}, u32[]{:S(2)}, u32[]{:S(2)}) collective-permute-start(bf16[64,1024]{1,0:T(8,128)(2,1)S(1)} %collective-permute-done.1.refs_2_), channel_id=1, source_target_pairs={{0,2},{2,0},{1,3},{3,1},{4,6},{6,4},{5,7},{7,5},{8,10},{10,8},{9,1... | collective-permute-start | bytes 393224 | tf_op jit(solution)/shard_map/ppermute | solution.py:331
  25.2 0.5 collective-permute-start.7
  25.8 4.3 %collective-permute-done.6.refs_7_.refs_6_ = bf16[64,1024]{1,0:T(8,128)(2,1)S(1)} collective-permute-done((bf16[64,1024]{1,0:T(8,128)(2,1)S(1)}, bf16[64,1024]{1,0:T(8,128)(2,1)S(1)}, u32[]{:S(2)}, u32[]{:S(2)}) %collective-permute-start.6) | collective-permute-done | bytes 131104 | tf_op jit(solution)/shard_map/ppermute | solution.py:331
  30.1 2.3 %collective-permute-done.7.refs_8_.refs_7_ = bf16[64,1024]{1,0:T(8,128)(2,1)S(1)} collective-permute-done((bf16[64,1024]{1,0:T(8,128)(2,1)S(1)}, bf16[64,1024]{1,0:T(8,128)(2,1)S(1)}, u32[]{:S(2)}, u32[]{:S(2)}) %collective-permute-start.7) | collective-permute-done | bytes 131104 | tf_op jit(solution)/shard_map/ppermute | solution.py:331
  32.5 0.6 copy-done.7
  33.1 0.8 %copy-done.8 = bf16[256,1024]{1,0:T(8,128)(2,1)} copy-done((bf16[256,1024]{1,0:T(8,128)(2,1)}, bf16[256,1024]{1,0:T(8,128)(2,1)S(1)}, u32[]{:S(2)}) %copy-start.8) | copy-done | bytes 524312
  33.9 4.3 %correlate.1 = (f32[256,64]{1,0:T(8,128)}, f32[256,64]{1,0:T(8,128)}) custom-call(bf16[64,1024]{1,0:T(8,128)(2,1)} %get-tuple-element.10.refs_0_, bf16[64,1024]{1,0:T(8,128)(2,1)} %copy-done.1, bf16[64,1024]{1,0:T(8,128)(2,1)} %copy-done.2, bf16[64,1024]{1,0:T(8,128)(2,1)} %copy-done.3, bf16[256,1024]{1,0:T(8,128)(2,1)} %copy-done.8, ...), custom_call_target="tpu_custom_call" | custom-call | tf_op jit(solution)/shard_map/correlate/pallas_call | solution.py:279
  38.2 4.7 %copy.22 = bf16[250,2,32,2]{3,2,1,0:T(8,128)(2,1)} copy(bf16[250,2,32,2]{0,2,3,1:T(8,128)(2,1)S(1)} %pad_maximum_fusion.1) | data formatting | bytes 128000 | tf_op jit(solution)/shard_map/stack | solution.py:327
  42.9 8.9 %convert_element_type.5.weight_ref = bf16[500,64]{1,0:T(8,128)(2,1)} reshape(bf16[250,2,32,2]{3,2,1,0:T(8,128)(2,1)} %copy.22) | data formatting | bytes 128000 | tf_op jit(solution)/shard_map/convert_element_type | solution.py:327
  51.8 4.9 %framed_weights.1.weight_ref = bf16[4000,512]{1,0:T(8,128)(2,1)} custom-call(bf16[500,64]{1,0:T(8,128)(2,1)} %convert_element_type.5.weight_ref, bf16[64,512]{1,0:T(8,128)(2,1)} %constant.28.clone.copy_ref), custom_call_target="tpu_custom_call" | custom-call | tf_op jit(solution)/shard_map/framed_weights/pallas_call | solution.py:193
  56.8 12.2 %beamform.1 = f32[4000,1024]{1,0:T(8,128)} custom-call(bf16[4000,512]{1,0:T(8,128)(2,1)} %framed_weights.1.weight_ref, bf16[64,1024]{1,0:T(8,128)(2,1)} %get-tuple-element.10.refs_0_, bf16[64,1024]{1,0:T(8,128)(2,1)} %copy-done.1, bf16[64,1024]{1,0:T(8,128)(2,1)} %copy-done.2, bf16[64,1024]{1,0:T(8,128)(2,1)} %copy-done.3, bf16[64,1024]{1,0:T(8,128)(2,1)} %copy-done.4, ...), custom_call_target="tpu_custom_call" | custom-call | tf_op jit(solution)/shard_map/beamform/pallas_call | solution.py:309
  69.0 0.7 add.6
  (28 shorter events, 0.1 us)
Async XLA Ops:
  0.6 22.6 %copy-start = (s32[500,32]{0,1:T(8,128)S(1)}, s32[500,32]{0,1:T(8,128)}, u32[]{:S(2)}) copy-start(s32[500,32]{0,1:T(8,128)} %param.13) | copy-start | bytes 192004
  5.9 8.4 %collective-permute-start = (bf16[64,1024]{1,0:T(8,128)(2,1)}, bf16[64,1024]{1,0:T(8,128)(2,1)S(1)}, u32[]{:S(2)}, u32[]{:S(2)}) collective-permute-start(bf16[64,1024]{1,0:T(8,128)(2,1)} %get-tuple-element.11), channel_id=1, source_target_pairs={{0,4},{4,0},{8,12},{12,8},{1,5},{5,1},{9,13},{13,9},{2,6},{6,2},{1... | collective-permute-start | bytes 393224 | tf_op jit(solution)/shard_map/ppermute | solution.py:331
  9.0 13.1 %collective-permute-start.1 = (bf16[64,1024]{1,0:T(8,128)(2,1)}, bf16[64,1024]{1,0:T(8,128)(2,1)S(1)}, u32[]{:S(2)}, u32[]{:S(2)}) collective-permute-start(bf16[64,1024]{1,0:T(8,128)(2,1)} %get-tuple-element.12), channel_id=1, source_target_pairs={{0,8},{4,12},{8,0},{12,4},{1,9},{5,13},{9,1},{13,5},{2,10},{6,14},... | collective-permute-start | bytes 393224 | tf_op jit(solution)/shard_map/ppermute | solution.py:331
  11.6 10.5 %collective-permute-start.2 = (bf16[64,1024]{1,0:T(8,128)(2,1)}, bf16[64,1024]{1,0:T(8,128)(2,1)S(1)}, u32[]{:S(2)}, u32[]{:S(2)}) collective-permute-start(bf16[64,1024]{1,0:T(8,128)(2,1)} %get-tuple-element.13), channel_id=1, source_target_pairs={{0,12},{4,8},{8,4},{12,0},{1,13},{5,9},{9,5},{13,1},{2,14},{6,10},... | collective-permute-start | bytes 393224 | tf_op jit(solution)/shard_map/ppermute | solution.py:331
  11.6 14.2 %collective-permute-start.5 = (bf16[64,1024]{1,0:T(8,128)(2,1)}, bf16[64,1024]{1,0:T(8,128)(2,1)S(1)}, u32[]{:S(2)}, u32[]{:S(2)}) collective-permute-start(bf16[64,1024]{1,0:T(8,128)(2,1)} %get-tuple-element.10.refs_0_), channel_id=1, source_target_pairs={{0,2},{2,0},{1,3},{3,1},{4,6},{6,4},{5,7},{7,5},{8,10},{10,8},{9,1... | collective-permute-start | bytes 393224 | tf_op jit(solution)/shard_map/ppermute | solution.py:331
  14.3 18.1 %copy-start.1 = (bf16[64,1024]{1,0:T(8,128)(2,1)}, bf16[64,1024]{1,0:T(8,128)(2,1)S(1)}, u32[]{:S(2)}) copy-start(bf16[64,1024]{1,0:T(8,128)(2,1)S(1)} %collective-permute-done.refs_1_) | copy-start | bytes 393220
  14.3 8.9 %collective-permute-start.3 = (bf16[64,1024]{1,0:T(8,128)(2,1)S(1)}, bf16[64,1024]{1,0:T(8,128)(2,1)S(1)}, u32[]{:S(2)}, u32[]{:S(2)}) collective-permute-start(bf16[64,1024]{1,0:T(8,128)(2,1)S(1)} %collective-permute-done.refs_1_), channel_id=1, source_target_pairs={{0,2},{2,0},{1,3},{3,1},{4,6},{6,4},{5,7},{7,5},{8,10},{10,8},{9,1... | collective-permute-start | bytes 393224 | tf_op jit(solution)/shard_map/ppermute | solution.py:331
  22.1 10.3 %copy-start.2 = (bf16[64,1024]{1,0:T(8,128)(2,1)}, bf16[64,1024]{1,0:T(8,128)(2,1)S(1)}, u32[]{:S(2)}) copy-start(bf16[64,1024]{1,0:T(8,128)(2,1)S(1)} %collective-permute-done.1.refs_2_) | copy-start | bytes 393220
  22.1 10.3 %copy-start.3 = (bf16[64,1024]{1,0:T(8,128)(2,1)}, bf16[64,1024]{1,0:T(8,128)(2,1)S(1)}, u32[]{:S(2)}) copy-start(bf16[64,1024]{1,0:T(8,128)(2,1)S(1)} %collective-permute-done.2.refs_3_) | copy-start | bytes 393220
  23.2 9.3 %copy-start.5 = (bf16[64,1024]{1,0:T(8,128)(2,1)}, bf16[64,1024]{1,0:T(8,128)(2,1)S(1)}, u32[]{:S(2)}) copy-start(bf16[64,1024]{1,0:T(8,128)(2,1)S(1)} %collective-permute-done.3.refs_6_.refs_5_) | copy-start | bytes 393220
  23.2 9.2 %collective-permute-start.4 = (bf16[256,1024]{1,0:T(8,128)(2,1)S(1)}, bf16[256,1024]{1,0:T(8,128)(2,1)S(1)}, u32[]{:S(2)}, u32[]{:S(2)}) collective-permute-start(bf16[256,1024]{1,0:T(8,128)(2,1)S(1)} %pad_maximum_fusion), channel_id=1, source_target_pairs={{0,1},{1,0},{2,3},{3,2},{4,5},{5,4},{6,7},{7,6},{8,9},{9,8},{10,11... | collective-permute-start | bytes 1572872 | tf_op jit(solution)/shard_map/ppermute | solution.py:331
  23.7 6.4 %collective-permute-start.6 = (bf16[64,1024]{1,0:T(8,128)(2,1)S(1)}, bf16[64,1024]{1,0:T(8,128)(2,1)S(1)}, u32[]{:S(2)}, u32[]{:S(2)}) collective-permute-start(bf16[64,1024]{1,0:T(8,128)(2,1)S(1)} %collective-permute-done.1.refs_2_), channel_id=1, source_target_pairs={{0,2},{2,0},{1,3},{3,1},{4,6},{6,4},{5,7},{7,5},{8,10},{10,8},{9,1... | collective-permute-start | bytes 393224 | tf_op jit(solution)/shard_map/ppermute | solution.py:331
  25.2 7.2 %collective-permute-start.7 = (bf16[64,1024]{1,0:T(8,128)(2,1)S(1)}, bf16[64,1024]{1,0:T(8,128)(2,1)S(1)}, u32[]{:S(2)}, u32[]{:S(2)}) collective-permute-start(bf16[64,1024]{1,0:T(8,128)(2,1)S(1)} %collective-permute-done.2.refs_3_), channel_id=1, source_target_pairs={{0,2},{2,0},{1,3},{3,1},{4,6},{6,4},{5,7},{7,5},{8,10},{10,8},{9,1... | collective-permute-start | bytes 393224 | tf_op jit(solution)/shard_map/ppermute | solution.py:331
  25.8 6.7 %copy-start.4 = (bf16[64,1024]{1,0:T(8,128)(2,1)}, bf16[64,1024]{1,0:T(8,128)(2,1)S(1)}, u32[]{:S(2)}) copy-start(bf16[64,1024]{1,0:T(8,128)(2,1)S(1)} %collective-permute-done.5.refs_5_.refs_4_) | copy-start | bytes 393220
  30.1 2.4 %copy-start.6 = (bf16[64,1024]{1,0:T(8,128)(2,1)}, bf16[64,1024]{1,0:T(8,128)(2,1)S(1)}, u32[]{:S(2)}) copy-start(bf16[64,1024]{1,0:T(8,128)(2,1)S(1)} %collective-permute-done.6.refs_7_.refs_6_) | copy-start | bytes 393220
  32.4 0.7 copy-start.7
  33.1 0.8 %copy-start.8 = (bf16[256,1024]{1,0:T(8,128)(2,1)}, bf16[256,1024]{1,0:T(8,128)(2,1)S(1)}, u32[]{:S(2)}) copy-start(bf16[256,1024]{1,0:T(8,128)(2,1)S(1)} %collective-permute-done.4.refs_4_) | copy-start | bytes 1572868
  38.2 30.8 %collective-permute-start.8 = (f32[256,64]{1,0:T(8,128)}, f32[256,64]{1,0:T(8,128)S(1)}, u32[]{:S(2)}, u32[]{:S(2)}) collective-permute-start(f32[256,64]{1,0:T(8,128)} %get-tuple-element.16), channel_id=1, source_target_pairs={{0,1},{1,0},{2,3},{3,2},{4,5},{5,4},{6,7},{7,6},{8,9},{9,8},{10,11... | collective-permute-start | bytes 196616 | tf_op jit(solution)/shard_map/ppermute | solution.py:331
  56.8 12.3 %copy-start.9 = (f32[256,64]{1,0:T(8,128)S(1)}, f32[256,64]{1,0:T(8,128)}, u32[]{:S(2)}) copy-start(f32[256,64]{1,0:T(8,128)} %get-tuple-element.15) | copy-start | bytes 196612

commit v2 on v1

v2 whole, which is shorter than its diff:
```python
import functools, math
import jax, jax.numpy as jnp, numpy as np
from jax import lax
from jax.experimental import pallas as pl
from jax.experimental.pallas import tpu as pltpu
from jax.sharding import PartitionSpec as P


LANES = 128
HALF = 4


def dft_parts(rows, cols, length):
    phase = np.outer(np.arange(rows), np.arange(cols)) % length * (2.0 * np.pi / length)
    return np.cos(phase), np.sin(phase)


def channel_tables(nfft, groups):
    depth = nfft // LANES
    per_group = LANES // depth
    cosine, sine = dft_parts(depth, depth, depth)
    pair = np.stack([np.stack([cosine, sine], -1), np.stack([-sine, cosine], -1)])
    first = np.einsum("akrc,fg->afkgrc", pair, np.eye(HALF))
    first = first.reshape(2 * HALF * depth, HALF * depth * 2)
    turn_cos, turn_sin = dft_parts(depth, LANES, nfft)
    cosine, sine = dft_parts(LANES, LANES, LANES)
    order = (np.arange(groups)[None, :] * per_group + np.arange(per_group)[:, None]).reshape(-1)
    cosine, sine = cosine[order] / math.sqrt(nfft), sine[order] / math.sqrt(nfft)
    second = np.concatenate([np.concatenate([cosine, sine], 1), np.concatenate([-sine, cosine], 1)], 0)
    spread = np.einsum("qr,fg,kl->qfkgrl", np.eye(per_group), np.eye(HALF), np.eye(depth))
    spread = spread.reshape(per_group * HALF * depth, HALF * per_group * depth)
    bf = lambda x: jnp.asarray(x, jnp.bfloat16)
    return bf(first), jnp.asarray(np.stack([turn_cos, turn_sin]), jnp.float32), bf(second), bf(spread)


def channel_kernel(owners, owner_ref, volt_ref, taps_ref, first_ref, turn_ref, second_ref, spread_ref, *rest):
    outs = rest[:owners]
    volts, tap_rows, first, turn, second, spread, filt, wide, pick, sems = rest[owners:]
    stations, blocks, rows, _ = volt_ref.shape
    taps = taps_ref.shape[0]
    frames = blocks - taps + 1
    halves = frames // HALF
    depth = rows // 2
    groups = owner_ref.shape[0]
    width = groups // owners
    quads = LANES // depth
    span = HALF * depth
    here = lax.axis_index("chan")
    copies = []
    for s in range(stations):
        copies.append(pltpu.make_async_copy(volt_ref.at[s], volts.at[s], sems.at[s]))
    consts = []
    for i, (src, dst) in enumerate([(first_ref, first), (turn_ref, turn), (second_ref, second), (spread_ref, spread)]):
        consts.append(pltpu.make_async_copy(src, dst, sems.at[stations + i]))
    for c in copies + consts:
        c.start()

    sub = lax.broadcasted_iota(jnp.int32, (8, LANES), 0)
    for t in range(taps):
        for m in range(rows // 8):
            parts = [jnp.broadcast_to(taps_ref[t : t + 1, pl.ds((4 * m + i) * LANES, LANES)], (8, LANES)) for i in range(4)]
            low = jnp.where(sub < 2, parts[0], parts[1])
            high = jnp.where(sub < 6, parts[2], parts[3])
            tap_rows[t, pl.ds(8 * m, 8), :] = jnp.where(sub < 4, low, high)

    sc = 2 * stations
    lane = lax.broadcasted_iota(jnp.int32, (sc, sc * groups), 1)
    base = lax.broadcasted_iota(jnp.int32, (sc, sc * groups), 0) * groups
    for k in range(owners):
        for j in range(width):
            g = owner_ref[(here ^ k) * width + j]
            p = (k * width + j) * sc
            pick[pl.ds(p, sc), :] = jnp.where(lane == base + g, 1.0, 0.0).astype(jnp.bfloat16)

    step = 16
    for s in range(stations):
        copies[s].wait()

        def fir(m, carry, s=s):
            at = pl.multiple_of(m * step, step)
            x = [volts[s, b, pl.ds(at, step), :].astype(jnp.float32) for b in range(blocks)]
            w = [tap_rows[t, pl.ds(at, step), :] for t in range(taps)]
            for f in range(frames):
                total = w[0] * x[f]
                for t in range(1, taps):
                    total = total + w[t] * x[f + t]
                row = pl.multiple_of((f % HALF) * rows + at, step)
                filt[s, pl.ds(row, step), pl.ds((f // HALF) * LANES, LANES)] = total.astype(jnp.bfloat16)
            return carry

        lax.fori_loop(0, rows // step, fir, 0)

    for c in consts:
        c.wait()
    f32 = jnp.float32
    cosine = jnp.concatenate([turn[0]] * HALF, 0)
    sine = jnp.concatenate([turn[1]] * HALF, 0)
    for s in range(stations):
        y = jnp.dot(first[...], filt[s], preferred_element_type=f32)
        re, im = y[:span], y[span:]
        turned = []
        for h in range(halves):
            a, b = re[:, h * LANES : (h + 1) * LANES], im[:, h * LANES : (h + 1) * LANES]
            turned.append(jnp.concatenate([a * cosine + b * sine, b * cosine - a * sine], 1))
        turned = jnp.concatenate(turned, 0).astype(jnp.bfloat16)
        z = lax.dot_general(second[...], turned, (((1,), (1,)), ((), ())), preferred_element_type=f32).astype(jnp.bfloat16)
        for c in range(2):
            for q in range(quads):
                for h in range(halves):
                    wide[h, pl.ds((s * 2 + c) * groups, groups), pl.ds(q * LANES, LANES)] = z[
                        c * quads * groups + q * groups : c * quads * groups + (q + 1) * groups, h * LANES : (h + 1) * LANES
                    ]
    for h in range(halves):
        y = jnp.dot(wide[h], spread[...], preferred_element_type=f32).astype(jnp.bfloat16)
        z = jnp.dot(pick[...], y, preferred_element_type=f32)
        for k in range(owners):
            for j in range(width):
                for f in range(HALF):
                    p = (k * width + j) * sc
                    outs[k][pl.ds((h * HALF + f) * sc, sc), pl.ds(j * LANES, LANES)] = z[
                        p : p + sc, f * LANES : (f + 1) * LANES
                    ].astype(jnp.bfloat16)


def channelise(voltages, filter_taps, block_owner, owners):
    _, stations, _, blocks, _, nfft = voltages.shape
    taps = filter_taps.shape[0]
    frames = blocks - taps + 1
    groups = block_owner.shape[0]
    depth = nfft // LANES
    volts = voltages.reshape(stations, blocks, 2, depth, LANES).transpose(0, 1, 3, 2, 4).reshape(stations, blocks, 2 * depth, LANES)
    first, turn, second, spread = channel_tables(nfft, groups)
    sc = 2 * stations
    width = groups // owners
    anyspec = pl.BlockSpec(memory_space=pl.ANY)
    bf = jnp.bfloat16
    return pl.pallas_call(
        functools.partial(channel_kernel, owners),
        out_shape=[jax.ShapeDtypeStruct((frames * sc, width * LANES), bf)] * owners,
        in_specs=[pl.BlockSpec(memory_space=pltpu.SMEM), anyspec, pl.BlockSpec(memory_space=pltpu.VMEM)] + [anyspec] * 4,
        out_specs=[pl.BlockSpec(memory_space=pltpu.VMEM)] * owners,
        scratch_shapes=[
            pltpu.VMEM(volts.shape, bf),
            pltpu.VMEM((taps, 2 * depth, LANES), jnp.float32),
            pltpu.VMEM(first.shape, bf),
            pltpu.VMEM(turn.shape, jnp.float32),
            pltpu.VMEM(second.shape, bf),
            pltpu.VMEM(spread.shape, bf),
            pltpu.VMEM((stations, HALF * 2 * depth, frames // HALF * LANES), bf),
            pltpu.VMEM((frames // HALF, sc * groups, spread.shape[0]), bf),
            pltpu.VMEM((groups * sc, sc * groups), bf),
            pltpu.SemaphoreType.DMA((stations + 4,)),
        ],
        compiler_params=grant(),
        name="channelise",
    )(block_owner, volts, filter_taps, first, turn, second, spread)


VMEM_BYTES = 24 * 2**20
RESIDENT = 8 * 2**20
SLICE = 32


def whole_vmem(count):
    return [pl.BlockSpec(memory_space=pltpu.VMEM)] * count


def grant(size=VMEM_BYTES):
    return pltpu.CompilerParams(vmem_limit_bytes=size)


def pieces(total, most):
    return max(d for d in range(1, most + 1) if total % d == 0)


def split_low(x, size):
    shift = size.bit_length() - 1
    assert size == 1 << shift
    return x >> shift, x & (size - 1)


def bf_pair(x):
    high = x.astype(jnp.bfloat16)
    return high, (x - high.astype(jnp.float32)).astype(jnp.bfloat16)


def dot_tt(a, b):
    return lax.dot_general(a, b, (((1,), (1,)), ((), ())), preferred_element_type=jnp.float32)


def weights_kernel(pairs, owned, share, table_ref, index_ref, copy_ref, out_ref, rows_ref):
    stations, beams = index_ref.shape
    tile, spread = copy_ref.shape
    frames = spread // tile
    count = 2 * owned
    start = lax.axis_index("stat") * owned
    factor = 1.0 / math.sqrt(stations)

    def prepare():
        row = lax.broadcasted_iota(jnp.int32, (count, beams), 0)
        lane = lax.broadcasted_iota(jnp.int32, (count, beams), 1)
        hit = lane == start + (row >> 1)
        one, zero = jnp.float32(1), jnp.float32(0)
        choose = [jnp.where(hit & ((row & 1) == c), one, zero).astype(jnp.bfloat16) for c in range(2)]
        for i in range(stations // SLICE):
            index = index_ref[i * SLICE : (i + 1) * SLICE, :]
            real = jnp.zeros(index.shape, jnp.float32)
            imag = jnp.zeros(index.shape, jnp.float32)
            for e in range(table_ref.shape[1]):
                here = index == e
                real = jnp.where(here, table_ref[0, e], real)
                imag = jnp.where(here, table_ref[1, e], imag)
            real, imag = real * factor, imag * factor
            upper = jnp.concatenate([real, -imag], 0).astype(jnp.bfloat16)
            lower = jnp.concatenate([imag, real], 0).astype(jnp.bfloat16)
            w = dot_tt(choose[0], upper) + dot_tt(choose[1], lower)
            rows_ref[:, i * spread : (i + 1) * spread] = jnp.dot(
                w.astype(jnp.bfloat16), copy_ref[...], preferred_element_type=jnp.float32
            )

    first = 0
    if share == count:
        prepare()
    else:
        pl.when(pl.program_id(0) == 0)(prepare)
        first = pl.program_id(0) * share
    width = out_ref.shape[1]
    lane = lax.broadcasted_iota(jnp.int32, (frames, width), 1)
    mine = split_low(split_low(lane, pairs)[0], frames)[1] == lax.broadcasted_iota(jnp.int32, (frames, width), 0)

    def fill(i, carry):
        row = rows_ref[pl.ds(first + i, 1), :]
        out_ref[pl.ds(pl.multiple_of(i * frames, frames), frames), :] = jnp.where(
            mine, jnp.broadcast_to(row, (frames, width)), 0.0
        ).astype(jnp.bfloat16)
        return carry

    lax.fori_loop(0, share, fill, 0, unroll=pieces(share, 10))


def framed_weights(beam_table, beam_index, frames, pairs, owned):
    stations = beam_index.shape[1]
    eye = np.eye
    copies = np.einsum("bp,sq,ct,f->cbspqft", eye(2 * SLICE // pairs), eye(pairs // 2), eye(2), np.ones(frames))
    copies = np.moveaxis(copies, (3, 5, 4, 6), (3, 4, 5, 6)).reshape(2 * SLICE, 2 * SLICE * frames)
    depth = 2 * stations * frames
    count = 2 * owned
    resident = count * frames * depth * 2 <= RESIDENT
    share = count if resident else pieces(count, 10)
    smem = pl.BlockSpec(memory_space=pltpu.SMEM)
    inputs = (beam_table, beam_index.T, jnp.asarray(copies, jnp.bfloat16))
    extra = {}
    if not resident:
        extra = dict(grid=(count // share,), out_specs=pl.BlockSpec((share * frames, depth), lambda i: (i, 0)))
    return pl.pallas_call(
        functools.partial(weights_kernel, pairs, owned, share),
        out_shape=jax.ShapeDtypeStruct((count * frames, depth), jnp.bfloat16),
        in_specs=[smem] + whole_vmem(2),
        scratch_shapes=[pltpu.VMEM((count, depth), jnp.float32)],
        compiler_params=grant() if resident else None,
        name="framed_weights",
        **extra,
    )(*inputs)


def pack(packed, slot, blocks, frames):
    rows, lanes = blocks[0].shape
    pairs = rows // frames
    for k, ref in enumerate(blocks):
        at = (slot * len(blocks) + k) * pairs
        for j in range(lanes // LANES):
            for f in range(frames):
                packed[j, pl.ds(at, pairs), pl.ds(f * LANES, LANES)] = ref[
                    pl.ds(f * pairs, pairs), pl.ds(j * LANES, LANES)
                ]


def settle(products, spread, merge):
    inputs = spread.shape[1] // 2
    v = bf_pair(jnp.concatenate(products, 0))
    u = sum(jnp.dot(x, spread, preferred_element_type=jnp.float32) for x in v)
    u = bf_pair(jnp.concatenate([u[:, :inputs], u[:, inputs:]], 0))
    return sum(jnp.dot(merge, x, preferred_element_type=jnp.float32) for x in u)


def near_kernel(owners, sections, frames, *refs):
    mine, twin = refs[:owners], refs[owners : 2 * owners]
    part_ref, packed, merge_ref, far_ref = refs[2 * owners :]
    width = packed.shape[0]
    pairs = mine[0].shape[0] // frames
    block = owners * pairs
    members = block // 2
    inputs = part_ref.shape[1]
    here, section, pol = lax.axis_index("chan"), lax.axis_index("stat"), lax.axis_index("pol")
    pack(packed, 0, mine, frames)
    pack(packed, 1, twin, frames)
    one, zero = jnp.float32(1), jnp.float32(0)

    def spread_of(slots, source, there):
        col = lax.broadcasted_iota(jnp.int32, (slots * block, 1), 0)
        slot, inner = split_low(col, block)
        k, rest = split_low(inner, pairs)
        target = (source(slot) * 2 + there(slot)) * members + (here ^ k) * (pairs // 2) + (rest >> 1)
        wide = lax.broadcasted_iota(jnp.int32, (slots * block, 2 * inputs), 1)
        return jnp.where(wide == target + (rest & 1) * inputs, one, zero).astype(jnp.bfloat16)

    near = spread_of(2, lambda slot: section, lambda slot: pol ^ slot)
    far_ref[...] = spread_of(sections - 1, lambda slot: section ^ (slot + 1), lambda slot: pol)
    height = width * block
    left = lax.broadcasted_iota(jnp.int32, (height, height), 0)
    right = lax.broadcasted_iota(jnp.int32, (1, height), 1)
    j, inner = split_low(right, block)
    k, rest = split_low(inner, pairs)
    aim = j * block + (here ^ k) * (pairs // 2) + (rest >> 1)
    part = rest & 1
    scale = jnp.float32(1)
    merge_ref[:, :height] = jnp.where(left == aim + part * members, scale, zero).astype(jnp.bfloat16)
    sign = jnp.where(part == 1, scale, -scale)
    merge_ref[:, height:] = jnp.where(left == aim + (1 - part) * members, sign, zero).astype(jnp.bfloat16)
    products = [dot_tt(packed[j, :block], packed[j]) for j in range(width)]
    part_ref[...] = settle(products, near, merge_ref[...]) * (1.0 / (frames * LANES))


def far_kernel(owners, sections, frames, part_ref, packed, merge_ref, far_ref, *refs):
    others = refs[: owners * (sections - 1)]
    out_ref, cross_ref, theirs = refs[owners * (sections - 1) :]
    width, double, _ = packed.shape
    block = double // 2
    for x in range(sections - 1):
        pack(theirs, x, others[x * owners : (x + 1) * owners], frames)
    products = [dot_tt(packed[j], theirs[j]) for j in range(width)]
    factor = 1.0 / (frames * LANES)
    out_ref[...] = part_ref[...] + settle([p[:block] for p in products], far_ref[...], merge_ref[...]) * factor
    cross_ref[...] = settle([p[block:] for p in products], far_ref[...], merge_ref[...]) * factor


def correlate_near(mine, twin, frames, sections):
    owners = len(mine)
    rows, lanes = mine[0].shape
    width, block = lanes // LANES, owners * rows // frames
    inputs = block * sections
    bf = jnp.bfloat16
    return pl.pallas_call(
        functools.partial(near_kernel, owners, sections, frames),
        out_shape=[
            jax.ShapeDtypeStruct((width * block, inputs), jnp.float32),
            jax.ShapeDtypeStruct((width, 2 * block, frames * LANES), bf),
            jax.ShapeDtypeStruct((width * block, 2 * width * block), bf),
            jax.ShapeDtypeStruct(((sections - 1) * block, 2 * inputs), bf),
        ],
        in_specs=whole_vmem(2 * owners),
        out_specs=whole_vmem(4),
        compiler_params=grant(),
        name="correlate_near",
    )(*mine, *twin)


def correlate_far(near, others, owners, frames, sections):
    part, packed, merge, far = near
    shape = jax.ShapeDtypeStruct(part.shape, jnp.float32)
    width, double, lanes = packed.shape
    return pl.pallas_call(
        functools.partial(far_kernel, owners, sections, frames),
        out_shape=[shape, shape],
        in_specs=whole_vmem(4 + len(others)),
        out_specs=whole_vmem(2),
        scratch_shapes=[pltpu.VMEM((width, (sections - 1) * double // 2, lanes), jnp.bfloat16)],
        compiler_params=grant(),
        name="correlate_far",
    )(part, packed, merge, far, *others)


def gather_rows(data, blocks, owners, sections):
    rows = blocks[0].shape[0]
    here, section = lax.axis_index("chan"), lax.axis_index("stat")
    for x in range(sections):
        for k in range(owners):
            at = ((section ^ x) * owners + (here ^ k)) * rows
            data[pl.ds(pl.multiple_of(at, rows), rows), :] = blocks[x * owners + k][...]


def beams_resident(owners, sections, share, span, weight_ref, *refs):
    blocks, (out_ref, data, held, sems) = refs[:-4], refs[-4:]
    gather_rows(data, blocks, owners, sections)
    slots = held.shape[0]
    steps = []
    for row in range(0, weight_ref.shape[0], share):
        for lane in range(0, data.shape[1], span):
            steps.append((row, lane))

    def copy(i):
        row, lane = steps[i]
        return pltpu.make_async_copy(
            held.at[i % slots], out_ref.at[pl.ds(row, share), pl.ds(lane, span)], sems.at[i % slots]
        )

    for i, (row, lane) in enumerate(steps):
        if i >= slots:
            copy(i - slots).wait()
        held[i % slots] = jnp.dot(
            weight_ref[row : row + share, :], data[:, lane : lane + span], preferred_element_type=jnp.float32
        )
        copy(i).start()
    for i in range(max(0, len(steps) - slots), len(steps)):
        copy(i).wait()


def beams_streamed(owners, sections, weight_ref, *refs):
    blocks, (out_ref, data) = refs[:-2], refs[-2:]
    pl.when(pl.program_id(0) == 0)(lambda: gather_rows(data, blocks, owners, sections))
    out_ref[...] = jnp.dot(weight_ref[...], data[...], preferred_element_type=jnp.float32)


def beamform(weights, blocks, owners, sections):
    height, depth = weights.shape
    rows, lanes = blocks[0].shape
    shape = jax.ShapeDtypeStruct((height, lanes), jnp.float32)
    data = pltpu.VMEM((depth, lanes), jnp.bfloat16)
    if height * depth * 2 <= RESIDENT:
        span = min(lanes, 512)
        share = 8 * pieces(height // 8, 100)
        slots = 4
        return pl.pallas_call(
            functools.partial(beams_resident, owners, sections, share, span),
            out_shape=shape,
            in_specs=whole_vmem(1 + len(blocks)),
            out_specs=pl.BlockSpec(memory_space=pl.ANY),
            scratch_shapes=[data, pltpu.VMEM((slots, share, span), jnp.float32), pltpu.SemaphoreType.DMA((slots,))],
            compiler_params=grant(),
            name="beamform",
        )(weights, *blocks)
    share = 8 * pieces(height // 8, max(1, 400 * 512 // depth // 8))
    whole = pl.BlockSpec((rows, lanes), lambda i: (0, 0))
    return pl.pallas_call(
        functools.partial(beams_streamed, owners, sections),
        grid=(height // share,),
        out_shape=shape,
        in_specs=[pl.BlockSpec((share, depth), lambda i: (i, 0))] + [whole] * len(blocks),
        out_specs=pl.BlockSpec((share, lanes), lambda i: (i, 0)),
        scratch_shapes=[data],
        name="beamform",
    )(weights, *blocks)


def partner(x, axis, distance):
    return lax.ppermute(x, axis, [(i, i ^ distance) for i in range(lax.axis_size(axis))])


def moved(parts, axis, distance):
    if len(parts) == 1:
        return [partner(parts[0], axis, distance)]
    return jnp.split(partner(jnp.concatenate(parts, 0), axis, distance), len(parts), 0)


def on_device(voltages, filter_taps, beam_table, beam_index, block_owner):
    owners, sections = lax.axis_size("chan"), lax.axis_size("stat")
    stations = voltages.shape[1]
    frames = voltages.shape[3] - filter_taps.shape[0] + 1
    pairs = 2 * stations
    groups = block_owner.shape[0]
    owned = beam_index.shape[0] // sections
    own = channelise(voltages, filter_taps, block_owner, owners)
    weights = framed_weights(beam_table, beam_index, frames, pairs, owned)
    mine = [own[0]] + [partner(own[k], "chan", k) for k in range(1, owners)]
    lead = max(1, owners // 4)
    twin, others = [], [[] for _ in range(1, sections)]
    for g in range(owners // lead):
        part = mine[g * lead : (g + 1) * lead]
        for x in range(1, sections):
            others[x - 1] += moved(part, "stat", x)
        twin += moved(part, "pol", 1)
    others = sum(others, [])
    near = correlate_near(mine, twin, frames, sections)
    vis, cross = correlate_far(near, others, owners, frames, sections)
    crossed = partner(cross, "pol", 1)
    last, _ = lax.optimization_barrier((others[-1], cross))
    beams = beamform(weights, mine + others[:-1] + [last], owners, sections)
    vis = (vis + crossed).reshape(groups // owners, 2, -1, vis.shape[1])
    return vis, beams.reshape(owned, 1, 2, frames, -1)


def solution(mesh):
    return jax.shard_map(
        on_device,
        mesh=mesh,
        in_specs=(P(("group", "stat"), "chan", "pol", None, None, None), P(), P(), P(), P()),
        out_specs=(
            P(("group", "chan"), None, ("stat", "pol"), None),
            P(("group", "stat"), "pol", None, None, "chan"),
        ),
        check_vma=False,
    )
```

time: 70.2 us -> 53.6 us (0.76)
  Pallas kernels: 26.7 us -> 15.9 us
  local copies, waits for them, and re-layouts: 15.9 us -> 6.51 us
  waiting for transfers between devices: 12.9 us -> 19.4 us
  other arithmetic: 2.04 us -> 0.67 us
  starting transfers between devices: 11.3 us -> 10.1 us
    pallas_call x3 -> x4, Pallas kernels: 21.5 us -> 11.9 us  [the longest x1 6.68 us: beamform(): pl.pallas_call(functools.partial(beams_resident, owners, sections, share,...]
    convert_element_type x1 -> x0, local copies, waits for them, and re-layouts: 8.88 us -> none  [beam_weights(): return jnp.stack([upper, lower], axis=1).astype(jnp.bfloat16)]
    ppermute x9 -> x12, waiting for transfers between devices: 12.9 us -> 19.4 us  [partner(): lax.ppermute(x, axis, [(i, i ^ distance) for i in range(lax.axis_size(axi...]
    unnamed x20, local copies, waits for them, and re-layouts: 1.43 us -> 6.51 us
    another operation x1 -> x0, local copies, waits for them, and re-layouts: 4.73 us -> none  [beam_weights(): return jnp.stack([upper, lower], axis=1).astype(jnp.bfloat16)]
    pallas_call x1, Pallas kernels: 5.25 us -> 3.96 us  [channelise(): pl.pallas_call(functools.partial(channel_kernel, owners), out_shape=[jax....]
    ppermute x9 -> x12, starting transfers between devices: 11.3 us -> 10.1 us  [partner(): lax.ppermute(x, axis, [(i, i ^ distance) for i in range(lax.axis_size(axi...]
    concatenate x1 -> x0, other arithmetic: 1.03 us -> none  [on_device(): held = lax.optimization_barrier((jnp.concatenate(mine, 0), others[1]))[0]]
  transfers between devices with their start and end apart: 9 -> 12, of which waited for: 4 -> 6; matrix products, arithmetic and copies ran while one was open for 23% -> 0% of each run, Pallas kernels for 25% -> 20%
where the time goes in v2:
time: 53.6 us; the launch traced here: 53.2 us
  waiting for transfers between devices  19.4 us (36%)
  Pallas kernels  15.9 us (30%)
  starting transfers between devices  10.1 us (19%)
  local copies, waits for them, and re-layouts  6.51 us (12%)
  between operations  0.74 us (1%)
  other arithmetic  0.67 us (1%)
    ppermute x12, waiting for transfers between devices, partner(): lax.ppermute(x, axis, [(i, i ^ distance) for i in range(lax.axis_size(axi...  19.4 us
    ppermute x12, starting transfers between devices, partner(): lax.ppermute(x, axis, [(i, i ^ distance) for i in range(lax.axis_size(axi...  10.1 us
    pallas_call x1, Pallas kernels, beamform(): pl.pallas_call(functools.partial(beams_resident, owners, sections, share,...  6.68 us
    unnamed x20, local copies, waits for them, and re-layouts  6.51 us
    pallas_call x1, Pallas kernels, channelise(): pl.pallas_call(functools.partial(channel_kernel, owners), out_shape=[jax....  3.96 us
    pallas_call x1, Pallas kernels, framed_weights(): pl.pallas_call(functools.partial(weights_kernel, pairs, owned, share), ou...  3.03 us
    pallas_call x1, Pallas kernels, correlate_far(): pl.pallas_call(functools.partial(far_kernel, owners, sections, frames), o...  1.25 us
  transfers between devices with their start and end apart: 12, of which 6 were waited for; matrix products, arithmetic and copies ran while one was open for 0% of the time, Pallas kernels for 20%

profile of v2, /device:TPU:0, one launch (start us, length us, event | category | flops | bytes accessed | tf_op | source)
XLA Modules:
  0.0 53.2 jit_solution(1433759396909366912)
XLA Ops:
  0.7 1.3 %copy-done = bf16[1,4,1,19,2,4096]{5,4,3,2,1,0:T(2,128)(2,1)S(1)} copy-done((bf16[1,4,1,19,2,4096]{5,4,3,2,1,0:T(2,128)(2,1)S(1)}, bf16[1,4,1,19,2,4096]{5,4,3,2,1,0:T(2,128)(2,1)}, u32[]{:S(2)}) %copy-start) | copy-done | bytes 1245208
  1.9 1.0 %copy-done.1 = bf16[512,512]{1,0:T(8,128)(2,1)S(1)} copy-done((bf16[512,512]{1,0:T(8,128)(2,1)S(1)}, bf16[512,512]{1,0:T(8,128)(2,1)}, u32[]{:S(2)}) %copy-start.1) | copy-done | bytes 524312
  3.0 0.9 %copy-done.2 = f32[12,4096]{1,0:T(8,128)S(1)} copy-done((f32[12,4096]{1,0:T(8,128)S(1)}, f32[12,4096]{1,0:T(8,128)}, u32[]{:S(2)}) %copy-start.2) | copy-done | bytes 196632
  3.9 0.9 %copy-done.3 = bf16[256,256]{1,0:T(8,128)(2,1)S(1)} copy-done((bf16[256,256]{1,0:T(8,128)(2,1)S(1)}, bf16[256,256]{1,0:T(8,128)(2,1)}, u32[]{:S(2)}) %copy-start.3) | copy-done | bytes 131096
  4.8 0.9 %copy-done.4 = bf16[256,256]{1,0:T(8,128)(2,1)S(1)} copy-done((bf16[256,256]{1,0:T(8,128)(2,1)S(1)}, bf16[256,256]{1,0:T(8,128)(2,1)}, u32[]{:S(2)}) %copy-start.4) | copy-done | bytes 131096
  5.7 0.8 %copy-done.7 = f32[2,32,128]{2,1,0:T(8,128)S(1)} copy-done((f32[2,32,128]{2,1,0:T(8,128)S(1)}, f32[2,32,128]{2,1,0:T(8,128)}, u32[]{:S(2)}) %copy-start.7) | copy-done | bytes 32792
  6.5 0.7 %copy-done.9 = s32[32]{0:T(128)S(1)} copy-done((s32[32]{0:T(128)S(1)}, s32[32]{0:T(128)}, u32[]{:S(2)}) %copy-start.9) | copy-done | bytes 152
  7.2 4.0 %channelise.1 = (bf16[64,1024]{1,0:T(8,128)(2,1)S(1)}, bf16[64,1024]{1,0:T(8,128)(2,1)S(1)}, bf16[64,1024]{1,0:T(8,128)(2,1)S(1)}, bf16[64,1024]{1,0:T(8,128)(2,1)S(1)}) custom-call(s32[32]{0:T(128)S(1)} %copy-done.9, bf16[4,19,64,128]{3,2,1,0:T(8,128)(2,1)S(1)} %bitcast.10, f32[12,4096]{1,0:T(8,128)S(1)} %copy-done.2, bf16[256,256]{1,0:T(8,128)(2,1)S(1)} %copy-done.4, ...), custom_call_target="tpu_custom_call" | custom-call | tf_op jit(solution)/shard_map/channelise/pallas_call | solution.py:137
  11.1 3.1 %collective-permute-start = (bf16[64,1024]{1,0:T(8,128)(2,1)S(1)}, bf16[64,1024]{1,0:T(8,128)(2,1)S(1)}, u32[]{:S(2)}, u32[]{:S(2)}) collective-permute-start(bf16[64,1024]{1,0:T(8,128)(2,1)S(1)} %get-tuple-element.14), channel_id=1, source_target_pairs={{0,4},{4,0},{8,12},{12,8},{1,5},{5,1},{9,13},{13,9},{2,6},{6,2},{1... | collective-permute-start | bytes 393224 | tf_op jit(solution)/shard_map/ppermute | solution.py:446
  14.3 2.6 %collective-permute-start.1 = (bf16[64,1024]{1,0:T(8,128)(2,1)S(1)}, bf16[64,1024]{1,0:T(8,128)(2,1)S(1)}, u32[]{:S(2)}, u32[]{:S(2)}) collective-permute-start(bf16[64,1024]{1,0:T(8,128)(2,1)S(1)} %get-tuple-element.15), channel_id=1, source_target_pairs={{0,8},{4,12},{8,0},{12,4},{1,9},{5,13},{9,1},{13,5},{2,10},{6,14},... | collective-permute-start | bytes 393224 | tf_op jit(solution)/shard_map/ppermute | solution.py:446
  16.8 2.5 %collective-permute-done.refs_1_ = bf16[64,1024]{1,0:T(8,128)(2,1)S(1)} collective-permute-done((bf16[64,1024]{1,0:T(8,128)(2,1)S(1)}, bf16[64,1024]{1,0:T(8,128)(2,1)S(1)}, u32[]{:S(2)}, u32[]{:S(2)}) %collective-permute-start) | collective-permute-done | bytes 131104 | tf_op jit(solution)/shard_map/ppermute | solution.py:446
  19.3 7.8 %collective-permute-done.1.refs_2_ = bf16[64,1024]{1,0:T(8,128)(2,1)S(1)} collective-permute-done((bf16[64,1024]{1,0:T(8,128)(2,1)S(1)}, bf16[64,1024]{1,0:T(8,128)(2,1)S(1)}, u32[]{:S(2)}, u32[]{:S(2)}) %collective-permute-start.1) | collective-permute-done | bytes 131104 | tf_op jit(solution)/shard_map/ppermute | solution.py:446
  27.1 1.5 %collective-permute-start.7 = (bf16[64,1024]{1,0:T(8,128)(2,1)S(1)}, bf16[64,1024]{1,0:T(8,128)(2,1)S(1)}, u32[]{:S(2)}, u32[]{:S(2)}) collective-permute-start(bf16[64,1024]{1,0:T(8,128)(2,1)S(1)} %get-tuple-element.13.refs_0_), channel_id=1, source_target_pairs={{0,2},{2,0},{1,3},{3,1},{4,6},{6,4},{5,7},{7,5},{8,10},{10,8},{9,1... | collective-permute-start | bytes 393224 | tf_op jit(solution)/shard_map/ppermute | solution.py:446
  29.4 1.5 %collective-permute-start.9 = (bf16[64,1024]{1,0:T(8,128)(2,1)S(1)}, bf16[64,1024]{1,0:T(8,128)(2,1)S(1)}, u32[]{:S(2)}, u32[]{:S(2)}) collective-permute-start(bf16[64,1024]{1,0:T(8,128)(2,1)S(1)} %collective-permute-done.1.refs_2_), channel_id=1, source_target_pairs={{0,2},{2,0},{1,3},{3,1},{4,6},{6,4},{5,7},{7,5},{8,10},{10,8},{9,1... | collective-permute-start | bytes 393224 | tf_op jit(solution)/shard_map/ppermute | solution.py:446
  30.9 0.5 %collective-permute-start.10 = (bf16[64,1024]{1,0:T(8,128)(2,1)S(1)}, bf16[64,1024]{1,0:T(8,128)(2,1)S(1)}, u32[]{:S(2)}, u32[]{:S(2)}) collective-permute-start(bf16[64,1024]{1,0:T(8,128)(2,1)S(1)} %collective-permute-done.2.refs_3_), channel_id=1, source_target_pairs={{0,2},{2,0},{1,3},{3,1},{4,6},{6,4},{5,7},{7,5},{8,10},{10,8},{9,1... | collective-permute-start | bytes 393224 | tf_op jit(solution)/shard_map/ppermute | solution.py:446
  31.4 1.0 %correlate_near.1 = (f32[256,64]{1,0:T(8,128)S(1)}, bf16[8,64,1024]{2,1,0:T(8,128)(2,1)S(1)}, bf16[256,512]{1,0:T(8,128)(2,1)S(1)}, bf16[32,128]{1,0:T(8,128)(2,1)S(1)}) custom-call(bf16[64,1024]{1,0:T(8,128)(2,1)S(1)} %get-tuple-element.13.refs_0_, bf16[64,1024]{1,0:T(8,128)(2,1)S(1)} %collective-permute-done.refs_1_, ...), custom_call_target="tpu_custom_call" | custom-call | tf_op jit(solution)/shard_map/correlate_near/pallas_call | solution.py:343
  32.4 1.1 %collective-permute-done.7.refs_0_.refs_4_ = bf16[64,1024]{1,0:T(8,128)(2,1)S(1)} collective-permute-done((bf16[64,1024]{1,0:T(8,128)(2,1)S(1)}, bf16[64,1024]{1,0:T(8,128)(2,1)S(1)}, u32[]{:S(2)}, u32[]{:S(2)}) %collective-permute-start.7) | collective-permute-done | bytes 131104 | tf_op jit(solution)/shard_map/ppermute | solution.py:446
  33.5 2.8 %collective-permute-done.8.refs_1_.refs_5_ = bf16[64,1024]{1,0:T(8,128)(2,1)S(1)} collective-permute-done((bf16[64,1024]{1,0:T(8,128)(2,1)S(1)}, bf16[64,1024]{1,0:T(8,128)(2,1)S(1)}, u32[]{:S(2)}, u32[]{:S(2)}) %collective-permute-start.8) | collective-permute-done | bytes 131104 | tf_op jit(solution)/shard_map/ppermute | solution.py:446
  36.3 2.8 %collective-permute-done.9.refs_2_.refs_6_ = bf16[64,1024]{1,0:T(8,128)(2,1)S(1)} collective-permute-done((bf16[64,1024]{1,0:T(8,128)(2,1)S(1)}, bf16[64,1024]{1,0:T(8,128)(2,1)S(1)}, u32[]{:S(2)}, u32[]{:S(2)}) %collective-permute-start.9) | collective-permute-done | bytes 131104 | tf_op jit(solution)/shard_map/ppermute | solution.py:446
  39.1 2.3 %collective-permute-done.10.refs_3_.refs_7_ = bf16[64,1024]{1,0:T(8,128)(2,1)S(1)} collective-permute-done((bf16[64,1024]{1,0:T(8,128)(2,1)S(1)}, bf16[64,1024]{1,0:T(8,128)(2,1)S(1)}, u32[]{:S(2)}, u32[]{:S(2)}) %collective-permute-start.10) | collective-permute-done | bytes 131104 | tf_op jit(solution)/shard_map/ppermute | solution.py:446
  41.5 1.2 %correlate_far.1 = (f32[256,64]{1,0:T(8,128)S(1)}, f32[256,64]{1,0:T(8,128)S(1)}) custom-call(f32[256,64]{1,0:T(8,128)S(1)} %get-tuple-element.17.part_ref, bf16[8,64,1024]{2,1,0:T(8,128)(2,1)S(1)} %get-tuple-element.18.packed, bf16[256,512]{1,0:T(8,128)(2,1)S(1)} %get-tuple-element.19.merge_ref, bf16[32,128]{1,0:T(8,128)(2,1)S(1)} %get-tuple-element.20.far_ref, ...), custom_call_target="tpu_custom_call" | custom-call | tf_op jit(solution)/shard_map/correlate_far/pallas_call | solution.py:362
  42.8 3.0 %framed_weights.1.weight_ref = bf16[4000,512]{1,0:T(8,128)(2,1)S(1)} custom-call(f32[2,16]{1,0:T(2,128)S(1)} %copy-done.8, s32[32,500]{1,0:T(8,128)S(1)} %bitcast.11, bf16[64,512]{1,0:T(8,128)(2,1)S(1)} %copy-done.6), custom_call_target="tpu_custom_call" | custom-call | tf_op jit(solution)/shard_map/framed_weights/pallas_call | solution.py:255
  45.9 6.7 %beamform.1 = f32[4000,1024]{1,0:T(8,128)} custom-call(bf16[4000,512]{1,0:T(8,128)(2,1)S(1)} %framed_weights.1.weight_ref, bf16[64,1024]{1,0:T(8,128)(2,1)S(1)} %get-tuple-element.13.refs_0_, bf16[64,1024]{1,0:T(8,128)(2,1)S(1)} %collective-permute-done.refs_1_, bf16[64,1024]{1,0:T(8,128)(2,1)S(1)} %collective-permute-done.1.refs_2_, ...), custom_call_target="tpu_custom_call" | custom-call | tf_op jit(solution)/shard_map/beamform/pallas_call | solution.py:423
  52.6 0.7 %add.3 = f32[256,64]{1,0:T(8,128)} add(f32[256,64]{1,0:T(8,128)S(1)} %get-tuple-element.21, f32[256,64]{1,0:T(8,128)S(1)} %collective-permute-done.11) | non-fusion elementwise | flops 16384 | bytes 196608 | tf_op jit(solution)/shard_map/add | solution.py:478
  (26 shorter events, 0.9 us)
Async XLA Ops:
  0.6 42.2 %copy-start.8 = (f32[2,16]{1,0:T(2,128)S(1)}, f32[2,16]{1,0:T(2,128)}, u32[]{:S(2)}) copy-start(f32[2,16]{1,0:T(2,128)} %table_ref.1) | copy-start | bytes 388
  0.6 1.3 %copy-start = (bf16[1,4,1,19,2,4096]{5,4,3,2,1,0:T(2,128)(2,1)S(1)}, bf16[1,4,1,19,2,4096]{5,4,3,2,1,0:T(2,128)(2,1)}, u32[]{:S(2)}) copy-start(bf16[1,4,1,19,2,4096]{5,4,3,2,1,0:T(2,128)(2,1)} %param.10) | copy-start | bytes 3735556
  1.9 1.0 %copy-start.1 = (bf16[512,512]{1,0:T(8,128)(2,1)S(1)}, bf16[512,512]{1,0:T(8,128)(2,1)}, u32[]{:S(2)}) copy-start(bf16[512,512]{1,0:T(8,128)(2,1)} %constant.13.clone.spread_ref) | copy-start | bytes 1572868
  3.0 0.9 %copy-start.2 = (f32[12,4096]{1,0:T(8,128)S(1)}, f32[12,4096]{1,0:T(8,128)}, u32[]{:S(2)}) copy-start(f32[12,4096]{1,0:T(8,128)} %taps_ref.1) | copy-start | bytes 589828
  3.9 0.9 %copy-start.3 = (bf16[256,256]{1,0:T(8,128)(2,1)S(1)}, bf16[256,256]{1,0:T(8,128)(2,1)}, u32[]{:S(2)}) copy-start(bf16[256,256]{1,0:T(8,128)(2,1)} %constant.12.clone.second_ref) | copy-start | bytes 393220
  4.8 0.9 %copy-start.4 = (bf16[256,256]{1,0:T(8,128)(2,1)S(1)}, bf16[256,256]{1,0:T(8,128)(2,1)}, u32[]{:S(2)}) copy-start(bf16[256,256]{1,0:T(8,128)(2,1)} %constant.10.clone.first_ref) | copy-start | bytes 393220
  5.7 0.8 %copy-start.7 = (f32[2,32,128]{2,1,0:T(8,128)S(1)}, f32[2,32,128]{2,1,0:T(8,128)}, u32[]{:S(2)}) copy-start(f32[2,32,128]{2,1,0:T(8,128)} %constant.11.clone.turn_ref) | copy-start | bytes 98308
  6.5 0.7 %copy-start.9 = (s32[32]{0:T(128)S(1)}, s32[32]{0:T(128)}, u32[]{:S(2)}) copy-start(s32[32]{0:T(128)} %owner_ref.1) | copy-start | bytes 388
  7.2 35.7 %copy-start.5 = (s32[500,32]{0,1:T(8,128)S(1)}, s32[500,32]{0,1:T(8,128)}, u32[]{:S(2)}) copy-start(s32[500,32]{0,1:T(8,128)} %param.13) | copy-start | bytes 192004
  7.2 35.7 %copy-start.6 = (bf16[64,512]{1,0:T(8,128)(2,1)S(1)}, bf16[64,512]{1,0:T(8,128)(2,1)}, u32[]{:S(2)}) copy-start(bf16[64,512]{1,0:T(8,128)(2,1)} %constant.14.clone.copy_ref) | copy-start | bytes 196612
  11.1 8.2 %collective-permute-start = (bf16[64,1024]{1,0:T(8,128)(2,1)S(1)}, bf16[64,1024]{1,0:T(8,128)(2,1)S(1)}, u32[]{:S(2)}, u32[]{:S(2)}) collective-permute-start(bf16[64,1024]{1,0:T(8,128)(2,1)S(1)} %get-tuple-element.14), channel_id=1, source_target_pairs={{0,4},{4,0},{8,12},{12,8},{1,5},{5,1},{9,13},{13,9},{2,6},{6,2},{1... | collective-permute-start | bytes 393224 | tf_op jit(solution)/shard_map/ppermute | solution.py:446
  14.3 12.9 %collective-permute-start.1 = (bf16[64,1024]{1,0:T(8,128)(2,1)S(1)}, bf16[64,1024]{1,0:T(8,128)(2,1)S(1)}, u32[]{:S(2)}, u32[]{:S(2)}) collective-permute-start(bf16[64,1024]{1,0:T(8,128)(2,1)S(1)} %get-tuple-element.15), channel_id=1, source_target_pairs={{0,8},{4,12},{8,0},{12,4},{1,9},{5,13},{9,1},{13,5},{2,10},{6,14},... | collective-permute-start | bytes 393224 | tf_op jit(solution)/shard_map/ppermute | solution.py:446
  16.8 11.8 %collective-permute-start.2 = (bf16[64,1024]{1,0:T(8,128)(2,1)S(1)}, bf16[64,1024]{1,0:T(8,128)(2,1)S(1)}, u32[]{:S(2)}, u32[]{:S(2)}) collective-permute-start(bf16[64,1024]{1,0:T(8,128)(2,1)S(1)} %get-tuple-element.16), channel_id=1, source_target_pairs={{0,12},{4,8},{8,4},{12,0},{1,13},{5,9},{9,5},{13,1},{2,14},{6,10},... | collective-permute-start | bytes 393224 | tf_op jit(solution)/shard_map/ppermute | solution.py:446
  16.8 12.0 %collective-permute-start.3 = (bf16[64,1024]{1,0:T(8,128)(2,1)S(1)}, bf16[64,1024]{1,0:T(8,128)(2,1)S(1)}, u32[]{:S(2)}, u32[]{:S(2)}) collective-permute-start(bf16[64,1024]{1,0:T(8,128)(2,1)S(1)} %get-tuple-element.13.refs_0_), channel_id=1, source_target_pairs={{0,1},{1,0},{2,3},{3,2},{4,5},{5,4},{6,7},{7,6},{8,9},{9,8},{10,11... | collective-permute-start | bytes 393224 | tf_op jit(solution)/shard_map/ppermute | solution.py:446
  19.3 10.1 %collective-permute-start.4 = (bf16[64,1024]{1,0:T(8,128)(2,1)S(1)}, bf16[64,1024]{1,0:T(8,128)(2,1)S(1)}, u32[]{:S(2)}, u32[]{:S(2)}) collective-permute-start(bf16[64,1024]{1,0:T(8,128)(2,1)S(1)} %collective-permute-done.refs_1_), channel_id=1, source_target_pairs={{0,1},{1,0},{2,3},{3,2},{4,5},{5,4},{6,7},{7,6},{8,9},{9,8},{10,11... | collective-permute-start | bytes 393224 | tf_op jit(solution)/shard_map/ppermute | solution.py:446
  27.1 3.8 %collective-permute-start.5 = (bf16[64,1024]{1,0:T(8,128)(2,1)S(1)}, bf16[64,1024]{1,0:T(8,128)(2,1)S(1)}, u32[]{:S(2)}, u32[]{:S(2)}) collective-permute-start(bf16[64,1024]{1,0:T(8,128)(2,1)S(1)} %collective-permute-done.1.refs_2_), channel_id=1, source_target_pairs={{0,1},{1,0},{2,3},{3,2},{4,5},{5,4},{6,7},{7,6},{8,9},{9,8},{10,11... | collective-permute-start | bytes 393224 | tf_op jit(solution)/shard_map/ppermute | solution.py:446
  27.1 6.4 %collective-permute-start.7 = (bf16[64,1024]{1,0:T(8,128)(2,1)S(1)}, bf16[64,1024]{1,0:T(8,128)(2,1)S(1)}, u32[]{:S(2)}, u32[]{:S(2)}) collective-permute-start(bf16[64,1024]{1,0:T(8,128)(2,1)S(1)} %get-tuple-element.13.refs_0_), channel_id=1, source_target_pairs={{0,2},{2,0},{1,3},{3,1},{4,6},{6,4},{5,7},{7,5},{8,10},{10,8},{9,1... | collective-permute-start | bytes 393224 | tf_op jit(solution)/shard_map/ppermute | solution.py:446
  28.6 2.8 %collective-permute-start.6 = (bf16[64,1024]{1,0:T(8,128)(2,1)S(1)}, bf16[64,1024]{1,0:T(8,128)(2,1)S(1)}, u32[]{:S(2)}, u32[]{:S(2)}) collective-permute-start(bf16[64,1024]{1,0:T(8,128)(2,1)S(1)} %collective-permute-done.2.refs_3_), channel_id=1, source_target_pairs={{0,1},{1,0},{2,3},{3,2},{4,5},{5,4},{6,7},{7,6},{8,9},{9,8},{10,11... | collective-permute-start | bytes 393224 | tf_op jit(solution)/shard_map/ppermute | solution.py:446
  28.9 7.5 %collective-permute-start.8 = (bf16[64,1024]{1,0:T(8,128)(2,1)S(1)}, bf16[64,1024]{1,0:T(8,128)(2,1)S(1)}, u32[]{:S(2)}, u32[]{:S(2)}) collective-permute-start(bf16[64,1024]{1,0:T(8,128)(2,1)S(1)} %collective-permute-done.refs_1_), channel_id=1, source_target_pairs={{0,2},{2,0},{1,3},{3,1},{4,6},{6,4},{5,7},{7,5},{8,10},{10,8},{9,1... | collective-permute-start | bytes 393224 | tf_op jit(solution)/shard_map/ppermute | solution.py:446
  29.4 9.7 %collective-permute-start.9 = (bf16[64,1024]{1,0:T(8,128)(2,1)S(1)}, bf16[64,1024]{1,0:T(8,128)(2,1)S(1)}, u32[]{:S(2)}, u32[]{:S(2)}) collective-permute-start(bf16[64,1024]{1,0:T(8,128)(2,1)S(1)} %collective-permute-done.1.refs_2_), channel_id=1, source_target_pairs={{0,2},{2,0},{1,3},{3,1},{4,6},{6,4},{5,7},{7,5},{8,10},{10,8},{9,1... | collective-permute-start | bytes 393224 | tf_op jit(solution)/shard_map/ppermute | solution.py:446
  30.9 10.6 %collective-permute-start.10 = (bf16[64,1024]{1,0:T(8,128)(2,1)S(1)}, bf16[64,1024]{1,0:T(8,128)(2,1)S(1)}, u32[]{:S(2)}, u32[]{:S(2)}) collective-permute-start(bf16[64,1024]{1,0:T(8,128)(2,1)S(1)} %collective-permute-done.2.refs_3_), channel_id=1, source_target_pairs={{0,2},{2,0},{1,3},{3,1},{4,6},{6,4},{5,7},{7,5},{8,10},{10,8},{9,1... | collective-permute-start | bytes 393224 | tf_op jit(solution)/shard_map/ppermute | solution.py:446
  42.7 9.8 %collective-permute-start.11 = (f32[256,64]{1,0:T(8,128)S(1)}, f32[256,64]{1,0:T(8,128)S(1)}, u32[]{:S(2)}, u32[]{:S(2)}) collective-permute-start(f32[256,64]{1,0:T(8,128)S(1)} %get-tuple-element.22), channel_id=1, source_target_pairs={{0,1},{1,0},{2,3},{3,2},{4,5},{5,4},{6,7},{7,6},{8,9},{9,8},{10,11... | collective-permute-start | bytes 196616 | tf_op jit(solution)/shard_map/ppermute | solution.py:446

commit v3 on v2

--- a/solution.py
+++ b/solution.py
@@ -33,9 +33,9 @@
     return bf(first), jnp.asarray(np.stack([turn_cos, turn_sin]), jnp.float32), bf(second), bf(spread)
 
 
-def channel_kernel(owners, owner_ref, volt_ref, taps_ref, first_ref, turn_ref, second_ref, spread_ref, *rest):
+def channel_kernel(owners, owner_ref, volt_ref, taps_hbm, first_ref, turn_ref, second_ref, spread_ref, *rest):
     outs = rest[:owners]
-    volts, tap_rows, first, turn, second, spread, filt, wide, pick, sems = rest[owners:]
+    volts, taps_ref, tap_rows, first, turn, second, spread, filt, wide, pick, sems = rest[owners:]
     stations, blocks, rows, _ = volt_ref.shape
     taps = taps_ref.shape[0]
     frames = blocks - taps + 1
@@ -46,6 +46,8 @@
     quads = LANES // depth
     span = HALF * depth
     here = lax.axis_index("chan")
+    tap_copy = pltpu.make_async_copy(taps_hbm, taps_ref, sems.at[stations + 4])
+    tap_copy.start()
     copies = []
     for s in range(stations):
         copies.append(pltpu.make_async_copy(volt_ref.at[s], volts.at[s], sems.at[s]))
@@ -54,6 +56,7 @@
         consts.append(pltpu.make_async_copy(src, dst, sems.at[stations + i]))
     for c in copies + consts:
         c.start()
+    tap_copy.wait()
 
     sub = lax.broadcasted_iota(jnp.int32, (8, LANES), 0)
     for t in range(taps):
@@ -132,15 +135,16 @@
     first, turn, second, spread = channel_tables(nfft, groups)
     sc = 2 * stations
     width = groups // owners
-    anyspec = pl.BlockSpec(memory_space=pl.ANY)
+    anyspec = pl.BlockSpec(memory_space=pltpu.HBM)
     bf = jnp.bfloat16
     return pl.pallas_call(
         functools.partial(channel_kernel, owners),
         out_shape=[jax.ShapeDtypeStruct((frames * sc, width * LANES), bf)] * owners,
-        in_specs=[pl.BlockSpec(memory_space=pltpu.SMEM), anyspec, pl.BlockSpec(memory_space=pltpu.VMEM)] + [anyspec] * 4,
+        in_specs=[pl.BlockSpec(memory_space=pltpu.SMEM)] + [anyspec] * 6,
         out_specs=[pl.BlockSpec(memory_space=pltpu.VMEM)] * owners,
         scratch_shapes=[
             pltpu.VMEM(volts.shape, bf),
+            pltpu.VMEM(filter_taps.shape, jnp.float32),
             pltpu.VMEM((taps, 2 * depth, LANES), jnp.float32),
             pltpu.VMEM(first.shape, bf),
             pltpu.VMEM(turn.shape, jnp.float32),
@@ -149,9 +153,8 @@
             pltpu.VMEM((stations, HALF * 2 * depth, frames // HALF * LANES), bf),
             pltpu.VMEM((frames // HALF, sc * groups, spread.shape[0]), bf),
             pltpu.VMEM((groups * sc, sc * groups), bf),
-            pltpu.SemaphoreType.DMA((stations + 4,)),
+            pltpu.SemaphoreType.DMA((stations + 5,)),
         ],
-        compiler_params=grant(),
         name="channelise",
     )(block_owner, volts, filter_taps, first, turn, second, spread)
 
@@ -188,7 +191,7 @@
     return lax.dot_general(a, b, (((1,), (1,)), ((), ())), preferred_element_type=jnp.float32)
 
 
-def weights_kernel(pairs, owned, share, table_ref, index_ref, copy_ref, out_ref, rows_ref):
+def weights_kernel(pairs, owned, share, table_ref, index_hbm, copy_hbm, out_ref, rows_ref, index_ref, copy_ref, sems):
     stations, beams = index_ref.shape
     tile, spread = copy_ref.shape
     frames = spread // tile
@@ -197,6 +200,14 @@
     factor = 1.0 / math.sqrt(stations)
 
     def prepare():
+        loads = [
+            pltpu.make_async_copy(index_hbm, index_ref, sems.at[0]),
+            pltpu.make_async_copy(copy_hbm, copy_ref, sems.at[1]),
+        ]
+        for load in loads:
+            load.start()
+        for load in loads:
+            load.wait()
         row = lax.broadcasted_iota(jnp.int32, (count, beams), 0)
         lane = lax.broadcasted_iota(jnp.int32, (count, beams), 1)
         hit = lane == start + (row >> 1)
@@ -255,9 +266,14 @@
     return pl.pallas_call(
         functools.partial(weights_kernel, pairs, owned, share),
         out_shape=jax.ShapeDtypeStruct((count * frames, depth), jnp.bfloat16),
-        in_specs=[smem] + whole_vmem(2),
-        scratch_shapes=[pltpu.VMEM((count, depth), jnp.float32)],
-        compiler_params=grant() if resident else None,
+        in_specs=[smem] + [pl.BlockSpec(memory_space=pltpu.HBM)] * 2,
+        scratch_shapes=[
+            pltpu.VMEM((count, depth), jnp.float32),
+            pltpu.VMEM(inputs[1].shape, jnp.int32),
+            pltpu.VMEM(inputs[2].shape, jnp.bfloat16),
+            pltpu.SemaphoreType.DMA((2,)),
+        ],
+        compiler_params=grant(52 * 2**20) if resident else None,
         name="framed_weights",
         **extra,
     )(*inputs)
@@ -285,7 +301,7 @@
 
 def near_kernel(owners, sections, frames, *refs):
     mine, twin = refs[:owners], refs[owners : 2 * owners]
-    part_ref, packed, merge_ref, far_ref = refs[2 * owners :]
+    part_ref, packed, merge_ref, far_ref, theirs = refs[2 * owners :]
     width = packed.shape[0]
     pairs = mine[0].shape[0] // frames
     block = owners * pairs
@@ -293,7 +309,7 @@
     inputs = part_ref.shape[1]
     here, section, pol = lax.axis_index("chan"), lax.axis_index("stat"), lax.axis_index("pol")
     pack(packed, 0, mine, frames)
-    pack(packed, 1, twin, frames)
+    pack(theirs, 0, twin, frames)
     one, zero = jnp.float32(1), jnp.float32(0)
 
     def spread_of(slots, source, there):
@@ -305,7 +321,9 @@
         return jnp.where(wide == target + (rest & 1) * inputs, one, zero).astype(jnp.bfloat16)
 
     near = spread_of(2, lambda slot: section, lambda slot: pol ^ slot)
-    far_ref[...] = spread_of(sections - 1, lambda slot: section ^ (slot + 1), lambda slot: pol)
+    far_ref[...] = spread_of(
+        2 * (sections - 1), lambda slot: section ^ ((slot >> 1) + 1), lambda slot: pol ^ (slot & 1)
+    )
     height = width * block
     left = lax.broadcasted_iota(jnp.int32, (height, height), 0)
     right = lax.broadcasted_iota(jnp.int32, (1, height), 1)
@@ -317,21 +335,10 @@
     merge_ref[:, :height] = jnp.where(left == aim + part * members, scale, zero).astype(jnp.bfloat16)
     sign = jnp.where(part == 1, scale, -scale)
     merge_ref[:, height:] = jnp.where(left == aim + (1 - part) * members, sign, zero).astype(jnp.bfloat16)
-    products = [dot_tt(packed[j, :block], packed[j]) for j in range(width)]
+    products = [
+        jnp.concatenate([dot_tt(packed[j], packed[j]), dot_tt(packed[j], theirs[j])], 1) for j in range(width)
+    ]
     part_ref[...] = settle(products, near, merge_ref[...]) * (1.0 / (frames * LANES))
-
-
-def far_kernel(owners, sections, frames, part_ref, packed, merge_ref, far_ref, *refs):
-    others = refs[: owners * (sections - 1)]
-    out_ref, cross_ref, theirs = refs[owners * (sections - 1) :]
-    width, double, _ = packed.shape
-    block = double // 2
-    for x in range(sections - 1):
-        pack(theirs, x, others[x * owners : (x + 1) * owners], frames)
-    products = [dot_tt(packed[j], theirs[j]) for j in range(width)]
-    factor = 1.0 / (frames * LANES)
-    out_ref[...] = part_ref[...] + settle([p[:block] for p in products], far_ref[...], merge_ref[...]) * factor
-    cross_ref[...] = settle([p[block:] for p in products], far_ref[...], merge_ref[...]) * factor
 
 
 def correlate_near(mine, twin, frames, sections):
@@ -344,30 +351,22 @@
         functools.partial(near_kernel, owners, sections, frames),
         out_shape=[
             jax.ShapeDtypeStruct((width * block, inputs), jnp.float32),
-            jax.ShapeDtypeStruct((width, 2 * block, frames * LANES), bf),
+            jax.ShapeDtypeStruct((width, block, frames * LANES), bf),
             jax.ShapeDtypeStruct((width * block, 2 * width * block), bf),
-            jax.ShapeDtypeStruct(((sections - 1) * block, 2 * inputs), bf),
+            jax.ShapeDtypeStruct((2 * (sections - 1) * block, 2 * inputs), bf),
         ],
         in_specs=whole_vmem(2 * owners),
         out_specs=whole_vmem(4),
+        scratch_shapes=[pltpu.VMEM((width, block, frames * LANES), bf)],
         compiler_params=grant(),
         name="correlate_near",
     )(*mine, *twin)
 
 
-def correlate_far(near, others, owners, frames, sections):
-    part, packed, merge, far = near
-    shape = jax.ShapeDtypeStruct(part.shape, jnp.float32)
-    width, double, lanes = packed.shape
-    return pl.pallas_call(
-        functools.partial(far_kernel, owners, sections, frames),
-        out_shape=[shape, shape],
-        in_specs=whole_vmem(4 + len(others)),
-        out_specs=whole_vmem(2),
-        scratch_shapes=[pltpu.VMEM((width, (sections - 1) * double // 2, lanes), jnp.bfloat16)],
-        compiler_params=grant(),
-        name="correlate_far",
-    )(part, packed, merge, far, *others)
+def far_products(packed, theirs, others, frames):
+    for slot, blocks in enumerate(others):
+        pack(theirs, slot, blocks, frames)
+    return [dot_tt(packed[j], theirs[j]) for j in range(packed.shape[0])]
 
 
 def gather_rows(data, blocks, owners, sections):
@@ -379,14 +378,14 @@
             data[pl.ds(pl.multiple_of(at, rows), rows), :] = blocks[x * owners + k][...]
 
 
-def beams_resident(owners, sections, share, span, weight_ref, *refs):
-    blocks, (out_ref, data, held, sems) = refs[:-4], refs[-4:]
-    gather_rows(data, blocks, owners, sections)
+def finish_kernel(owners, sections, frames, share, span, weight_ref, part_ref, packed, merge_ref, far_ref, *refs):
+    count = owners * sections
+    blocks, crossed = refs[:count], refs[count : 2 * count - owners]
+    out_ref, vis_ref, data, theirs, vis, held, sems, *chunk = refs[2 * count - owners :]
     slots = held.shape[0]
-    steps = []
-    for row in range(0, weight_ref.shape[0], share):
-        for lane in range(0, data.shape[1], span):
-            steps.append((row, lane))
+    height, lanes = out_ref.shape
+    steps = [(row, lane) for row in range(0, height, share) for lane in range(0, lanes, span)]
+    vis_copy = pltpu.make_async_copy(vis, vis_ref, sems.at[slots])
 
     def copy(i):
         row, lane = steps[i]
@@ -394,52 +393,60 @@
             held.at[i % slots], out_ref.at[pl.ds(row, share), pl.ds(lane, span)], sems.at[i % slots]
         )
 
+    gather_rows(data, blocks, owners, sections)
     for i, (row, lane) in enumerate(steps):
         if i >= slots:
             copy(i - slots).wait()
-        held[i % slots] = jnp.dot(
-            weight_ref[row : row + share, :], data[:, lane : lane + span], preferred_element_type=jnp.float32
-        )
+        if chunk:
+            load = pltpu.make_async_copy(weight_ref.at[pl.ds(row, share)], chunk[0], sems.at[slots + 1])
+            load.start()
+            load.wait()
+            weights = chunk[0][...]
+        else:
+            weights = weight_ref[row : row + share, :]
+        held[i % slots] = jnp.dot(weights, data[:, lane : lane + span], preferred_element_type=jnp.float32)
         copy(i).start()
+        if i == min(slots, len(steps)) - 1:
+            others = []
+            for x in range(1, sections):
+                others.append(blocks[x * owners : (x + 1) * owners])
+                others.append(crossed[(x - 1) * owners : x * owners])
+            products = far_products(packed, theirs, others, frames)
+            vis[...] = part_ref[...] + settle(products, far_ref[...], merge_ref[...]) * (1.0 / (frames * LANES))
+            vis_copy.start()
     for i in range(max(0, len(steps) - slots), len(steps)):
         copy(i).wait()
-
-
-def beams_streamed(owners, sections, weight_ref, *refs):
-    blocks, (out_ref, data) = refs[:-2], refs[-2:]
-    pl.when(pl.program_id(0) == 0)(lambda: gather_rows(data, blocks, owners, sections))
-    out_ref[...] = jnp.dot(weight_ref[...], data[...], preferred_element_type=jnp.float32)
-
-
-def beamform(weights, blocks, owners, sections):
+    vis_copy.wait()
+
+
+def finish(weights, near, mine, others, crossed, frames, sections):
+    owners = len(mine)
     height, depth = weights.shape
-    rows, lanes = blocks[0].shape
-    shape = jax.ShapeDtypeStruct((height, lanes), jnp.float32)
-    data = pltpu.VMEM((depth, lanes), jnp.bfloat16)
-    if height * depth * 2 <= RESIDENT:
-        span = min(lanes, 512)
-        share = 8 * pieces(height // 8, 100)
-        slots = 4
-        return pl.pallas_call(
-            functools.partial(beams_resident, owners, sections, share, span),
-            out_shape=shape,
-            in_specs=whole_vmem(1 + len(blocks)),
-            out_specs=pl.BlockSpec(memory_space=pl.ANY),
-            scratch_shapes=[data, pltpu.VMEM((slots, share, span), jnp.float32), pltpu.SemaphoreType.DMA((slots,))],
-            compiler_params=grant(),
-            name="beamform",
-        )(weights, *blocks)
-    share = 8 * pieces(height // 8, max(1, 400 * 512 // depth // 8))
-    whole = pl.BlockSpec((rows, lanes), lambda i: (0, 0))
+    _, lanes = mine[0].shape
+    part, packed, merge, far = near
+    width, block, length = packed.shape
+    resident = height * depth * 2 <= RESIDENT
+    span = min(lanes, 512)
+    share = 8 * pieces(height // 8, 100 if resident else 25)
+    slots = 4
+    weight_spec = pl.BlockSpec(memory_space=pltpu.VMEM if resident else pltpu.HBM)
+    chunk = [] if resident else [pltpu.VMEM((share, depth), jnp.bfloat16)]
     return pl.pallas_call(
-        functools.partial(beams_streamed, owners, sections),
-        grid=(height // share,),
-        out_shape=shape,
-        in_specs=[pl.BlockSpec((share, depth), lambda i: (i, 0))] + [whole] * len(blocks),
-        out_specs=pl.BlockSpec((share, lanes), lambda i: (i, 0)),
-        scratch_shapes=[data],
-        name="beamform",
-    )(weights, *blocks)
+        functools.partial(finish_kernel, owners, sections, frames, share, span),
+        out_shape=[jax.ShapeDtypeStruct((height, lanes), jnp.float32), jax.ShapeDtypeStruct(part.shape, jnp.float32)],
+        in_specs=[weight_spec] + whole_vmem(4 + 2 * len(others) + owners),
+        out_specs=[pl.BlockSpec(memory_space=pl.ANY)] * 2,
+        scratch_shapes=[
+            pltpu.VMEM((depth, lanes), jnp.bfloat16),
+            pltpu.VMEM((width, 2 * (sections - 1) * block, length), jnp.bfloat16),
+            pltpu.VMEM(part.shape, jnp.float32),
+            pltpu.VMEM((slots, share, span), jnp.float32),
+            pltpu.SemaphoreType.DMA((slots + 2,)),
+        ]
+        + chunk,
+        compiler_params=grant() if resident else None,
+        name="finish",
+    )(weights, part, packed, merge, far, *mine, *others, *crossed)
 
 
 def partner(x, axis, distance):
@@ -463,19 +470,17 @@
     weights = framed_weights(beam_table, beam_index, frames, pairs, owned)
     mine = [own[0]] + [partner(own[k], "chan", k) for k in range(1, owners)]
     lead = max(1, owners // 4)
-    twin, others = [], [[] for _ in range(1, sections)]
+    twin, others, crossed = [], [[] for _ in range(1, sections)], [[] for _ in range(1, sections)]
     for g in range(owners // lead):
         part = mine[g * lead : (g + 1) * lead]
+        twin += moved(part, "pol", 1)
         for x in range(1, sections):
-            others[x - 1] += moved(part, "stat", x)
-        twin += moved(part, "pol", 1)
-    others = sum(others, [])
+            far = moved(part, "stat", x)
+            others[x - 1] += far
+            crossed[x - 1] += moved(far, "pol", 1)
     near = correlate_near(mine, twin, frames, sections)
-    vis, cross = correlate_far(near, others, owners, frames, sections)
-    crossed = partner(cross, "pol", 1)
-    last, _ = lax.optimization_barrier((others[-1], cross))
-    beams = beamform(weights, mine + others[:-1] + [last], owners, sections)
-    vis = (vis + crossed).reshape(groups // owners, 2, -1, vis.shape[1])
+    beams, vis = finish(weights, near, mine, sum(others, []), sum(crossed, []), frames, sections)
+    vis = vis.reshape(groups // owners, 2, -1, vis.shape[1])
     return vis, beams.reshape(owned, 1, 2, frames, -1)
 
 

time: 53.6 us -> 49.5 us (0.924)
  waiting for transfers between devices: 19.4 us -> 12.5 us
  Pallas kernels: 15.9 us -> 19 us
  starting transfers between devices: 10.1 us -> 12.4 us
  local copies, waits for them, and re-layouts: 6.51 us -> 4.52 us
  other arithmetic: 0.67 us -> 0 us
    ppermute x12 -> x15, waiting for transfers between devices: 19.4 us -> 12.5 us  [partner(): lax.ppermute(x, axis, [(i, i ^ distance) for i in range(lax.axis_size(axi...]
    pallas_call x1, Pallas kernels: 3.03 us -> 5.48 us  [framed_weights(): pl.pallas_call(functools.partial(weights_kernel, pairs, owned, share), ou...]
    ppermute x12 -> x15, starting transfers between devices: 10.1 us -> 12.4 us  [partner(): lax.ppermute(x, axis, [(i, i ^ distance) for i in range(lax.axis_size(axi...]
    unnamed x20 -> x10, local copies, waits for them, and re-layouts: 6.51 us -> 4.52 us
    pallas_call x1, Pallas kernels: 3.96 us -> 5.03 us  [channelise(): pl.pallas_call(functools.partial(channel_kernel, owners), out_shape=[jax....]
    add x1 -> x0, other arithmetic: 0.67 us -> none  [on_device(): vis = (vis + crossed).reshape(groups // owners, 2, -1, vis.shape[1])]
    pallas_call x2 -> x1, Pallas kernels: 7.93 us -> 7.44 us  [finish(): pl.pallas_call(functools.partial(finish_kernel, owners, sections, frames,...]
  transfers between devices with their start and end apart: 12 -> 15, of which waited for: 6 -> 4; matrix products, arithmetic and copies ran while one was open for 0% -> 0% of each run, Pallas kernels for 20% -> 13%
where the time goes in v3:
time: 49.5 us; the launch traced here: 49.1 us
  Pallas kernels  19 us (38%)
  waiting for transfers between devices  12.5 us (25%)
  starting transfers between devices  12.4 us (25%)
  local copies, waits for them, and re-layouts  4.52 us (9%)
  between operations  0.73 us (1%)
    ppermute x15, waiting for transfers between devices, partner(): lax.ppermute(x, axis, [(i, i ^ distance) for i in range(lax.axis_size(axi...  12.5 us
    ppermute x15, starting transfers between devices, partner(): lax.ppermute(x, axis, [(i, i ^ distance) for i in range(lax.axis_size(axi...  12.4 us
    pallas_call x1, Pallas kernels, finish(): pl.pallas_call(functools.partial(finish_kernel, owners, sections, frames,...  7.44 us
    pallas_call x1, Pallas kernels, framed_weights(): pl.pallas_call(functools.partial(weights_kernel, pairs, owned, share), ou...  5.48 us
    pallas_call x1, Pallas kernels, channelise(): pl.pallas_call(functools.partial(channel_kernel, owners), out_shape=[jax....  5.03 us
    unnamed x10, local copies, waits for them, and re-layouts  4.52 us
    pallas_call x1, Pallas kernels, correlate_near(): pl.pallas_call(functools.partial(near_kernel, owners, sections, frames),...  1.01 us
  transfers between devices with their start and end apart: 15, of which 4 were waited for; matrix products, arithmetic and copies ran while one was open for 0% of the time, Pallas kernels for 13%

profile of v3, /device:TPU:0, one launch (start us, length us, event | category | flops | bytes accessed | tf_op | source)
XLA Modules:
  0.0 49.1 jit_solution(429099276447032428)
XLA Ops:
  0.6 5.0 %channelise.1 = (bf16[64,1024]{1,0:T(8,128)(2,1)}, bf16[64,1024]{1,0:T(8,128)(2,1)}, bf16[64,1024]{1,0:T(8,128)(2,1)}, bf16[64,1024]{1,0:T(8,128)(2,1)}) custom-call(s32[32]{0:T(128)} %owner_ref.1, bf16[4,19,64,128]{3,2,1,0:T(8,128)(2,1)} %bitcast.11, f32[12,4096]{1,0:T(8,128)} %taps_hbm.1, bf16[256,256]{1,0:T(8,128)(2,1)} %constant.10.clone.first_ref, ...), custom_call_target="tpu_custom_call" | custom-call | tf_op jit(solution)/shard_map/channelise/pallas_call | solution.py:140
  5.7 0.0 copy-start.1
  5.7 3.1 %collective-permute-start = (bf16[64,1024]{1,0:T(8,128)(2,1)}, bf16[64,1024]{1,0:T(8,128)(2,1)S(1)}, u32[]{:S(2)}, u32[]{:S(2)}) collective-permute-start(bf16[64,1024]{1,0:T(8,128)(2,1)} %get-tuple-element.13), channel_id=1, source_target_pairs={{0,4},{4,0},{8,12},{12,8},{1,5},{5,1},{9,13},{13,9},{2,6},{6,2},{1... | collective-permute-start | bytes 393224 | tf_op jit(solution)/shard_map/ppermute | solution.py:453
  8.8 2.6 %collective-permute-start.1 = (bf16[64,1024]{1,0:T(8,128)(2,1)}, bf16[64,1024]{1,0:T(8,128)(2,1)S(1)}, u32[]{:S(2)}, u32[]{:S(2)}) collective-permute-start(bf16[64,1024]{1,0:T(8,128)(2,1)} %get-tuple-element.14), channel_id=1, source_target_pairs={{0,8},{4,12},{8,0},{12,4},{1,9},{5,13},{9,1},{13,5},{2,10},{6,14},... | collective-permute-start | bytes 393224 | tf_op jit(solution)/shard_map/ppermute | solution.py:453
  11.4 1.7 %collective-permute-start.7 = (bf16[64,1024]{1,0:T(8,128)(2,1)}, bf16[64,1024]{1,0:T(8,128)(2,1)S(1)}, u32[]{:S(2)}, u32[]{:S(2)}) collective-permute-start(bf16[64,1024]{1,0:T(8,128)(2,1)} %get-tuple-element.12.refs_0_), channel_id=1, source_target_pairs={{0,2},{2,0},{1,3},{3,1},{4,6},{6,4},{5,7},{7,5},{8,10},{10,8},{9,1... | collective-permute-start | bytes 393224 | tf_op jit(solution)/shard_map/ppermute | solution.py:453
  13.1 1.0 %collective-permute-done.refs_1_ = bf16[64,1024]{1,0:T(8,128)(2,1)S(1)} collective-permute-done((bf16[64,1024]{1,0:T(8,128)(2,1)}, bf16[64,1024]{1,0:T(8,128)(2,1)S(1)}, u32[]{:S(2)}, u32[]{:S(2)}) %collective-permute-start) | collective-permute-done | bytes 131104 | tf_op jit(solution)/shard_map/ppermute | solution.py:453
  14.1 1.7 %collective-permute-start.8 = (bf16[64,1024]{1,0:T(8,128)(2,1)S(1)}, bf16[64,1024]{1,0:T(8,128)(2,1)S(1)}, u32[]{:S(2)}, u32[]{:S(2)}) collective-permute-start(bf16[64,1024]{1,0:T(8,128)(2,1)S(1)} %collective-permute-done.refs_1_), channel_id=1, source_target_pairs={{0,2},{2,0},{1,3},{3,1},{4,6},{6,4},{5,7},{7,5},{8,10},{10,8},{9,1... | collective-permute-start | bytes 393224 | tf_op jit(solution)/shard_map/ppermute | solution.py:453
  15.8 6.1 %collective-permute-done.1.refs_2_ = bf16[64,1024]{1,0:T(8,128)(2,1)S(1)} collective-permute-done((bf16[64,1024]{1,0:T(8,128)(2,1)}, bf16[64,1024]{1,0:T(8,128)(2,1)S(1)}, u32[]{:S(2)}, u32[]{:S(2)}) %collective-permute-start.1) | collective-permute-done | bytes 131104 | tf_op jit(solution)/shard_map/ppermute | solution.py:453
  21.9 1.5 %collective-permute-start.9 = (bf16[64,1024]{1,0:T(8,128)(2,1)S(1)}, bf16[64,1024]{1,0:T(8,128)(2,1)S(1)}, u32[]{:S(2)}, u32[]{:S(2)}) collective-permute-start(bf16[64,1024]{1,0:T(8,128)(2,1)S(1)} %collective-permute-done.1.refs_2_), channel_id=1, source_target_pairs={{0,2},{2,0},{1,3},{3,1},{4,6},{6,4},{5,7},{7,5},{8,10},{10,8},{9,1... | collective-permute-start | bytes 393224 | tf_op jit(solution)/shard_map/ppermute | solution.py:453
  23.4 0.2 collective-permute-start.5
  23.6 0.5 %collective-permute-start.10 = (bf16[64,1024]{1,0:T(8,128)(2,1)S(1)}, bf16[64,1024]{1,0:T(8,128)(2,1)S(1)}, u32[]{:S(2)}, u32[]{:S(2)}) collective-permute-start(bf16[64,1024]{1,0:T(8,128)(2,1)S(1)} %collective-permute-done.2.refs_3_), channel_id=1, source_target_pairs={{0,2},{2,0},{1,3},{3,1},{4,6},{6,4},{5,7},{7,5},{8,10},{10,8},{9,1... | collective-permute-start | bytes 393224 | tf_op jit(solution)/shard_map/ppermute | solution.py:453
  24.2 0.0 collective-permute-start.6
  24.2 0.5 %collective-permute-start.11 = (bf16[64,1024]{1,0:T(8,128)(2,1)S(1)}, bf16[64,1024]{1,0:T(8,128)(2,1)S(1)}, u32[]{:S(2)}, u32[]{:S(2)}) collective-permute-start(bf16[64,1024]{1,0:T(8,128)(2,1)S(1)} %collective-permute-done.7.refs_4_), channel_id=1, source_target_pairs={{0,1},{1,0},{2,3},{3,2},{4,5},{5,4},{6,7},{7,6},{8,9},{9,8},{10,11... | collective-permute-start | bytes 393224 | tf_op jit(solution)/shard_map/ppermute | solution.py:453
  24.7 3.6 %collective-permute-done.9.refs_6_ = bf16[64,1024]{1,0:T(8,128)(2,1)S(1)} collective-permute-done((bf16[64,1024]{1,0:T(8,128)(2,1)S(1)}, bf16[64,1024]{1,0:T(8,128)(2,1)S(1)}, u32[]{:S(2)}, u32[]{:S(2)}) %collective-permute-start.9) | collective-permute-done | bytes 131104 | tf_op jit(solution)/shard_map/ppermute | solution.py:453
  28.3 0.5 %collective-permute-start.13 = (bf16[64,1024]{1,0:T(8,128)(2,1)S(1)}, bf16[64,1024]{1,0:T(8,128)(2,1)S(1)}, u32[]{:S(2)}, u32[]{:S(2)}) collective-permute-start(bf16[64,1024]{1,0:T(8,128)(2,1)S(1)} %collective-permute-done.9.refs_6_), channel_id=1, source_target_pairs={{0,1},{1,0},{2,3},{3,2},{4,5},{5,4},{6,7},{7,6},{8,9},{9,8},{10,11... | collective-permute-start | bytes 393224 | tf_op jit(solution)/shard_map/ppermute | solution.py:453
  28.8 1.8 %collective-permute-done.10.refs_7_ = bf16[64,1024]{1,0:T(8,128)(2,1)S(1)} collective-permute-done((bf16[64,1024]{1,0:T(8,128)(2,1)S(1)}, bf16[64,1024]{1,0:T(8,128)(2,1)S(1)}, u32[]{:S(2)}, u32[]{:S(2)}) %collective-permute-start.10) | collective-permute-done | bytes 131104 | tf_op jit(solution)/shard_map/ppermute | solution.py:453
  30.6 0.8 %copy-done.2 = s32[500,32]{0,1:T(8,128)S(1)} copy-done((s32[500,32]{0,1:T(8,128)S(1)}, s32[500,32]{0,1:T(8,128)}, u32[]{:S(2)}) %copy-start.2) | copy-done | bytes 64024
  31.5 0.8 %copy-done.3 = bf16[64,512]{1,0:T(8,128)(2,1)S(1)} copy-done((bf16[64,512]{1,0:T(8,128)(2,1)S(1)}, bf16[64,512]{1,0:T(8,128)(2,1)}, u32[]{:S(2)}) %copy-start.3) | copy-done | bytes 65560
  32.3 0.7 %copy-done.4 = f32[2,16]{1,0:T(2,128)S(1)} copy-done((f32[2,16]{1,0:T(2,128)S(1)}, f32[2,16]{1,0:T(2,128)}, u32[]{:S(2)}) %copy-start.4) | copy-done | bytes 152
  33.0 5.5 %framed_weights.1.weight_ref = bf16[4000,512]{1,0:T(8,128)(2,1)} custom-call(f32[2,16]{1,0:T(2,128)S(1)} %copy-done.4, s32[32,500]{1,0:T(8,128)S(1)} %bitcast.10, bf16[64,512]{1,0:T(8,128)(2,1)S(1)} %copy-done.3), custom_call_target="tpu_custom_call" | custom-call | tf_op jit(solution)/shard_map/framed_weights/pallas_call | solution.py:266
  38.5 1.0 %correlate_near.1 = (f32[256,64]{1,0:T(8,128)S(1)}, bf16[8,32,1024]{2,1,0:T(8,128)(2,1)S(1)}, bf16[256,512]{1,0:T(8,128)(2,1)S(1)}, bf16[64,128]{1,0:T(8,128)(2,1)S(1)}) custom-call(bf16[64,1024]{1,0:T(8,128)(2,1)S(1)} %copy-done.1, bf16[64,1024]{1,0:T(8,128)(2,1)S(1)} %collective-permute-done.refs_1_, bf16[64,1024]{1,0:T(8,128)(2,1)S(1)} %collective-permute-done.1.refs_2_, ...), custom_call_target="tpu_custom_call" | custom-call | tf_op jit(solution)/shard_map/correlate_near/pallas_call | solution.py:350
  39.5 0.0 copy-start
  39.6 2.2 %copy-done = bf16[4000,512]{1,0:T(8,128)(2,1)S(1)} copy-done((bf16[4000,512]{1,0:T(8,128)(2,1)S(1)}, bf16[4000,512]{1,0:T(8,128)(2,1)}, u32[]{:S(2)}) %copy-start) | copy-done | bytes 4096024
  41.7 7.4 %finish.1 = (f32[4000,1024]{1,0:T(8,128)}, f32[256,64]{1,0:T(8,128)}) custom-call(bf16[4000,512]{1,0:T(8,128)(2,1)S(1)} %copy-done, f32[256,64]{1,0:T(8,128)S(1)} %get-tuple-element.16.part_ref, bf16[8,32,1024]{2,1,0:T(8,128)(2,1)S(1)} %get-tuple-element.17.packed, bf16[256,512]{1,0:T(8,128)(2,1)S(1)} %get-tuple-element.18.merge_ref, ...), custom_call_target="tpu_custom_call" | custom-call | tf_op jit(solution)/shard_map/finish/pallas_call | solution.py:434
  (20 shorter events, 0.0 us)
Async XLA Ops:
  5.7 32.8 %copy-start.1 = (bf16[64,1024]{1,0:T(8,128)(2,1)S(1)}, bf16[64,1024]{1,0:T(8,128)(2,1)}, u32[]{:S(2)}) copy-start(bf16[64,1024]{1,0:T(8,128)(2,1)} %get-tuple-element.12.refs_0_) | copy-start | bytes 393220
  5.7 8.4 %collective-permute-start = (bf16[64,1024]{1,0:T(8,128)(2,1)}, bf16[64,1024]{1,0:T(8,128)(2,1)S(1)}, u32[]{:S(2)}, u32[]{:S(2)}) collective-permute-start(bf16[64,1024]{1,0:T(8,128)(2,1)} %get-tuple-element.13), channel_id=1, source_target_pairs={{0,4},{4,0},{8,12},{12,8},{1,5},{5,1},{9,13},{13,9},{2,6},{6,2},{1... | collective-permute-start | bytes 393224 | tf_op jit(solution)/shard_map/ppermute | solution.py:453
  8.8 13.1 %collective-permute-start.1 = (bf16[64,1024]{1,0:T(8,128)(2,1)}, bf16[64,1024]{1,0:T(8,128)(2,1)S(1)}, u32[]{:S(2)}, u32[]{:S(2)}) collective-permute-start(bf16[64,1024]{1,0:T(8,128)(2,1)} %get-tuple-element.14), channel_id=1, source_target_pairs={{0,8},{4,12},{8,0},{12,4},{1,9},{5,13},{9,1},{13,5},{2,10},{6,14},... | collective-permute-start | bytes 393224 | tf_op jit(solution)/shard_map/ppermute | solution.py:453
  11.4 10.5 %collective-permute-start.2 = (bf16[64,1024]{1,0:T(8,128)(2,1)}, bf16[64,1024]{1,0:T(8,128)(2,1)S(1)}, u32[]{:S(2)}, u32[]{:S(2)}) collective-permute-start(bf16[64,1024]{1,0:T(8,128)(2,1)} %get-tuple-element.15), channel_id=1, source_target_pairs={{0,12},{4,8},{8,4},{12,0},{1,13},{5,9},{9,5},{13,1},{2,14},{6,10},... | collective-permute-start | bytes 393224 | tf_op jit(solution)/shard_map/ppermute | solution.py:453
  11.4 12.0 %collective-permute-start.7 = (bf16[64,1024]{1,0:T(8,128)(2,1)}, bf16[64,1024]{1,0:T(8,128)(2,1)S(1)}, u32[]{:S(2)}, u32[]{:S(2)}) collective-permute-start(bf16[64,1024]{1,0:T(8,128)(2,1)} %get-tuple-element.12.refs_0_), channel_id=1, source_target_pairs={{0,2},{2,0},{1,3},{3,1},{4,6},{6,4},{5,7},{7,5},{8,10},{10,8},{9,1... | collective-permute-start | bytes 393224 | tf_op jit(solution)/shard_map/ppermute | solution.py:453
  13.1 10.5 %collective-permute-start.3 = (bf16[64,1024]{1,0:T(8,128)(2,1)}, bf16[64,1024]{1,0:T(8,128)(2,1)S(1)}, u32[]{:S(2)}, u32[]{:S(2)}) collective-permute-start(bf16[64,1024]{1,0:T(8,128)(2,1)} %get-tuple-element.12.refs_0_), channel_id=1, source_target_pairs={{0,1},{1,0},{2,3},{3,2},{4,5},{5,4},{6,7},{7,6},{8,9},{9,8},{10,11... | collective-permute-start | bytes 393224 | tf_op jit(solution)/shard_map/ppermute | solution.py:453
  14.1 10.1 %collective-permute-start.8 = (bf16[64,1024]{1,0:T(8,128)(2,1)S(1)}, bf16[64,1024]{1,0:T(8,128)(2,1)S(1)}, u32[]{:S(2)}, u32[]{:S(2)}) collective-permute-start(bf16[64,1024]{1,0:T(8,128)(2,1)S(1)} %collective-permute-done.refs_1_), channel_id=1, source_target_pairs={{0,2},{2,0},{1,3},{3,1},{4,6},{6,4},{5,7},{7,5},{8,10},{10,8},{9,1... | collective-permute-start | bytes 393224 | tf_op jit(solution)/shard_map/ppermute | solution.py:453
  21.9 2.3 %collective-permute-start.4 = (bf16[64,1024]{1,0:T(8,128)(2,1)S(1)}, bf16[64,1024]{1,0:T(8,128)(2,1)S(1)}, u32[]{:S(2)}, u32[]{:S(2)}) collective-permute-start(bf16[64,1024]{1,0:T(8,128)(2,1)S(1)} %collective-permute-done.refs_1_), channel_id=1, source_target_pairs={{0,1},{1,0},{2,3},{3,2},{4,5},{5,4},{6,7},{7,6},{8,9},{9,8},{10,11... | collective-permute-start | bytes 393224 | tf_op jit(solution)/shard_map/ppermute | solution.py:453
  21.9 6.4 %collective-permute-start.9 = (bf16[64,1024]{1,0:T(8,128)(2,1)S(1)}, bf16[64,1024]{1,0:T(8,128)(2,1)S(1)}, u32[]{:S(2)}, u32[]{:S(2)}) collective-permute-start(bf16[64,1024]{1,0:T(8,128)(2,1)S(1)} %collective-permute-done.1.refs_2_), channel_id=1, source_target_pairs={{0,2},{2,0},{1,3},{3,1},{4,6},{6,4},{5,7},{7,5},{8,10},{10,8},{9,1... | collective-permute-start | bytes 393224 | tf_op jit(solution)/shard_map/ppermute | solution.py:453
  23.4 4.9 %collective-permute-start.5 = (bf16[64,1024]{1,0:T(8,128)(2,1)S(1)}, bf16[64,1024]{1,0:T(8,128)(2,1)S(1)}, u32[]{:S(2)}, u32[]{:S(2)}) collective-permute-start(bf16[64,1024]{1,0:T(8,128)(2,1)S(1)} %collective-permute-done.1.refs_2_), channel_id=1, source_target_pairs={{0,1},{1,0},{2,3},{3,2},{4,5},{5,4},{6,7},{7,6},{8,9},{9,8},{10,11... | collective-permute-start | bytes 393224 | tf_op jit(solution)/shard_map/ppermute | solution.py:453
  23.6 7.0 %collective-permute-start.10 = (bf16[64,1024]{1,0:T(8,128)(2,1)S(1)}, bf16[64,1024]{1,0:T(8,128)(2,1)S(1)}, u32[]{:S(2)}, u32[]{:S(2)}) collective-permute-start(bf16[64,1024]{1,0:T(8,128)(2,1)S(1)} %collective-permute-done.2.refs_3_), channel_id=1, source_target_pairs={{0,2},{2,0},{1,3},{3,1},{4,6},{6,4},{5,7},{7,5},{8,10},{10,8},{9,1... | collective-permute-start | bytes 393224 | tf_op jit(solution)/shard_map/ppermute | solution.py:453
  24.2 14.3 %collective-permute-start.6 = (bf16[64,1024]{1,0:T(8,128)(2,1)S(1)}, bf16[64,1024]{1,0:T(8,128)(2,1)S(1)}, u32[]{:S(2)}, u32[]{:S(2)}) collective-permute-start(bf16[64,1024]{1,0:T(8,128)(2,1)S(1)} %collective-permute-done.2.refs_3_), channel_id=1, source_target_pairs={{0,1},{1,0},{2,3},{3,2},{4,5},{5,4},{6,7},{7,6},{8,9},{9,8},{10,11... | collective-permute-start | bytes 393224 | tf_op jit(solution)/shard_map/ppermute | solution.py:453
  24.2 15.3 %collective-permute-start.11 = (bf16[64,1024]{1,0:T(8,128)(2,1)S(1)}, bf16[64,1024]{1,0:T(8,128)(2,1)S(1)}, u32[]{:S(2)}, u32[]{:S(2)}) collective-permute-start(bf16[64,1024]{1,0:T(8,128)(2,1)S(1)} %collective-permute-done.7.refs_4_), channel_id=1, source_target_pairs={{0,1},{1,0},{2,3},{3,2},{4,5},{5,4},{6,7},{7,6},{8,9},{9,8},{10,11... | collective-permute-start | bytes 393224 | tf_op jit(solution)/shard_map/ppermute | solution.py:453
  28.3 11.2 %collective-permute-start.12 = (bf16[64,1024]{1,0:T(8,128)(2,1)S(1)}, bf16[64,1024]{1,0:T(8,128)(2,1)S(1)}, u32[]{:S(2)}, u32[]{:S(2)}) collective-permute-start(bf16[64,1024]{1,0:T(8,128)(2,1)S(1)} %collective-permute-done.8.refs_5_), channel_id=1, source_target_pairs={{0,1},{1,0},{2,3},{3,2},{4,5},{5,4},{6,7},{7,6},{8,9},{9,8},{10,11... | collective-permute-start | bytes 393224 | tf_op jit(solution)/shard_map/ppermute | solution.py:453
  28.3 11.2 %collective-permute-start.13 = (bf16[64,1024]{1,0:T(8,128)(2,1)S(1)}, bf16[64,1024]{1,0:T(8,128)(2,1)S(1)}, u32[]{:S(2)}, u32[]{:S(2)}) collective-permute-start(bf16[64,1024]{1,0:T(8,128)(2,1)S(1)} %collective-permute-done.9.refs_6_), channel_id=1, source_target_pairs={{0,1},{1,0},{2,3},{3,2},{4,5},{5,4},{6,7},{7,6},{8,9},{9,8},{10,11... | collective-permute-start | bytes 393224 | tf_op jit(solution)/shard_map/ppermute | solution.py:453
  30.6 8.9 %collective-permute-start.14 = (bf16[64,1024]{1,0:T(8,128)(2,1)S(1)}, bf16[64,1024]{1,0:T(8,128)(2,1)S(1)}, u32[]{:S(2)}, u32[]{:S(2)}) collective-permute-start(bf16[64,1024]{1,0:T(8,128)(2,1)S(1)} %collective-permute-done.10.refs_7_), channel_id=1, source_target_pairs={{0,1},{1,0},{2,3},{3,2},{4,5},{5,4},{6,7},{7,6},{8,9},{9,8},{10,11... | collective-permute-start | bytes 393224 | tf_op jit(solution)/shard_map/ppermute | solution.py:453
  30.6 0.8 %copy-start.2 = (s32[500,32]{0,1:T(8,128)S(1)}, s32[500,32]{0,1:T(8,128)}, u32[]{:S(2)}) copy-start(s32[500,32]{0,1:T(8,128)} %param.13) | copy-start | bytes 192004
  31.5 0.8 %copy-start.3 = (bf16[64,512]{1,0:T(8,128)(2,1)S(1)}, bf16[64,512]{1,0:T(8,128)(2,1)}, u32[]{:S(2)}) copy-start(bf16[64,512]{1,0:T(8,128)(2,1)} %constant.14.clone.copy_hbm) | copy-start | bytes 196612
  32.3 0.7 %copy-start.4 = (f32[2,16]{1,0:T(2,128)S(1)}, f32[2,16]{1,0:T(2,128)}, u32[]{:S(2)}) copy-start(f32[2,16]{1,0:T(2,128)} %table_ref.1) | copy-start | bytes 388
  39.5 2.2 %copy-start = (bf16[4000,512]{1,0:T(8,128)(2,1)S(1)}, bf16[4000,512]{1,0:T(8,128)(2,1)}, u32[]{:S(2)}) copy-start(bf16[4000,512]{1,0:T(8,128)(2,1)} %framed_weights.1.weight_ref) | copy-start | bytes 12288004

commit v4 on v3

--- a/solution.py
+++ b/solution.py
@@ -33,21 +33,23 @@
     return bf(first), jnp.asarray(np.stack([turn_cos, turn_sin]), jnp.float32), bf(second), bf(spread)
 
 
-def channel_kernel(owners, owner_ref, volt_ref, taps_hbm, first_ref, turn_ref, second_ref, spread_ref, *rest):
+def channel_kernel(owners, owner_hbm, volt_ref, taps_hbm, first_ref, turn_ref, second_ref, spread_ref, *rest):
     outs = rest[:owners]
-    volts, taps_ref, tap_rows, first, turn, second, spread, filt, wide, pick, sems = rest[owners:]
+    owner_ref, volts, taps_ref, tap_rows, first, turn, second, spread, filt, wide, pick, sems = rest[owners:]
     stations, blocks, rows, _ = volt_ref.shape
     taps = taps_ref.shape[0]
     frames = blocks - taps + 1
     halves = frames // HALF
     depth = rows // 2
-    groups = owner_ref.shape[0]
+    groups = owner_hbm.shape[0]
     width = groups // owners
     quads = LANES // depth
     span = HALF * depth
     here = lax.axis_index("chan")
     tap_copy = pltpu.make_async_copy(taps_hbm, taps_ref, sems.at[stations + 4])
     tap_copy.start()
+    owner_copy = pltpu.make_async_copy(owner_hbm, owner_ref, sems.at[stations + 5])
+    owner_copy.start()
     copies = []
     for s in range(stations):
         copies.append(pltpu.make_async_copy(volt_ref.at[s], volts.at[s], sems.at[s]))
@@ -66,6 +68,7 @@
             high = jnp.where(sub < 6, parts[2], parts[3])
             tap_rows[t, pl.ds(8 * m, 8), :] = jnp.where(sub < 4, low, high)
 
+    owner_copy.wait()
     sc = 2 * stations
     lane = lax.broadcasted_iota(jnp.int32, (sc, sc * groups), 1)
     base = lax.broadcasted_iota(jnp.int32, (sc, sc * groups), 0) * groups
@@ -135,14 +138,16 @@
     first, turn, second, spread = channel_tables(nfft, groups)
     sc = 2 * stations
     width = groups // owners
+    inputs = (block_owner, volts, filter_taps, first, turn, second, spread)
     anyspec = pl.BlockSpec(memory_space=pltpu.HBM)
     bf = jnp.bfloat16
     return pl.pallas_call(
         functools.partial(channel_kernel, owners),
         out_shape=[jax.ShapeDtypeStruct((frames * sc, width * LANES), bf)] * owners,
-        in_specs=[pl.BlockSpec(memory_space=pltpu.SMEM)] + [anyspec] * 6,
+        in_specs=[anyspec] * 7,
         out_specs=[pl.BlockSpec(memory_space=pltpu.VMEM)] * owners,
         scratch_shapes=[
+            pltpu.SMEM(block_owner.shape, jnp.int32),
             pltpu.VMEM(volts.shape, bf),
             pltpu.VMEM(filter_taps.shape, jnp.float32),
             pltpu.VMEM((taps, 2 * depth, LANES), jnp.float32),
@@ -153,10 +158,11 @@
             pltpu.VMEM((stations, HALF * 2 * depth, frames // HALF * LANES), bf),
             pltpu.VMEM((frames // HALF, sc * groups, spread.shape[0]), bf),
             pltpu.VMEM((groups * sc, sc * groups), bf),
-            pltpu.SemaphoreType.DMA((stations + 5,)),
+            pltpu.SemaphoreType.DMA((stations + 6,)),
         ],
+        compiler_params=grant(),
         name="channelise",
-    )(block_owner, volts, filter_taps, first, turn, second, spread)
+    )(*[pltpu.with_memory_space_constraint(x, pltpu.HBM) for x in inputs])
 
 
 VMEM_BYTES = 24 * 2**20
@@ -191,7 +197,7 @@
     return lax.dot_general(a, b, (((1,), (1,)), ((), ())), preferred_element_type=jnp.float32)
 
 
-def weights_kernel(pairs, owned, share, table_ref, index_hbm, copy_hbm, out_ref, rows_ref, index_ref, copy_ref, sems):
+def weights_kernel(pairs, owned, share, table_hbm, index_hbm, copy_hbm, out_ref, rows_ref, table_ref, index_ref, copy_ref, sems):
     stations, beams = index_ref.shape
     tile, spread = copy_ref.shape
     frames = spread // tile
@@ -200,10 +206,8 @@
     factor = 1.0 / math.sqrt(stations)
 
     def prepare():
-        loads = [
-            pltpu.make_async_copy(index_hbm, index_ref, sems.at[0]),
-            pltpu.make_async_copy(copy_hbm, copy_ref, sems.at[1]),
-        ]
+        pairs_of = zip((table_hbm, index_hbm, copy_hbm), (table_ref, index_ref, copy_ref))
+        loads = [pltpu.make_async_copy(src, dst, sems.at[i]) for i, (src, dst) in enumerate(pairs_of)]
         for load in loads:
             load.start()
         for load in loads:
@@ -219,8 +223,8 @@
             imag = jnp.zeros(index.shape, jnp.float32)
             for e in range(table_ref.shape[1]):
                 here = index == e
-                real = jnp.where(here, table_ref[0, e], real)
-                imag = jnp.where(here, table_ref[1, e], imag)
+                real = jnp.where(here, jnp.broadcast_to(table_ref[0:1, e : e + 1], index.shape), real)
+                imag = jnp.where(here, jnp.broadcast_to(table_ref[1:2, e : e + 1], index.shape), imag)
             real, imag = real * factor, imag * factor
             upper = jnp.concatenate([real, -imag], 0).astype(jnp.bfloat16)
             lower = jnp.concatenate([imag, real], 0).astype(jnp.bfloat16)
@@ -249,34 +253,33 @@
     lax.fori_loop(0, share, fill, 0, unroll=pieces(share, 10))
 
 
-def framed_weights(beam_table, beam_index, frames, pairs, owned):
-    stations = beam_index.shape[1]
+def weight_inputs(beam_table, beam_index, frames, pairs):
     eye = np.eye
     copies = np.einsum("bp,sq,ct,f->cbspqft", eye(2 * SLICE // pairs), eye(pairs // 2), eye(2), np.ones(frames))
     copies = np.moveaxis(copies, (3, 5, 4, 6), (3, 4, 5, 6)).reshape(2 * SLICE, 2 * SLICE * frames)
+    return beam_table, beam_index.T, jnp.asarray(copies, jnp.bfloat16)
+
+
+def framed_weights(inputs, frames, pairs, owned):
+    stations = inputs[1].shape[0]
     depth = 2 * stations * frames
     count = 2 * owned
     resident = count * frames * depth * 2 <= RESIDENT
     share = count if resident else pieces(count, 10)
-    smem = pl.BlockSpec(memory_space=pltpu.SMEM)
-    inputs = (beam_table, beam_index.T, jnp.asarray(copies, jnp.bfloat16))
     extra = {}
     if not resident:
         extra = dict(grid=(count // share,), out_specs=pl.BlockSpec((share * frames, depth), lambda i: (i, 0)))
     return pl.pallas_call(
         functools.partial(weights_kernel, pairs, owned, share),
         out_shape=jax.ShapeDtypeStruct((count * frames, depth), jnp.bfloat16),
-        in_specs=[smem] + [pl.BlockSpec(memory_space=pltpu.HBM)] * 2,
-        scratch_shapes=[
-            pltpu.VMEM((count, depth), jnp.float32),
-            pltpu.VMEM(inputs[1].shape, jnp.int32),
-            pltpu.VMEM(inputs[2].shape, jnp.bfloat16),
-            pltpu.SemaphoreType.DMA((2,)),
-        ],
-        compiler_params=grant(52 * 2**20) if resident else None,
+        in_specs=[pl.BlockSpec(memory_space=pltpu.HBM)] * 3,
+        scratch_shapes=[pltpu.VMEM((count, depth), jnp.float32)]
+        + [pltpu.VMEM(x.shape, x.dtype) for x in inputs]
+        + [pltpu.SemaphoreType.DMA((3,))],
+        compiler_params=grant() if resident else None,
         name="framed_weights",
         **extra,
-    )(*inputs)
+    )(*[pltpu.with_memory_space_constraint(x, pltpu.HBM) for x in inputs])
 
 
 def pack(packed, slot, blocks, frames):
@@ -466,8 +469,9 @@
     pairs = 2 * stations
     groups = block_owner.shape[0]
     owned = beam_index.shape[0] // sections
+    tables = weight_inputs(beam_table, beam_index, frames, pairs)
     own = channelise(voltages, filter_taps, block_owner, owners)
-    weights = framed_weights(beam_table, beam_index, frames, pairs, owned)
+    weights = framed_weights(tables, frames, pairs, owned)
     mine = [own[0]] + [partner(own[k], "chan", k) for k in range(1, owners)]
     lead = max(1, owners // 4)
     twin, others, crossed = [], [[] for _ in range(1, sections)], [[] for _ in range(1, sections)]

time: 49.5 us -> 41.3 us (0.83)
  local copies, waits for them, and re-layouts: 4.52 us -> 0 us
  Pallas kernels: 19 us -> 15.7 us
    unnamed x10 -> x0, local copies, waits for them, and re-layouts: 4.52 us -> none
    pallas_call x1, Pallas kernels: 5.48 us -> 3.58 us  [framed_weights(): pl.pallas_call(functools.partial(weights_kernel, pairs, owned, share), ou...]
    pallas_call x1, Pallas kernels: 5.03 us -> 3.67 us  [channelise(): pl.pallas_call(functools.partial(channel_kernel, owners), out_shape=[jax....]
  transfers between devices with their start and end apart: 15 -> 15, of which waited for: 4 -> 4; matrix products, arithmetic and copies ran while one was open for 0% -> 0% of each run, Pallas kernels for 13% -> 11%
where the time goes in v4:
time: 41.3 us; the launch traced here: 41.1 us
  Pallas kernels  15.7 us (38%)
  starting transfers between devices  12.4 us (30%)
  waiting for transfers between devices  12.3 us (30%)
  between operations  0.7 us (2%)
    ppermute x15, starting transfers between devices, partner(): lax.ppermute(x, axis, [(i, i ^ distance) for i in range(lax.axis_size(axi...  12.4 us
    ppermute x15, waiting for transfers between devices, partner(): lax.ppermute(x, axis, [(i, i ^ distance) for i in range(lax.axis_size(axi...  12.3 us
    pallas_call x1, Pallas kernels, finish(): pl.pallas_call(functools.partial(finish_kernel, owners, sections, frames,...  7.43 us
    pallas_call x1, Pallas kernels, channelise(): pl.pallas_call(functools.partial(channel_kernel, owners), out_shape=[jax....  3.67 us
    pallas_call x1, Pallas kernels, framed_weights(): pl.pallas_call(functools.partial(weights_kernel, pairs, owned, share), ou...  3.58 us
    pallas_call x1, Pallas kernels, correlate_near(): pl.pallas_call(functools.partial(near_kernel, owners, sections, frames),...  0.99 us
  transfers between devices with their start and end apart: 15, of which 4 were waited for; matrix products, arithmetic and copies ran while one was open for 0% of the time, Pallas kernels for 11%

profile of v4, /device:TPU:0, one launch (start us, length us, event | category | flops | bytes accessed | tf_op | source)
XLA Modules:
  0.0 41.1 jit_solution(13191839258155221301)
XLA Ops:
  0.6 3.7 %channelise.1 = (bf16[64,1024]{1,0:T(8,128)(2,1)S(1)}, bf16[64,1024]{1,0:T(8,128)(2,1)S(1)}, bf16[64,1024]{1,0:T(8,128)(2,1)S(1)}, bf16[64,1024]{1,0:T(8,128)(2,1)S(1)}) custom-call(s32[32]{0:T(128)} %owner_hbm.1, bf16[4,19,64,128]{3,2,1,0:T(8,128)(2,1)} %bitcast.10, f32[12,4096]{1,0:T(8,128)} %taps_hbm.1, bf16[256,256]{1,0:T(8,128)(2,1)} %constant.11.clone.first_ref, ...), custom_call_target="tpu_custom_call" | custom-call | tf_op jit(solution)/shard_map/channelise/pallas_call | solution.py:144
  4.3 3.1 %collective-permute-start = (bf16[64,1024]{1,0:T(8,128)(2,1)S(1)}, bf16[64,1024]{1,0:T(8,128)(2,1)S(1)}, u32[]{:S(2)}, u32[]{:S(2)}) collective-permute-start(bf16[64,1024]{1,0:T(8,128)(2,1)S(1)} %get-tuple-element.13), channel_id=1, source_target_pairs={{0,4},{4,0},{8,12},{12,8},{1,5},{5,1},{9,13},{13,9},{2,6},{6,2},{1... | collective-permute-start | bytes 393224 | tf_op jit(solution)/shard_map/ppermute | solution.py:456
  7.4 2.6 %collective-permute-start.1 = (bf16[64,1024]{1,0:T(8,128)(2,1)S(1)}, bf16[64,1024]{1,0:T(8,128)(2,1)S(1)}, u32[]{:S(2)}, u32[]{:S(2)}) collective-permute-start(bf16[64,1024]{1,0:T(8,128)(2,1)S(1)} %get-tuple-element.14), channel_id=1, source_target_pairs={{0,8},{4,12},{8,0},{12,4},{1,9},{5,13},{9,1},{13,5},{2,10},{6,14},... | collective-permute-start | bytes 393224 | tf_op jit(solution)/shard_map/ppermute | solution.py:456
  10.0 0.0 collective-permute-start.2
  10.0 1.7 %collective-permute-start.7 = (bf16[64,1024]{1,0:T(8,128)(2,1)S(1)}, bf16[64,1024]{1,0:T(8,128)(2,1)S(1)}, u32[]{:S(2)}, u32[]{:S(2)}) collective-permute-start(bf16[64,1024]{1,0:T(8,128)(2,1)S(1)} %get-tuple-element.12.refs_0_), channel_id=1, source_target_pairs={{0,2},{2,0},{1,3},{3,1},{4,6},{6,4},{5,7},{7,5},{8,10},{10,8},{9,1... | collective-permute-start | bytes 393224 | tf_op jit(solution)/shard_map/ppermute | solution.py:456
  11.7 0.0 collective-permute-start.3
  11.7 0.8 %collective-permute-done.refs_1_ = bf16[64,1024]{1,0:T(8,128)(2,1)S(1)} collective-permute-done((bf16[64,1024]{1,0:T(8,128)(2,1)S(1)}, bf16[64,1024]{1,0:T(8,128)(2,1)S(1)}, u32[]{:S(2)}, u32[]{:S(2)}) %collective-permute-start) | collective-permute-done | bytes 131104 | tf_op jit(solution)/shard_map/ppermute | solution.py:456
  12.5 1.7 %collective-permute-start.8 = (bf16[64,1024]{1,0:T(8,128)(2,1)S(1)}, bf16[64,1024]{1,0:T(8,128)(2,1)S(1)}, u32[]{:S(2)}, u32[]{:S(2)}) collective-permute-start(bf16[64,1024]{1,0:T(8,128)(2,1)S(1)} %collective-permute-done.refs_1_), channel_id=1, source_target_pairs={{0,2},{2,0},{1,3},{3,1},{4,6},{6,4},{5,7},{7,5},{8,10},{10,8},{9,1... | collective-permute-start | bytes 393224 | tf_op jit(solution)/shard_map/ppermute | solution.py:456
  14.2 6.1 %collective-permute-done.1.refs_2_ = bf16[64,1024]{1,0:T(8,128)(2,1)S(1)} collective-permute-done((bf16[64,1024]{1,0:T(8,128)(2,1)S(1)}, bf16[64,1024]{1,0:T(8,128)(2,1)S(1)}, u32[]{:S(2)}, u32[]{:S(2)}) %collective-permute-start.1) | collective-permute-done | bytes 131104 | tf_op jit(solution)/shard_map/ppermute | solution.py:456
  20.3 0.0 collective-permute-start.4
  20.3 1.5 %collective-permute-start.9 = (bf16[64,1024]{1,0:T(8,128)(2,1)S(1)}, bf16[64,1024]{1,0:T(8,128)(2,1)S(1)}, u32[]{:S(2)}, u32[]{:S(2)}) collective-permute-start(bf16[64,1024]{1,0:T(8,128)(2,1)S(1)} %collective-permute-done.1.refs_2_), channel_id=1, source_target_pairs={{0,2},{2,0},{1,3},{3,1},{4,6},{6,4},{5,7},{7,5},{8,10},{10,8},{9,1... | collective-permute-start | bytes 393224 | tf_op jit(solution)/shard_map/ppermute | solution.py:456
  21.8 0.2 collective-permute-start.5
  22.0 0.5 %collective-permute-start.10 = (bf16[64,1024]{1,0:T(8,128)(2,1)S(1)}, bf16[64,1024]{1,0:T(8,128)(2,1)S(1)}, u32[]{:S(2)}, u32[]{:S(2)}) collective-permute-start(bf16[64,1024]{1,0:T(8,128)(2,1)S(1)} %collective-permute-done.2.refs_3_), channel_id=1, source_target_pairs={{0,2},{2,0},{1,3},{3,1},{4,6},{6,4},{5,7},{7,5},{8,10},{10,8},{9,1... | collective-permute-start | bytes 393224 | tf_op jit(solution)/shard_map/ppermute | solution.py:456
  22.6 0.0 collective-permute-done.8.refs_5_
  22.6 0.0 collective-permute-start.6
  22.6 0.0 collective-permute-done.4.refs_5_
  22.6 0.5 %collective-permute-start.11 = (bf16[64,1024]{1,0:T(8,128)(2,1)S(1)}, bf16[64,1024]{1,0:T(8,128)(2,1)S(1)}, u32[]{:S(2)}, u32[]{:S(2)}) collective-permute-start(bf16[64,1024]{1,0:T(8,128)(2,1)S(1)} %collective-permute-done.7.refs_4_), channel_id=1, source_target_pairs={{0,1},{1,0},{2,3},{3,2},{4,5},{5,4},{6,7},{7,6},{8,9},{9,8},{10,11... | collective-permute-start | bytes 393224 | tf_op jit(solution)/shard_map/ppermute | solution.py:456
  23.1 3.6 %collective-permute-done.9.refs_6_ = bf16[64,1024]{1,0:T(8,128)(2,1)S(1)} collective-permute-done((bf16[64,1024]{1,0:T(8,128)(2,1)S(1)}, bf16[64,1024]{1,0:T(8,128)(2,1)S(1)}, u32[]{:S(2)}, u32[]{:S(2)}) %collective-permute-start.9) | collective-permute-done | bytes 131104 | tf_op jit(solution)/shard_map/ppermute | solution.py:456
  26.7 0.5 %collective-permute-start.13 = (bf16[64,1024]{1,0:T(8,128)(2,1)S(1)}, bf16[64,1024]{1,0:T(8,128)(2,1)S(1)}, u32[]{:S(2)}, u32[]{:S(2)}) collective-permute-start(bf16[64,1024]{1,0:T(8,128)(2,1)S(1)} %collective-permute-done.9.refs_6_), channel_id=1, source_target_pairs={{0,1},{1,0},{2,3},{3,2},{4,5},{5,4},{6,7},{7,6},{8,9},{9,8},{10,11... | collective-permute-start | bytes 393224 | tf_op jit(solution)/shard_map/ppermute | solution.py:456
  27.2 1.8 %collective-permute-done.10.refs_7_ = bf16[64,1024]{1,0:T(8,128)(2,1)S(1)} collective-permute-done((bf16[64,1024]{1,0:T(8,128)(2,1)S(1)}, bf16[64,1024]{1,0:T(8,128)(2,1)S(1)}, u32[]{:S(2)}, u32[]{:S(2)}) %collective-permute-start.10) | collective-permute-done | bytes 131104 | tf_op jit(solution)/shard_map/ppermute | solution.py:456
  29.0 0.0 collective-permute-start.14
  29.0 3.6 %framed_weights.1.weight_ref = bf16[4000,512]{1,0:T(8,128)(2,1)S(1)} custom-call(f32[2,16]{1,0:T(2,128)} %table_hbm.1, s32[32,500]{1,0:T(8,128)} %bitcast.11, bf16[64,512]{1,0:T(8,128)(2,1)} %constant.10.clone.copy_hbm), custom_call_target="tpu_custom_call" | custom-call | tf_op jit(solution)/shard_map/framed_weights/pallas_call | solution.py:272
  32.6 1.0 %correlate_near.1 = (f32[256,64]{1,0:T(8,128)S(1)}, bf16[8,32,1024]{2,1,0:T(8,128)(2,1)S(1)}, bf16[256,512]{1,0:T(8,128)(2,1)S(1)}, bf16[64,128]{1,0:T(8,128)(2,1)S(1)}) custom-call(bf16[64,1024]{1,0:T(8,128)(2,1)S(1)} %get-tuple-element.12.refs_0_, bf16[64,1024]{1,0:T(8,128)(2,1)S(1)} %collective-permute-done.refs_1_, ...), custom_call_target="tpu_custom_call" | custom-call | tf_op jit(solution)/shard_map/correlate_near/pallas_call | solution.py:353
  33.7 7.4 %finish.1 = (f32[4000,1024]{1,0:T(8,128)}, f32[256,64]{1,0:T(8,128)}) custom-call(bf16[4000,512]{1,0:T(8,128)(2,1)S(1)} %framed_weights.1.weight_ref, f32[256,64]{1,0:T(8,128)S(1)} %get-tuple-element.16.part_ref, bf16[8,32,1024]{2,1,0:T(8,128)(2,1)S(1)} %get-tuple-element.17.packed, bf16[256,512]{1,0:T(8,128)(2,1)S(1)} %get-tuple-element.18.merge_ref, ...), custom_call_target="tpu_custom_call" | custom-call | tf_op jit(solution)/shard_map/finish/pallas_call | solution.py:437
  (10 shorter events, 0.0 us)
Async XLA Ops:
  4.3 8.2 %collective-permute-start = (bf16[64,1024]{1,0:T(8,128)(2,1)S(1)}, bf16[64,1024]{1,0:T(8,128)(2,1)S(1)}, u32[]{:S(2)}, u32[]{:S(2)}) collective-permute-start(bf16[64,1024]{1,0:T(8,128)(2,1)S(1)} %get-tuple-element.13), channel_id=1, source_target_pairs={{0,4},{4,0},{8,12},{12,8},{1,5},{5,1},{9,13},{13,9},{2,6},{6,2},{1... | collective-permute-start | bytes 393224 | tf_op jit(solution)/shard_map/ppermute | solution.py:456
  7.4 12.9 %collective-permute-start.1 = (bf16[64,1024]{1,0:T(8,128)(2,1)S(1)}, bf16[64,1024]{1,0:T(8,128)(2,1)S(1)}, u32[]{:S(2)}, u32[]{:S(2)}) collective-permute-start(bf16[64,1024]{1,0:T(8,128)(2,1)S(1)} %get-tuple-element.14), channel_id=1, source_target_pairs={{0,8},{4,12},{8,0},{12,4},{1,9},{5,13},{9,1},{13,5},{2,10},{6,14},... | collective-permute-start | bytes 393224 | tf_op jit(solution)/shard_map/ppermute | solution.py:456
  10.0 10.3 %collective-permute-start.2 = (bf16[64,1024]{1,0:T(8,128)(2,1)S(1)}, bf16[64,1024]{1,0:T(8,128)(2,1)S(1)}, u32[]{:S(2)}, u32[]{:S(2)}) collective-permute-start(bf16[64,1024]{1,0:T(8,128)(2,1)S(1)} %get-tuple-element.15), channel_id=1, source_target_pairs={{0,12},{4,8},{8,4},{12,0},{1,13},{5,9},{9,5},{13,1},{2,14},{6,10},... | collective-permute-start | bytes 393224 | tf_op jit(solution)/shard_map/ppermute | solution.py:456
  10.0 11.8 %collective-permute-start.7 = (bf16[64,1024]{1,0:T(8,128)(2,1)S(1)}, bf16[64,1024]{1,0:T(8,128)(2,1)S(1)}, u32[]{:S(2)}, u32[]{:S(2)}) collective-permute-start(bf16[64,1024]{1,0:T(8,128)(2,1)S(1)} %get-tuple-element.12.refs_0_), channel_id=1, source_target_pairs={{0,2},{2,0},{1,3},{3,1},{4,6},{6,4},{5,7},{7,5},{8,10},{10,8},{9,1... | collective-permute-start | bytes 393224 | tf_op jit(solution)/shard_map/ppermute | solution.py:456
  11.7 10.3 %collective-permute-start.3 = (bf16[64,1024]{1,0:T(8,128)(2,1)S(1)}, bf16[64,1024]{1,0:T(8,128)(2,1)S(1)}, u32[]{:S(2)}, u32[]{:S(2)}) collective-permute-start(bf16[64,1024]{1,0:T(8,128)(2,1)S(1)} %get-tuple-element.12.refs_0_), channel_id=1, source_target_pairs={{0,1},{1,0},{2,3},{3,2},{4,5},{5,4},{6,7},{7,6},{8,9},{9,8},{10,11... | collective-permute-start | bytes 393224 | tf_op jit(solution)/shard_map/ppermute | solution.py:456
  12.5 10.1 %collective-permute-start.8 = (bf16[64,1024]{1,0:T(8,128)(2,1)S(1)}, bf16[64,1024]{1,0:T(8,128)(2,1)S(1)}, u32[]{:S(2)}, u32[]{:S(2)}) collective-permute-start(bf16[64,1024]{1,0:T(8,128)(2,1)S(1)} %collective-permute-done.refs_1_), channel_id=1, source_target_pairs={{0,2},{2,0},{1,3},{3,1},{4,6},{6,4},{5,7},{7,5},{8,10},{10,8},{9,1... | collective-permute-start | bytes 393224 | tf_op jit(solution)/shard_map/ppermute | solution.py:456
  20.3 2.3 %collective-permute-start.4 = (bf16[64,1024]{1,0:T(8,128)(2,1)S(1)}, bf16[64,1024]{1,0:T(8,128)(2,1)S(1)}, u32[]{:S(2)}, u32[]{:S(2)}) collective-permute-start(bf16[64,1024]{1,0:T(8,128)(2,1)S(1)} %collective-permute-done.refs_1_), channel_id=1, source_target_pairs={{0,1},{1,0},{2,3},{3,2},{4,5},{5,4},{6,7},{7,6},{8,9},{9,8},{10,11... | collective-permute-start | bytes 393224 | tf_op jit(solution)/shard_map/ppermute | solution.py:456
  20.3 6.4 %collective-permute-start.9 = (bf16[64,1024]{1,0:T(8,128)(2,1)S(1)}, bf16[64,1024]{1,0:T(8,128)(2,1)S(1)}, u32[]{:S(2)}, u32[]{:S(2)}) collective-permute-start(bf16[64,1024]{1,0:T(8,128)(2,1)S(1)} %collective-permute-done.1.refs_2_), channel_id=1, source_target_pairs={{0,2},{2,0},{1,3},{3,1},{4,6},{6,4},{5,7},{7,5},{8,10},{10,8},{9,1... | collective-permute-start | bytes 393224 | tf_op jit(solution)/shard_map/ppermute | solution.py:456
  21.8 4.9 %collective-permute-start.5 = (bf16[64,1024]{1,0:T(8,128)(2,1)S(1)}, bf16[64,1024]{1,0:T(8,128)(2,1)S(1)}, u32[]{:S(2)}, u32[]{:S(2)}) collective-permute-start(bf16[64,1024]{1,0:T(8,128)(2,1)S(1)} %collective-permute-done.1.refs_2_), channel_id=1, source_target_pairs={{0,1},{1,0},{2,3},{3,2},{4,5},{5,4},{6,7},{7,6},{8,9},{9,8},{10,11... | collective-permute-start | bytes 393224 | tf_op jit(solution)/shard_map/ppermute | solution.py:456
  22.0 7.0 %collective-permute-start.10 = (bf16[64,1024]{1,0:T(8,128)(2,1)S(1)}, bf16[64,1024]{1,0:T(8,128)(2,1)S(1)}, u32[]{:S(2)}, u32[]{:S(2)}) collective-permute-start(bf16[64,1024]{1,0:T(8,128)(2,1)S(1)} %collective-permute-done.2.refs_3_), channel_id=1, source_target_pairs={{0,2},{2,0},{1,3},{3,1},{4,6},{6,4},{5,7},{7,5},{8,10},{10,8},{9,1... | collective-permute-start | bytes 393224 | tf_op jit(solution)/shard_map/ppermute | solution.py:456
  22.6 10.0 %collective-permute-start.6 = (bf16[64,1024]{1,0:T(8,128)(2,1)S(1)}, bf16[64,1024]{1,0:T(8,128)(2,1)S(1)}, u32[]{:S(2)}, u32[]{:S(2)}) collective-permute-start(bf16[64,1024]{1,0:T(8,128)(2,1)S(1)} %collective-permute-done.2.refs_3_), channel_id=1, source_target_pairs={{0,1},{1,0},{2,3},{3,2},{4,5},{5,4},{6,7},{7,6},{8,9},{9,8},{10,11... | collective-permute-start | bytes 393224 | tf_op jit(solution)/shard_map/ppermute | solution.py:456
  22.6 11.0 %collective-permute-start.11 = (bf16[64,1024]{1,0:T(8,128)(2,1)S(1)}, bf16[64,1024]{1,0:T(8,128)(2,1)S(1)}, u32[]{:S(2)}, u32[]{:S(2)}) collective-permute-start(bf16[64,1024]{1,0:T(8,128)(2,1)S(1)} %collective-permute-done.7.refs_4_), channel_id=1, source_target_pairs={{0,1},{1,0},{2,3},{3,2},{4,5},{5,4},{6,7},{7,6},{8,9},{9,8},{10,11... | collective-permute-start | bytes 393224 | tf_op jit(solution)/shard_map/ppermute | solution.py:456
  26.7 7.0 %collective-permute-start.12 = (bf16[64,1024]{1,0:T(8,128)(2,1)S(1)}, bf16[64,1024]{1,0:T(8,128)(2,1)S(1)}, u32[]{:S(2)}, u32[]{:S(2)}) collective-permute-start(bf16[64,1024]{1,0:T(8,128)(2,1)S(1)} %collective-permute-done.8.refs_5_), channel_id=1, source_target_pairs={{0,1},{1,0},{2,3},{3,2},{4,5},{5,4},{6,7},{7,6},{8,9},{9,8},{10,11... | collective-permute-start | bytes 393224 | tf_op jit(solution)/shard_map/ppermute | solution.py:456
  26.7 7.0 %collective-permute-start.13 = (bf16[64,1024]{1,0:T(8,128)(2,1)S(1)}, bf16[64,1024]{1,0:T(8,128)(2,1)S(1)}, u32[]{:S(2)}, u32[]{:S(2)}) collective-permute-start(bf16[64,1024]{1,0:T(8,128)(2,1)S(1)} %collective-permute-done.9.refs_6_), channel_id=1, source_target_pairs={{0,1},{1,0},{2,3},{3,2},{4,5},{5,4},{6,7},{7,6},{8,9},{9,8},{10,11... | collective-permute-start | bytes 393224 | tf_op jit(solution)/shard_map/ppermute | solution.py:456
  29.0 4.6 %collective-permute-start.14 = (bf16[64,1024]{1,0:T(8,128)(2,1)S(1)}, bf16[64,1024]{1,0:T(8,128)(2,1)S(1)}, u32[]{:S(2)}, u32[]{:S(2)}) collective-permute-start(bf16[64,1024]{1,0:T(8,128)(2,1)S(1)} %collective-permute-done.10.refs_7_), channel_id=1, source_target_pairs={{0,1},{1,0},{2,3},{3,2},{4,5},{5,4},{6,7},{7,6},{8,9},{9,8},{10,11... | collective-permute-start | bytes 393224 | tf_op jit(solution)/shard_map/ppermute | solution.py:456

commit v5 on v4

--- a/solution.py
+++ b/solution.py
@@ -33,9 +33,9 @@
     return bf(first), jnp.asarray(np.stack([turn_cos, turn_sin]), jnp.float32), bf(second), bf(spread)
 
 
-def channel_kernel(owners, owner_hbm, volt_ref, taps_hbm, first_ref, turn_ref, second_ref, spread_ref, *rest):
-    outs = rest[:owners]
-    owner_ref, volts, taps_ref, tap_rows, first, turn, second, spread, filt, wide, pick, sems = rest[owners:]
+def channel_kernel(owners, paired, owner_hbm, volt_ref, taps_hbm, first_ref, turn_ref, second_ref, spread_ref, *rest):
+    passed, outs, handed = rest[:3], rest[3 : 3 + owners + paired], rest[3 + owners + paired : 6 + owners + paired]
+    owner_ref, volts, taps_ref, tap_rows, first, turn, second, spread, filt, wide, pick, sems = rest[6 + owners + paired :]
     stations, blocks, rows, _ = volt_ref.shape
     taps = taps_ref.shape[0]
     frames = blocks - taps + 1
@@ -56,6 +56,8 @@
     consts = []
     for i, (src, dst) in enumerate([(first_ref, first), (turn_ref, turn), (second_ref, second), (spread_ref, spread)]):
         consts.append(pltpu.make_async_copy(src, dst, sems.at[stations + i]))
+    for i, (src, dst) in enumerate(zip(passed, handed)):
+        consts.append(pltpu.make_async_copy(src, dst, sems.at[stations + 6 + i]))
     for c in copies + consts:
         c.start()
     tap_copy.wait()
@@ -123,12 +125,14 @@
             for j in range(width):
                 for f in range(HALF):
                     p = (k * width + j) * sc
-                    outs[k][pl.ds((h * HALF + f) * sc, sc), pl.ds(j * LANES, LANES)] = z[
-                        p : p + sc, f * LANES : (f + 1) * LANES
-                    ].astype(jnp.bfloat16)
-
-
-def channelise(voltages, filter_taps, block_owner, owners):
+                    block = z[p : p + sc, f * LANES : (f + 1) * LANES].astype(jnp.bfloat16)
+                    row = (h * HALF + f) * sc
+                    outs[k][pl.ds(row, sc), pl.ds(j * LANES, LANES)] = block
+                    if paired and k < 2:
+                        outs[owners][pl.ds(k * frames * sc + row, sc), pl.ds(j * LANES, LANES)] = block
+
+
+def channelise(voltages, filter_taps, block_owner, owners, paired, passed):
     _, stations, _, blocks, _, nfft = voltages.shape
     taps = filter_taps.shape[0]
     frames = blocks - taps + 1
@@ -138,14 +142,16 @@
     first, turn, second, spread = channel_tables(nfft, groups)
     sc = 2 * stations
     width = groups // owners
-    inputs = (block_owner, volts, filter_taps, first, turn, second, spread)
+    inputs = (block_owner, volts, filter_taps, first, turn, second, spread, *passed)
+    block = jax.ShapeDtypeStruct((frames * sc, width * LANES), jnp.bfloat16)
+    pair = jax.ShapeDtypeStruct((2 * frames * sc, width * LANES), jnp.bfloat16)
     anyspec = pl.BlockSpec(memory_space=pltpu.HBM)
     bf = jnp.bfloat16
     return pl.pallas_call(
-        functools.partial(channel_kernel, owners),
-        out_shape=[jax.ShapeDtypeStruct((frames * sc, width * LANES), bf)] * owners,
-        in_specs=[anyspec] * 7,
-        out_specs=[pl.BlockSpec(memory_space=pltpu.VMEM)] * owners,
+        functools.partial(channel_kernel, owners, paired),
+        out_shape=[block] * owners + [pair] * paired + [jax.ShapeDtypeStruct(x.shape, x.dtype) for x in passed],
+        in_specs=[anyspec] * len(inputs),
+        out_specs=[pl.BlockSpec(memory_space=pltpu.VMEM)] * (owners + paired + len(passed)),
         scratch_shapes=[
             pltpu.SMEM(block_owner.shape, jnp.int32),
             pltpu.VMEM(volts.shape, bf),
@@ -158,7 +164,7 @@
             pltpu.VMEM((stations, HALF * 2 * depth, frames // HALF * LANES), bf),
             pltpu.VMEM((frames // HALF, sc * groups, spread.shape[0]), bf),
             pltpu.VMEM((groups * sc, sc * groups), bf),
-            pltpu.SemaphoreType.DMA((stations + 6,)),
+            pltpu.SemaphoreType.DMA((stations + 9,)),
         ],
         compiler_params=grant(),
         name="channelise",
@@ -197,7 +203,7 @@
     return lax.dot_general(a, b, (((1,), (1,)), ((), ())), preferred_element_type=jnp.float32)
 
 
-def weights_kernel(pairs, owned, share, table_hbm, index_hbm, copy_hbm, out_ref, rows_ref, table_ref, index_ref, copy_ref, sems):
+def weights_kernel(pairs, owned, share, table_ref, index_ref, copy_ref, out_ref, rows_ref):
     stations, beams = index_ref.shape
     tile, spread = copy_ref.shape
     frames = spread // tile
@@ -206,12 +212,6 @@
     factor = 1.0 / math.sqrt(stations)
 
     def prepare():
-        pairs_of = zip((table_hbm, index_hbm, copy_hbm), (table_ref, index_ref, copy_ref))
-        loads = [pltpu.make_async_copy(src, dst, sems.at[i]) for i, (src, dst) in enumerate(pairs_of)]
-        for load in loads:
-            load.start()
-        for load in loads:
-            load.wait()
         row = lax.broadcasted_iota(jnp.int32, (count, beams), 0)
         lane = lax.broadcasted_iota(jnp.int32, (count, beams), 1)
         hit = lane == start + (row >> 1)
@@ -272,14 +272,12 @@
     return pl.pallas_call(
         functools.partial(weights_kernel, pairs, owned, share),
         out_shape=jax.ShapeDtypeStruct((count * frames, depth), jnp.bfloat16),
-        in_specs=[pl.BlockSpec(memory_space=pltpu.HBM)] * 3,
-        scratch_shapes=[pltpu.VMEM((count, depth), jnp.float32)]
-        + [pltpu.VMEM(x.shape, x.dtype) for x in inputs]
-        + [pltpu.SemaphoreType.DMA((3,))],
+        in_specs=whole_vmem(3),
+        scratch_shapes=[pltpu.VMEM((count, depth), jnp.float32)],
         compiler_params=grant() if resident else None,
         name="framed_weights",
         **extra,
-    )(*[pltpu.with_memory_space_constraint(x, pltpu.HBM) for x in inputs])
+    )(*inputs)
 
 
 def pack(packed, slot, blocks, frames):
@@ -470,16 +468,25 @@
     groups = block_owner.shape[0]
     owned = beam_index.shape[0] // sections
     tables = weight_inputs(beam_table, beam_index, frames, pairs)
-    own = channelise(voltages, filter_taps, block_owner, owners)
+    lead = max(1, owners // 4)
+    paired = int(lead == 1)
+    own = channelise(voltages, filter_taps, block_owner, owners, paired, tables)
+    pair, tables = own[owners], own[owners + paired :]
     weights = framed_weights(tables, frames, pairs, owned)
     mine = [own[0]] + [partner(own[k], "chan", k) for k in range(1, owners)]
-    lead = max(1, owners // 4)
     twin, others, crossed = [], [[] for _ in range(1, sections)], [[] for _ in range(1, sections)]
     for g in range(owners // lead):
         part = mine[g * lead : (g + 1) * lead]
         twin += moved(part, "pol", 1)
         for x in range(1, sections):
-            far = moved(part, "stat", x)
+            if paired and g == 0:
+                both = partner(pair, "stat", x)
+                rows = both.shape[0] // 2
+                far, later = [both[:rows]], partner(both[rows:], "chan", 1)
+            elif paired and g == 1:
+                far = [later]
+            else:
+                far = moved(part, "stat", x)
             others[x - 1] += far
             crossed[x - 1] += moved(far, "pol", 1)
     near = correlate_near(mine, twin, frames, sections)

time: 41.3 us -> 39.5 us (0.956)
  Pallas kernels: 15.7 us -> 14.7 us
  starting transfers between devices: 12.4 us -> 11.4 us
    ppermute x15, starting transfers between devices: 12.4 us -> 11.4 us  [partner(): lax.ppermute(x, axis, [(i, i ^ distance) for i in range(lax.axis_size(axi...]
    pallas_call x1, Pallas kernels: 3.58 us -> 2.59 us  [framed_weights(): pl.pallas_call(functools.partial(weights_kernel, pairs, owned, share), ou...]
  transfers between devices with their start and end apart: 15 -> 15, of which waited for: 4 -> 4; matrix products, arithmetic and copies ran while one was open for 0% -> 0% of each run, Pallas kernels for 11% -> 9%
where the time goes in v5:
time: 39.5 us; the launch traced here: 39.3 us
  Pallas kernels  14.7 us (37%)
  waiting for transfers between devices  12.5 us (32%)
  starting transfers between devices  11.4 us (29%)
  between operations  0.72 us (2%)
    ppermute x15, waiting for transfers between devices, partner(): lax.ppermute(x, axis, [(i, i ^ distance) for i in range(lax.axis_size(axi...  12.5 us
    ppermute x15, starting transfers between devices, partner(): lax.ppermute(x, axis, [(i, i ^ distance) for i in range(lax.axis_size(axi...  11.4 us
    pallas_call x1, Pallas kernels, finish(): pl.pallas_call(functools.partial(finish_kernel, owners, sections, frames,...  7.43 us
    pallas_call x1, Pallas kernels, channelise(): pl.pallas_call(functools.partial(channel_kernel, owners, paired), out_sha...  3.7 us
    pallas_call x1, Pallas kernels, framed_weights(): pl.pallas_call(functools.partial(weights_kernel, pairs, owned, share), ou...  2.59 us
    pallas_call x1, Pallas kernels, correlate_near(): pl.pallas_call(functools.partial(near_kernel, owners, sections, frames),...  0.99 us
  transfers between devices with their start and end apart: 15, of which 4 were waited for; matrix products, arithmetic and copies ran while one was open for 0% of the time, Pallas kernels for 9%

profile of v5, /device:TPU:0, one launch (start us, length us, event | category | flops | bytes accessed | tf_op | source)
XLA Modules:
  0.0 39.3 jit_solution(17646701285848717746)
XLA Ops:
  0.6 3.7 %channelise.1 = (bf16[64,1024]{1,0:T(8,128)(2,1)S(1)}, bf16[64,1024]{1,0:T(8,128)(2,1)S(1)}, bf16[64,1024]{1,0:T(8,128)(2,1)S(1)}, bf16[64,1024]{1,0:T(8,128)(2,...) custom-call(s32[32]{0:T(128)} %owner_hbm.1, ...), custom_call_target="tpu_custom_call" | custom-call | tf_op jit(solution)/shard_map/channelise/pallas_call | solution.py:150
  4.3 3.0 %collective-permute-start.7 = (bf16[128,1024]{1,0:T(8,128)(2,1)S(1)}, bf16[128,1024]{1,0:T(8,128)(2,1)S(1)}, u32[]{:S(2)}, u32[]{:S(2)}) collective-permute-start(bf16[128,1024]{1,0:T(8,128)(2,1)S(1)} %get-tuple-element.27), channel_id=1, source_target_pairs={{0,2},{2,0},{1,3},{3,1},{4,6},{6,4},{5,7},{7,5},{8,10},{10,8},{9,1... | collective-permute-start | bytes 786440 | tf_op jit(solution)/shard_map/ppermute | solution.py:454
  7.4 2.6 %collective-permute-start.1 = (bf16[64,1024]{1,0:T(8,128)(2,1)S(1)}, bf16[64,1024]{1,0:T(8,128)(2,1)S(1)}, u32[]{:S(2)}, u32[]{:S(2)}) collective-permute-start(bf16[64,1024]{1,0:T(8,128)(2,1)S(1)} %get-tuple-element.21), channel_id=1, source_target_pairs={{0,8},{4,12},{8,0},{12,4},{1,9},{5,13},{9,1},{13,5},{2,10},{6,14},... | collective-permute-start | bytes 393224 | tf_op jit(solution)/shard_map/ppermute | solution.py:454
  10.0 1.6 %collective-permute-start = (bf16[64,1024]{1,0:T(8,128)(2,1)S(1)}, bf16[64,1024]{1,0:T(8,128)(2,1)S(1)}, u32[]{:S(2)}, u32[]{:S(2)}) collective-permute-start(bf16[64,1024]{1,0:T(8,128)(2,1)S(1)} %get-tuple-element.20), channel_id=1, source_target_pairs={{0,4},{4,0},{8,12},{12,8},{1,5},{5,1},{9,13},{13,9},{2,6},{6,2},{1... | collective-permute-start | bytes 393224 | tf_op jit(solution)/shard_map/ppermute | solution.py:454
  11.5 0.2 collective-permute-start.2
  11.8 0.0 collective-permute-start.3
  11.8 8.2 %collective-permute-done.1.refs_2_ = bf16[64,1024]{1,0:T(8,128)(2,1)S(1)} collective-permute-done((bf16[64,1024]{1,0:T(8,128)(2,1)S(1)}, bf16[64,1024]{1,0:T(8,128)(2,1)S(1)}, u32[]{:S(2)}, u32[]{:S(2)}) %collective-permute-start.1) | collective-permute-done | bytes 131104 | tf_op jit(solution)/shard_map/ppermute | solution.py:454
  20.0 0.5 %collective-permute-start.9 = (bf16[64,1024]{1,0:T(8,128)(2,1)S(1)}, bf16[64,1024]{1,0:T(8,128)(2,1)S(1)}, u32[]{:S(2)}, u32[]{:S(2)}) collective-permute-start(bf16[64,1024]{1,0:T(8,128)(2,1)S(1)} %collective-permute-done.1.refs_2_), channel_id=1, source_target_pairs={{0,2},{2,0},{1,3},{3,1},{4,6},{6,4},{5,7},{7,5},{8,10},{10,8},{9,1... | collective-permute-start | bytes 393224 | tf_op jit(solution)/shard_map/ppermute | solution.py:454
  20.5 0.5 %collective-permute-start.4 = (bf16[64,1024]{1,0:T(8,128)(2,1)S(1)}, bf16[64,1024]{1,0:T(8,128)(2,1)S(1)}, u32[]{:S(2)}, u32[]{:S(2)}) collective-permute-start(bf16[64,1024]{1,0:T(8,128)(2,1)S(1)} %collective-permute-done.refs_1_), channel_id=1, source_target_pairs={{0,1},{1,0},{2,3},{3,2},{4,5},{5,4},{6,7},{7,6},{8,9},{9,8},{10,11... | collective-permute-start | bytes 393224 | tf_op jit(solution)/shard_map/ppermute | solution.py:454
  21.0 1.5 %collective-permute-start.10 = (bf16[64,1024]{1,0:T(8,128)(2,1)S(1)}, bf16[64,1024]{1,0:T(8,128)(2,1)S(1)}, u32[]{:S(2)}, u32[]{:S(2)}) collective-permute-start(bf16[64,1024]{1,0:T(8,128)(2,1)S(1)} %collective-permute-done.2.refs_3_), channel_id=1, source_target_pairs={{0,2},{2,0},{1,3},{3,1},{4,6},{6,4},{5,7},{7,5},{8,10},{10,8},{9,1... | collective-permute-start | bytes 393224 | tf_op jit(solution)/shard_map/ppermute | solution.py:454
  22.5 0.4 %collective-permute-start.8 = (bf16[64,1024]{1,0:T(8,128)(2,1)S(1)}, bf16[64,1024]{1,0:T(8,128)(2,1)S(1)}, u32[]{:S(2)}, u32[]{:S(2)}) collective-permute-start(bf16[64,1024]{1,0:T(8,128)(2,1)S(1)} %get-tuple-element.32), channel_id=1, source_target_pairs={{0,4},{4,0},{8,12},{12,8},{1,5},{5,1},{9,13},{13,9},{2,6},{6,2},{1... | collective-permute-start | bytes 393224 | tf_op jit(solution)/shard_map/ppermute | solution.py:454
  23.0 0.0 collective-permute-done.4.refs_5_
  23.0 0.0 collective-permute-start.6
  23.0 3.2 %collective-permute-done.9.refs_6_ = bf16[64,1024]{1,0:T(8,128)(2,1)S(1)} collective-permute-done((bf16[64,1024]{1,0:T(8,128)(2,1)S(1)}, bf16[64,1024]{1,0:T(8,128)(2,1)S(1)}, u32[]{:S(2)}, u32[]{:S(2)}) %collective-permute-start.9) | collective-permute-done | bytes 131104 | tf_op jit(solution)/shard_map/ppermute | solution.py:454
  26.2 0.0 collective-permute-start.11
  26.2 0.5 %collective-permute-start.13 = (bf16[64,1024]{1,0:T(8,128)(2,1)S(1)}, bf16[64,1024]{1,0:T(8,128)(2,1)S(1)}, u32[]{:S(2)}, u32[]{:S(2)}) collective-permute-start(bf16[64,1024]{1,0:T(8,128)(2,1)S(1)} %collective-permute-done.9.refs_6_), channel_id=1, source_target_pairs={{0,1},{1,0},{2,3},{3,2},{4,5},{5,4},{6,7},{7,6},{8,9},{9,8},{10,11... | collective-permute-start | bytes 393224 | tf_op jit(solution)/shard_map/ppermute | solution.py:454
  26.7 1.0 %collective-permute-done.10.refs_7_ = bf16[64,1024]{1,0:T(8,128)(2,1)S(1)} collective-permute-done((bf16[64,1024]{1,0:T(8,128)(2,1)S(1)}, bf16[64,1024]{1,0:T(8,128)(2,1)S(1)}, u32[]{:S(2)}, u32[]{:S(2)}) %collective-permute-start.10) | collective-permute-done | bytes 131104 | tf_op jit(solution)/shard_map/ppermute | solution.py:454
  27.7 0.0 collective-permute-start.14
  27.7 0.1 collective-permute-done.8.refs_5_
  27.8 0.5 %collective-permute-start.12 = (bf16[64,1024]{1,0:T(8,128)(2,1)S(1)}, bf16[64,1024]{1,0:T(8,128)(2,1)S(1)}, u32[]{:S(2)}, u32[]{:S(2)}) collective-permute-start(bf16[64,1024]{1,0:T(8,128)(2,1)S(1)} %collective-permute-done.8.refs_5_), channel_id=1, source_target_pairs={{0,1},{1,0},{2,3},{3,2},{4,5},{5,4},{6,7},{7,6},{8,9},{9,8},{10,11... | collective-permute-start | bytes 393224 | tf_op jit(solution)/shard_map/ppermute | solution.py:454
  28.2 2.6 %framed_weights.1.weight_ref = bf16[4000,512]{1,0:T(8,128)(2,1)S(1)} custom-call(f32[2,16]{1,0:T(2,128)S(1)} %get-tuple-element.16.table_ref, s32[32,500]{1,0:T(8,128)S(1)} %get-tuple-element.17.index_ref, bf16[64,512]{1,0:T(8,128)(2,1)S(1)} %get-tuple-element.18.copy_ref), custom_call_target="tpu_custom_call" | custom-call | tf_op jit(solution)/shard_map/framed_weights/pallas_call | solution.py:272
  30.9 1.0 %correlate_near.1 = (f32[256,64]{1,0:T(8,128)S(1)}, bf16[8,32,1024]{2,1,0:T(8,128)(2,1)S(1)}, bf16[256,512]{1,0:T(8,128)(2,1)S(1)}, bf16[64,128]{1,0:T(8,128)(2,1)S(1)}) custom-call(bf16[64,1024]{1,0:T(8,128)(2,1)S(1)} %get-tuple-element.19.refs_0_, bf16[64,1024]{1,0:T(8,128)(2,1)S(1)} %collective-permute-done.refs_1_, ...), custom_call_target="tpu_custom_call" | custom-call | tf_op jit(solution)/shard_map/correlate_near/pallas_call | solution.py:351
  31.9 0.0 collective-permute-done.11.refs_8_
  31.9 7.4 %finish.1 = (f32[4000,1024]{1,0:T(8,128)}, f32[256,64]{1,0:T(8,128)}) custom-call(bf16[4000,512]{1,0:T(8,128)(2,1)S(1)} %framed_weights.1.weight_ref, f32[256,64]{1,0:T(8,128)S(1)} %get-tuple-element.23.part_ref, bf16[8,32,1024]{2,1,0:T(8,128)(2,1)S(1)} %get-tuple-element.24.packed, bf16[256,512]{1,0:T(8,128)(2,1)S(1)} %get-tuple-element.25.merge_ref, ...), custom_call_target="tpu_custom_call" | custom-call | tf_op jit(solution)/shard_map/finish/pallas_call | solution.py:435
  (11 shorter events, 0.0 us)
Async XLA Ops:
  4.3 16.6 %collective-permute-start.7 = (bf16[128,1024]{1,0:T(8,128)(2,1)S(1)}, bf16[128,1024]{1,0:T(8,128)(2,1)S(1)}, u32[]{:S(2)}, u32[]{:S(2)}) collective-permute-start(bf16[128,1024]{1,0:T(8,128)(2,1)S(1)} %get-tuple-element.27), channel_id=1, source_target_pairs={{0,2},{2,0},{1,3},{3,1},{4,6},{6,4},{5,7},{7,5},{8,10},{10,8},{9,1... | collective-permute-start | bytes 786440 | tf_op jit(solution)/shard_map/ppermute | solution.py:454
  7.4 12.6 %collective-permute-start.1 = (bf16[64,1024]{1,0:T(8,128)(2,1)S(1)}, bf16[64,1024]{1,0:T(8,128)(2,1)S(1)}, u32[]{:S(2)}, u32[]{:S(2)}) collective-permute-start(bf16[64,1024]{1,0:T(8,128)(2,1)S(1)} %get-tuple-element.21), channel_id=1, source_target_pairs={{0,8},{4,12},{8,0},{12,4},{1,9},{5,13},{9,1},{13,5},{2,10},{6,14},... | collective-permute-start | bytes 393224 | tf_op jit(solution)/shard_map/ppermute | solution.py:454
  10.0 10.5 %collective-permute-start = (bf16[64,1024]{1,0:T(8,128)(2,1)S(1)}, bf16[64,1024]{1,0:T(8,128)(2,1)S(1)}, u32[]{:S(2)}, u32[]{:S(2)}) collective-permute-start(bf16[64,1024]{1,0:T(8,128)(2,1)S(1)} %get-tuple-element.20), channel_id=1, source_target_pairs={{0,4},{4,0},{8,12},{12,8},{1,5},{5,1},{9,13},{13,9},{2,6},{6,2},{1... | collective-permute-start | bytes 393224 | tf_op jit(solution)/shard_map/ppermute | solution.py:454
  11.5 8.9 %collective-permute-start.2 = (bf16[64,1024]{1,0:T(8,128)(2,1)S(1)}, bf16[64,1024]{1,0:T(8,128)(2,1)S(1)}, u32[]{:S(2)}, u32[]{:S(2)}) collective-permute-start(bf16[64,1024]{1,0:T(8,128)(2,1)S(1)} %get-tuple-element.22), channel_id=1, source_target_pairs={{0,12},{4,8},{8,4},{12,0},{1,13},{5,9},{9,5},{13,1},{2,14},{6,10},... | collective-permute-start | bytes 393224 | tf_op jit(solution)/shard_map/ppermute | solution.py:454
  11.8 10.8 %collective-permute-start.3 = (bf16[64,1024]{1,0:T(8,128)(2,1)S(1)}, bf16[64,1024]{1,0:T(8,128)(2,1)S(1)}, u32[]{:S(2)}, u32[]{:S(2)}) collective-permute-start(bf16[64,1024]{1,0:T(8,128)(2,1)S(1)} %get-tuple-element.19.refs_0_), channel_id=1, source_target_pairs={{0,1},{1,0},{2,3},{3,2},{4,5},{5,4},{6,7},{7,6},{8,9},{9,8},{10,11... | collective-permute-start | bytes 393224 | tf_op jit(solution)/shard_map/ppermute | solution.py:454
  20.0 6.3 %collective-permute-start.9 = (bf16[64,1024]{1,0:T(8,128)(2,1)S(1)}, bf16[64,1024]{1,0:T(8,128)(2,1)S(1)}, u32[]{:S(2)}, u32[]{:S(2)}) collective-permute-start(bf16[64,1024]{1,0:T(8,128)(2,1)S(1)} %collective-permute-done.1.refs_2_), channel_id=1, source_target_pairs={{0,2},{2,0},{1,3},{3,1},{4,6},{6,4},{5,7},{7,5},{8,10},{10,8},{9,1... | collective-permute-start | bytes 393224 | tf_op jit(solution)/shard_map/ppermute | solution.py:454
  20.5 5.8 %collective-permute-start.5 = (bf16[64,1024]{1,0:T(8,128)(2,1)S(1)}, bf16[64,1024]{1,0:T(8,128)(2,1)S(1)}, u32[]{:S(2)}, u32[]{:S(2)}) collective-permute-start(bf16[64,1024]{1,0:T(8,128)(2,1)S(1)} %collective-permute-done.1.refs_2_), channel_id=1, source_target_pairs={{0,1},{1,0},{2,3},{3,2},{4,5},{5,4},{6,7},{7,6},{8,9},{9,8},{10,11... | collective-permute-start | bytes 393224 | tf_op jit(solution)/shard_map/ppermute | solution.py:454
  20.5 2.5 %collective-permute-start.4 = (bf16[64,1024]{1,0:T(8,128)(2,1)S(1)}, bf16[64,1024]{1,0:T(8,128)(2,1)S(1)}, u32[]{:S(2)}, u32[]{:S(2)}) collective-permute-start(bf16[64,1024]{1,0:T(8,128)(2,1)S(1)} %collective-permute-done.refs_1_), channel_id=1, source_target_pairs={{0,1},{1,0},{2,3},{3,2},{4,5},{5,4},{6,7},{7,6},{8,9},{9,8},{10,11... | collective-permute-start | bytes 393224 | tf_op jit(solution)/shard_map/ppermute | solution.py:454
  21.0 6.8 %collective-permute-start.10 = (bf16[64,1024]{1,0:T(8,128)(2,1)S(1)}, bf16[64,1024]{1,0:T(8,128)(2,1)S(1)}, u32[]{:S(2)}, u32[]{:S(2)}) collective-permute-start(bf16[64,1024]{1,0:T(8,128)(2,1)S(1)} %collective-permute-done.2.refs_3_), channel_id=1, source_target_pairs={{0,2},{2,0},{1,3},{3,1},{4,6},{6,4},{5,7},{7,5},{8,10},{10,8},{9,1... | collective-permute-start | bytes 393224 | tf_op jit(solution)/shard_map/ppermute | solution.py:454
  22.5 5.3 %collective-permute-start.8 = (bf16[64,1024]{1,0:T(8,128)(2,1)S(1)}, bf16[64,1024]{1,0:T(8,128)(2,1)S(1)}, u32[]{:S(2)}, u32[]{:S(2)}) collective-permute-start(bf16[64,1024]{1,0:T(8,128)(2,1)S(1)} %get-tuple-element.32), channel_id=1, source_target_pairs={{0,4},{4,0},{8,12},{12,8},{1,5},{5,1},{9,13},{13,9},{2,6},{6,2},{1... | collective-permute-start | bytes 393224 | tf_op jit(solution)/shard_map/ppermute | solution.py:454
  23.0 7.9 %collective-permute-start.6 = (bf16[64,1024]{1,0:T(8,128)(2,1)S(1)}, bf16[64,1024]{1,0:T(8,128)(2,1)S(1)}, u32[]{:S(2)}, u32[]{:S(2)}) collective-permute-start(bf16[64,1024]{1,0:T(8,128)(2,1)S(1)} %collective-permute-done.2.refs_3_), channel_id=1, source_target_pairs={{0,1},{1,0},{2,3},{3,2},{4,5},{5,4},{6,7},{7,6},{8,9},{9,8},{10,11... | collective-permute-start | bytes 393224 | tf_op jit(solution)/shard_map/ppermute | solution.py:454
  26.2 5.7 %collective-permute-start.11 = (bf16[64,1024]{1,0:T(8,128)(2,1)S(1)}, bf16[64,1024]{1,0:T(8,128)(2,1)S(1)}, u32[]{:S(2)}, u32[]{:S(2)}) collective-permute-start(bf16[64,1024]{1,0:T(8,128)(2,1)S(1)} %get-tuple-element.33.refs_4_), channel_id=1, source_target_pairs={{0,1},{1,0},{2,3},{3,2},{4,5},{5,4},{6,7},{7,6},{8,9},{9,8},{10,11... | collective-permute-start | bytes 393224 | tf_op jit(solution)/shard_map/ppermute | solution.py:454
  26.2 5.6 %collective-permute-start.13 = (bf16[64,1024]{1,0:T(8,128)(2,1)S(1)}, bf16[64,1024]{1,0:T(8,128)(2,1)S(1)}, u32[]{:S(2)}, u32[]{:S(2)}) collective-permute-start(bf16[64,1024]{1,0:T(8,128)(2,1)S(1)} %collective-permute-done.9.refs_6_), channel_id=1, source_target_pairs={{0,1},{1,0},{2,3},{3,2},{4,5},{5,4},{6,7},{7,6},{8,9},{9,8},{10,11... | collective-permute-start | bytes 393224 | tf_op jit(solution)/shard_map/ppermute | solution.py:454
  27.7 4.1 %collective-permute-start.14 = (bf16[64,1024]{1,0:T(8,128)(2,1)S(1)}, bf16[64,1024]{1,0:T(8,128)(2,1)S(1)}, u32[]{:S(2)}, u32[]{:S(2)}) collective-permute-start(bf16[64,1024]{1,0:T(8,128)(2,1)S(1)} %collective-permute-done.10.refs_7_), channel_id=1, source_target_pairs={{0,1},{1,0},{2,3},{3,2},{4,5},{5,4},{6,7},{7,6},{8,9},{9,8},{10,11... | collective-permute-start | bytes 393224 | tf_op jit(solution)/shard_map/ppermute | solution.py:454
  27.8 4.1 %collective-permute-start.12 = (bf16[64,1024]{1,0:T(8,128)(2,1)S(1)}, bf16[64,1024]{1,0:T(8,128)(2,1)S(1)}, u32[]{:S(2)}, u32[]{:S(2)}) collective-permute-start(bf16[64,1024]{1,0:T(8,128)(2,1)S(1)} %collective-permute-done.8.refs_5_), channel_id=1, source_target_pairs={{0,1},{1,0},{2,3},{3,2},{4,5},{5,4},{6,7},{7,6},{8,9},{9,8},{10,11... | collective-permute-start | bytes 393224 | tf_op jit(solution)/shard_map/ppermute | solution.py:454

commit v6 on v5

--- a/solution.py
+++ b/solution.py
@@ -379,35 +379,40 @@
             data[pl.ds(pl.multiple_of(at, rows), rows), :] = blocks[x * owners + k][...]
 
 
-def finish_kernel(owners, sections, frames, share, span, weight_ref, part_ref, packed, merge_ref, far_ref, *refs):
+def finish_kernel(owners, sections, frames, strips, span, weight_ref, part_ref, packed, merge_ref, far_ref, *refs):
     count = owners * sections
     blocks, crossed = refs[:count], refs[count : 2 * count - owners]
     out_ref, vis_ref, data, theirs, vis, held, sems, *chunk = refs[2 * count - owners :]
     slots = held.shape[0]
-    height, lanes = out_ref.shape
-    steps = [(row, lane) for row in range(0, height, share) for lane in range(0, lanes, span)]
+    _, lanes = out_ref.shape
+    steps = []
+    for lane in range(0, lanes, span):
+        row = 0
+        for size in strips if lane == 0 else strips[::-1]:
+            steps.append((row, size, lane))
+            row += size
     vis_copy = pltpu.make_async_copy(vis, vis_ref, sems.at[slots])
 
     def copy(i):
-        row, lane = steps[i]
+        row, size, lane = steps[i]
         return pltpu.make_async_copy(
-            held.at[i % slots], out_ref.at[pl.ds(row, share), pl.ds(lane, span)], sems.at[i % slots]
+            held.at[i % slots, pl.ds(0, size)], out_ref.at[pl.ds(row, size), pl.ds(lane, span)], sems.at[i % slots]
         )
 
     gather_rows(data, blocks, owners, sections)
-    for i, (row, lane) in enumerate(steps):
+    for i, (row, size, lane) in enumerate(steps):
         if i >= slots:
             copy(i - slots).wait()
         if chunk:
-            load = pltpu.make_async_copy(weight_ref.at[pl.ds(row, share)], chunk[0], sems.at[slots + 1])
+            load = pltpu.make_async_copy(weight_ref.at[pl.ds(row, size)], chunk[0].at[pl.ds(0, size)], sems.at[slots + 1])
             load.start()
             load.wait()
-            weights = chunk[0][...]
+            weights = chunk[0][:size]
         else:
-            weights = weight_ref[row : row + share, :]
-        held[i % slots] = jnp.dot(weights, data[:, lane : lane + span], preferred_element_type=jnp.float32)
+            weights = weight_ref[row : row + size, :]
+        held[i % slots, :size] = jnp.dot(weights, data[:, lane : lane + span], preferred_element_type=jnp.float32)
         copy(i).start()
-        if i == min(slots, len(steps)) - 1:
+        if i == min(slots + 1, len(steps) - 1):
             others = []
             for x in range(1, sections):
                 others.append(blocks[x * owners : (x + 1) * owners])
@@ -428,12 +433,17 @@
     width, block, length = packed.shape
     resident = height * depth * 2 <= RESIDENT
     span = min(lanes, 512)
-    share = 8 * pieces(height // 8, 100 if resident else 25)
+    lead = height // 80 * 8
+    third = (height - lead) // 24 * 8
+    strips = [lead, third, third, height - lead - 2 * third]
+    if not resident:
+        strips = [8 * pieces(height // 8, 25)] * (height // 8 // pieces(height // 8, 25))
+    share = max(strips)
     slots = 4
     weight_spec = pl.BlockSpec(memory_space=pltpu.VMEM if resident else pltpu.HBM)
     chunk = [] if resident else [pltpu.VMEM((share, depth), jnp.bfloat16)]
     return pl.pallas_call(
-        functools.partial(finish_kernel, owners, sections, frames, share, span),
+        functools.partial(finish_kernel, owners, sections, frames, strips, span),
         out_shape=[jax.ShapeDtypeStruct((height, lanes), jnp.float32), jax.ShapeDtypeStruct(part.shape, jnp.float32)],
         in_specs=[weight_spec] + whole_vmem(4 + 2 * len(others) + owners),
         out_specs=[pl.BlockSpec(memory_space=pl.ANY)] * 2,

time: 39.5 us -> 39.2 us (level)
  no operation moved by 1% of the time
where the time goes in v6:
time: 39.2 us; the launch traced here: 39.1 us
  Pallas kernels  14.5 us (37%)
  waiting for transfers between devices  12.5 us (32%)
  starting transfers between devices  11.4 us (29%)
  between operations  0.72 us (2%)
    ppermute x15, waiting for transfers between devices, partner(): lax.ppermute(x, axis, [(i, i ^ distance) for i in range(lax.axis_size(axi...  12.5 us
    ppermute x15, starting transfers between devices, partner(): lax.ppermute(x, axis, [(i, i ^ distance) for i in range(lax.axis_size(axi...  11.4 us
    pallas_call x1, Pallas kernels, finish(): pl.pallas_call(functools.partial(finish_kernel, owners, sections, frames,...  7.2 us
    pallas_call x1, Pallas kernels, channelise(): pl.pallas_call(functools.partial(channel_kernel, owners, paired), out_sha...  3.7 us
    pallas_call x1, Pallas kernels, framed_weights(): pl.pallas_call(functools.partial(weights_kernel, pairs, owned, share), ou...  2.59 us
    pallas_call x1, Pallas kernels, correlate_near(): pl.pallas_call(functools.partial(near_kernel, owners, sections, frames),...  0.99 us
  transfers between devices with their start and end apart: 15, of which 4 were waited for; matrix products, arithmetic and copies ran while one was open for 0% of the time, Pallas kernels for 9%

profile of v6, /device:TPU:0, one launch (start us, length us, event | category | flops | bytes accessed | tf_op | source)
XLA Modules:
  0.0 39.1 jit_solution(659758978018442300)
XLA Ops:
  0.6 3.7 %channelise.1 = (bf16[64,1024]{1,0:T(8,128)(2,1)S(1)}, bf16[64,1024]{1,0:T(8,128)(2,1)S(1)}, bf16[64,1024]{1,0:T(8,128)(2,1)S(1)}, bf16[64,1024]{1,0:T(8,128)(2,...) custom-call(s32[32]{0:T(128)} %owner_hbm.1, ...), custom_call_target="tpu_custom_call" | custom-call | tf_op jit(solution)/shard_map/channelise/pallas_call | solution.py:150
  4.3 3.0 %collective-permute-start.7 = (bf16[128,1024]{1,0:T(8,128)(2,1)S(1)}, bf16[128,1024]{1,0:T(8,128)(2,1)S(1)}, u32[]{:S(2)}, u32[]{:S(2)}) collective-permute-start(bf16[128,1024]{1,0:T(8,128)(2,1)S(1)} %get-tuple-element.27), channel_id=1, source_target_pairs={{0,2},{2,0},{1,3},{3,1},{4,6},{6,4},{5,7},{7,5},{8,10},{10,8},{9,1... | collective-permute-start | bytes 786440 | tf_op jit(solution)/shard_map/ppermute | solution.py:464
  7.4 2.6 %collective-permute-start.1 = (bf16[64,1024]{1,0:T(8,128)(2,1)S(1)}, bf16[64,1024]{1,0:T(8,128)(2,1)S(1)}, u32[]{:S(2)}, u32[]{:S(2)}) collective-permute-start(bf16[64,1024]{1,0:T(8,128)(2,1)S(1)} %get-tuple-element.21), channel_id=1, source_target_pairs={{0,8},{4,12},{8,0},{12,4},{1,9},{5,13},{9,1},{13,5},{2,10},{6,14},... | collective-permute-start | bytes 393224 | tf_op jit(solution)/shard_map/ppermute | solution.py:464
  10.0 1.6 %collective-permute-start = (bf16[64,1024]{1,0:T(8,128)(2,1)S(1)}, bf16[64,1024]{1,0:T(8,128)(2,1)S(1)}, u32[]{:S(2)}, u32[]{:S(2)}) collective-permute-start(bf16[64,1024]{1,0:T(8,128)(2,1)S(1)} %get-tuple-element.20), channel_id=1, source_target_pairs={{0,4},{4,0},{8,12},{12,8},{1,5},{5,1},{9,13},{13,9},{2,6},{6,2},{1... | collective-permute-start | bytes 393224 | tf_op jit(solution)/shard_map/ppermute | solution.py:464
  11.5 0.2 collective-permute-start.2
  11.8 0.0 collective-permute-start.3
  11.8 8.2 %collective-permute-done.1.refs_2_ = bf16[64,1024]{1,0:T(8,128)(2,1)S(1)} collective-permute-done((bf16[64,1024]{1,0:T(8,128)(2,1)S(1)}, bf16[64,1024]{1,0:T(8,128)(2,1)S(1)}, u32[]{:S(2)}, u32[]{:S(2)}) %collective-permute-start.1) | collective-permute-done | bytes 131104 | tf_op jit(solution)/shard_map/ppermute | solution.py:464
  20.0 0.5 %collective-permute-start.9 = (bf16[64,1024]{1,0:T(8,128)(2,1)S(1)}, bf16[64,1024]{1,0:T(8,128)(2,1)S(1)}, u32[]{:S(2)}, u32[]{:S(2)}) collective-permute-start(bf16[64,1024]{1,0:T(8,128)(2,1)S(1)} %collective-permute-done.1.refs_2_), channel_id=1, source_target_pairs={{0,2},{2,0},{1,3},{3,1},{4,6},{6,4},{5,7},{7,5},{8,10},{10,8},{9,1... | collective-permute-start | bytes 393224 | tf_op jit(solution)/shard_map/ppermute | solution.py:464
  20.5 0.5 %collective-permute-start.4 = (bf16[64,1024]{1,0:T(8,128)(2,1)S(1)}, bf16[64,1024]{1,0:T(8,128)(2,1)S(1)}, u32[]{:S(2)}, u32[]{:S(2)}) collective-permute-start(bf16[64,1024]{1,0:T(8,128)(2,1)S(1)} %collective-permute-done.refs_1_), channel_id=1, source_target_pairs={{0,1},{1,0},{2,3},{3,2},{4,5},{5,4},{6,7},{7,6},{8,9},{9,8},{10,11... | collective-permute-start | bytes 393224 | tf_op jit(solution)/shard_map/ppermute | solution.py:464
  21.0 1.5 %collective-permute-start.10 = (bf16[64,1024]{1,0:T(8,128)(2,1)S(1)}, bf16[64,1024]{1,0:T(8,128)(2,1)S(1)}, u32[]{:S(2)}, u32[]{:S(2)}) collective-permute-start(bf16[64,1024]{1,0:T(8,128)(2,1)S(1)} %collective-permute-done.2.refs_3_), channel_id=1, source_target_pairs={{0,2},{2,0},{1,3},{3,1},{4,6},{6,4},{5,7},{7,5},{8,10},{10,8},{9,1... | collective-permute-start | bytes 393224 | tf_op jit(solution)/shard_map/ppermute | solution.py:464
  22.5 0.4 %collective-permute-start.8 = (bf16[64,1024]{1,0:T(8,128)(2,1)S(1)}, bf16[64,1024]{1,0:T(8,128)(2,1)S(1)}, u32[]{:S(2)}, u32[]{:S(2)}) collective-permute-start(bf16[64,1024]{1,0:T(8,128)(2,1)S(1)} %get-tuple-element.32), channel_id=1, source_target_pairs={{0,4},{4,0},{8,12},{12,8},{1,5},{5,1},{9,13},{13,9},{2,6},{6,2},{1... | collective-permute-start | bytes 393224 | tf_op jit(solution)/shard_map/ppermute | solution.py:464
  23.0 0.0 collective-permute-done.4.refs_5_
  23.0 0.0 collective-permute-start.6
  23.0 3.2 %collective-permute-done.9.refs_6_ = bf16[64,1024]{1,0:T(8,128)(2,1)S(1)} collective-permute-done((bf16[64,1024]{1,0:T(8,128)(2,1)S(1)}, bf16[64,1024]{1,0:T(8,128)(2,1)S(1)}, u32[]{:S(2)}, u32[]{:S(2)}) %collective-permute-start.9) | collective-permute-done | bytes 131104 | tf_op jit(solution)/shard_map/ppermute | solution.py:464
  26.2 0.0 collective-permute-start.11
  26.2 0.5 %collective-permute-start.13 = (bf16[64,1024]{1,0:T(8,128)(2,1)S(1)}, bf16[64,1024]{1,0:T(8,128)(2,1)S(1)}, u32[]{:S(2)}, u32[]{:S(2)}) collective-permute-start(bf16[64,1024]{1,0:T(8,128)(2,1)S(1)} %collective-permute-done.9.refs_6_), channel_id=1, source_target_pairs={{0,1},{1,0},{2,3},{3,2},{4,5},{5,4},{6,7},{7,6},{8,9},{9,8},{10,11... | collective-permute-start | bytes 393224 | tf_op jit(solution)/shard_map/ppermute | solution.py:464
  26.7 1.0 %collective-permute-done.10.refs_7_ = bf16[64,1024]{1,0:T(8,128)(2,1)S(1)} collective-permute-done((bf16[64,1024]{1,0:T(8,128)(2,1)S(1)}, bf16[64,1024]{1,0:T(8,128)(2,1)S(1)}, u32[]{:S(2)}, u32[]{:S(2)}) %collective-permute-start.10) | collective-permute-done | bytes 131104 | tf_op jit(solution)/shard_map/ppermute | solution.py:464
  27.7 0.0 collective-permute-start.14
  27.7 0.1 collective-permute-done.8.refs_5_
  27.8 0.5 %collective-permute-start.12 = (bf16[64,1024]{1,0:T(8,128)(2,1)S(1)}, bf16[64,1024]{1,0:T(8,128)(2,1)S(1)}, u32[]{:S(2)}, u32[]{:S(2)}) collective-permute-start(bf16[64,1024]{1,0:T(8,128)(2,1)S(1)} %collective-permute-done.8.refs_5_), channel_id=1, source_target_pairs={{0,1},{1,0},{2,3},{3,2},{4,5},{5,4},{6,7},{7,6},{8,9},{9,8},{10,11... | collective-permute-start | bytes 393224 | tf_op jit(solution)/shard_map/ppermute | solution.py:464
  28.2 2.6 %framed_weights.1.weight_ref = bf16[4000,512]{1,0:T(8,128)(2,1)S(1)} custom-call(f32[2,16]{1,0:T(2,128)S(1)} %get-tuple-element.16.table_ref, s32[32,500]{1,0:T(8,128)S(1)} %get-tuple-element.17.index_ref, bf16[64,512]{1,0:T(8,128)(2,1)S(1)} %get-tuple-element.18.copy_ref), custom_call_target="tpu_custom_call" | custom-call | tf_op jit(solution)/shard_map/framed_weights/pallas_call | solution.py:272
  30.9 1.0 %correlate_near.1 = (f32[256,64]{1,0:T(8,128)S(1)}, bf16[8,32,1024]{2,1,0:T(8,128)(2,1)S(1)}, bf16[256,512]{1,0:T(8,128)(2,1)S(1)}, bf16[64,128]{1,0:T(8,128)(2,1)S(1)}) custom-call(bf16[64,1024]{1,0:T(8,128)(2,1)S(1)} %get-tuple-element.19.refs_0_, bf16[64,1024]{1,0:T(8,128)(2,1)S(1)} %collective-permute-done.refs_1_, ...), custom_call_target="tpu_custom_call" | custom-call | tf_op jit(solution)/shard_map/correlate_near/pallas_call | solution.py:351
  31.9 0.0 collective-permute-done.11.refs_8_
  31.9 7.2 %finish.1 = (f32[4000,1024]{1,0:T(8,128)}, f32[256,64]{1,0:T(8,128)}) custom-call(bf16[4000,512]{1,0:T(8,128)(2,1)S(1)} %framed_weights.1.weight_ref, f32[256,64]{1,0:T(8,128)S(1)} %get-tuple-element.23.part_ref, bf16[8,32,1024]{2,1,0:T(8,128)(2,1)S(1)} %get-tuple-element.24.packed, bf16[256,512]{1,0:T(8,128)(2,1)S(1)} %get-tuple-element.25.merge_ref, ...), custom_call_target="tpu_custom_call" | custom-call | tf_op jit(solution)/shard_map/finish/pallas_call | solution.py:445
  (11 shorter events, 0.0 us)
Async XLA Ops:
  4.3 16.6 %collective-permute-start.7 = (bf16[128,1024]{1,0:T(8,128)(2,1)S(1)}, bf16[128,1024]{1,0:T(8,128)(2,1)S(1)}, u32[]{:S(2)}, u32[]{:S(2)}) collective-permute-start(bf16[128,1024]{1,0:T(8,128)(2,1)S(1)} %get-tuple-element.27), channel_id=1, source_target_pairs={{0,2},{2,0},{1,3},{3,1},{4,6},{6,4},{5,7},{7,5},{8,10},{10,8},{9,1... | collective-permute-start | bytes 786440 | tf_op jit(solution)/shard_map/ppermute | solution.py:464
  7.4 12.6 %collective-permute-start.1 = (bf16[64,1024]{1,0:T(8,128)(2,1)S(1)}, bf16[64,1024]{1,0:T(8,128)(2,1)S(1)}, u32[]{:S(2)}, u32[]{:S(2)}) collective-permute-start(bf16[64,1024]{1,0:T(8,128)(2,1)S(1)} %get-tuple-element.21), channel_id=1, source_target_pairs={{0,8},{4,12},{8,0},{12,4},{1,9},{5,13},{9,1},{13,5},{2,10},{6,14},... | collective-permute-start | bytes 393224 | tf_op jit(solution)/shard_map/ppermute | solution.py:464
  10.0 10.5 %collective-permute-start = (bf16[64,1024]{1,0:T(8,128)(2,1)S(1)}, bf16[64,1024]{1,0:T(8,128)(2,1)S(1)}, u32[]{:S(2)}, u32[]{:S(2)}) collective-permute-start(bf16[64,1024]{1,0:T(8,128)(2,1)S(1)} %get-tuple-element.20), channel_id=1, source_target_pairs={{0,4},{4,0},{8,12},{12,8},{1,5},{5,1},{9,13},{13,9},{2,6},{6,2},{1... | collective-permute-start | bytes 393224 | tf_op jit(solution)/shard_map/ppermute | solution.py:464
  11.5 8.9 %collective-permute-start.2 = (bf16[64,1024]{1,0:T(8,128)(2,1)S(1)}, bf16[64,1024]{1,0:T(8,128)(2,1)S(1)}, u32[]{:S(2)}, u32[]{:S(2)}) collective-permute-start(bf16[64,1024]{1,0:T(8,128)(2,1)S(1)} %get-tuple-element.22), channel_id=1, source_target_pairs={{0,12},{4,8},{8,4},{12,0},{1,13},{5,9},{9,5},{13,1},{2,14},{6,10},... | collective-permute-start | bytes 393224 | tf_op jit(solution)/shard_map/ppermute | solution.py:464
  11.8 10.8 %collective-permute-start.3 = (bf16[64,1024]{1,0:T(8,128)(2,1)S(1)}, bf16[64,1024]{1,0:T(8,128)(2,1)S(1)}, u32[]{:S(2)}, u32[]{:S(2)}) collective-permute-start(bf16[64,1024]{1,0:T(8,128)(2,1)S(1)} %get-tuple-element.19.refs_0_), channel_id=1, source_target_pairs={{0,1},{1,0},{2,3},{3,2},{4,5},{5,4},{6,7},{7,6},{8,9},{9,8},{10,11... | collective-permute-start | bytes 393224 | tf_op jit(solution)/shard_map/ppermute | solution.py:464
  20.0 6.3 %collective-permute-start.9 = (bf16[64,1024]{1,0:T(8,128)(2,1)S(1)}, bf16[64,1024]{1,0:T(8,128)(2,1)S(1)}, u32[]{:S(2)}, u32[]{:S(2)}) collective-permute-start(bf16[64,1024]{1,0:T(8,128)(2,1)S(1)} %collective-permute-done.1.refs_2_), channel_id=1, source_target_pairs={{0,2},{2,0},{1,3},{3,1},{4,6},{6,4},{5,7},{7,5},{8,10},{10,8},{9,1... | collective-permute-start | bytes 393224 | tf_op jit(solution)/shard_map/ppermute | solution.py:464
  20.5 5.8 %collective-permute-start.5 = (bf16[64,1024]{1,0:T(8,128)(2,1)S(1)}, bf16[64,1024]{1,0:T(8,128)(2,1)S(1)}, u32[]{:S(2)}, u32[]{:S(2)}) collective-permute-start(bf16[64,1024]{1,0:T(8,128)(2,1)S(1)} %collective-permute-done.1.refs_2_), channel_id=1, source_target_pairs={{0,1},{1,0},{2,3},{3,2},{4,5},{5,4},{6,7},{7,6},{8,9},{9,8},{10,11... | collective-permute-start | bytes 393224 | tf_op jit(solution)/shard_map/ppermute | solution.py:464
  20.5 2.5 %collective-permute-start.4 = (bf16[64,1024]{1,0:T(8,128)(2,1)S(1)}, bf16[64,1024]{1,0:T(8,128)(2,1)S(1)}, u32[]{:S(2)}, u32[]{:S(2)}) collective-permute-start(bf16[64,1024]{1,0:T(8,128)(2,1)S(1)} %collective-permute-done.refs_1_), channel_id=1, source_target_pairs={{0,1},{1,0},{2,3},{3,2},{4,5},{5,4},{6,7},{7,6},{8,9},{9,8},{10,11... | collective-permute-start | bytes 393224 | tf_op jit(solution)/shard_map/ppermute | solution.py:464
  21.0 6.8 %collective-permute-start.10 = (bf16[64,1024]{1,0:T(8,128)(2,1)S(1)}, bf16[64,1024]{1,0:T(8,128)(2,1)S(1)}, u32[]{:S(2)}, u32[]{:S(2)}) collective-permute-start(bf16[64,1024]{1,0:T(8,128)(2,1)S(1)} %collective-permute-done.2.refs_3_), channel_id=1, source_target_pairs={{0,2},{2,0},{1,3},{3,1},{4,6},{6,4},{5,7},{7,5},{8,10},{10,8},{9,1... | collective-permute-start | bytes 393224 | tf_op jit(solution)/shard_map/ppermute | solution.py:464
  22.5 5.3 %collective-permute-start.8 = (bf16[64,1024]{1,0:T(8,128)(2,1)S(1)}, bf16[64,1024]{1,0:T(8,128)(2,1)S(1)}, u32[]{:S(2)}, u32[]{:S(2)}) collective-permute-start(bf16[64,1024]{1,0:T(8,128)(2,1)S(1)} %get-tuple-element.32), channel_id=1, source_target_pairs={{0,4},{4,0},{8,12},{12,8},{1,5},{5,1},{9,13},{13,9},{2,6},{6,2},{1... | collective-permute-start | bytes 393224 | tf_op jit(solution)/shard_map/ppermute | solution.py:464
  23.0 7.9 %collective-permute-start.6 = (bf16[64,1024]{1,0:T(8,128)(2,1)S(1)}, bf16[64,1024]{1,0:T(8,128)(2,1)S(1)}, u32[]{:S(2)}, u32[]{:S(2)}) collective-permute-start(bf16[64,1024]{1,0:T(8,128)(2,1)S(1)} %collective-permute-done.2.refs_3_), channel_id=1, source_target_pairs={{0,1},{1,0},{2,3},{3,2},{4,5},{5,4},{6,7},{7,6},{8,9},{9,8},{10,11... | collective-permute-start | bytes 393224 | tf_op jit(solution)/shard_map/ppermute | solution.py:464
  26.2 5.7 %collective-permute-start.11 = (bf16[64,1024]{1,0:T(8,128)(2,1)S(1)}, bf16[64,1024]{1,0:T(8,128)(2,1)S(1)}, u32[]{:S(2)}, u32[]{:S(2)}) collective-permute-start(bf16[64,1024]{1,0:T(8,128)(2,1)S(1)} %get-tuple-element.33.refs_4_), channel_id=1, source_target_pairs={{0,1},{1,0},{2,3},{3,2},{4,5},{5,4},{6,7},{7,6},{8,9},{9,8},{10,11... | collective-permute-start | bytes 393224 | tf_op jit(solution)/shard_map/ppermute | solution.py:464
  26.2 5.6 %collective-permute-start.13 = (bf16[64,1024]{1,0:T(8,128)(2,1)S(1)}, bf16[64,1024]{1,0:T(8,128)(2,1)S(1)}, u32[]{:S(2)}, u32[]{:S(2)}) collective-permute-start(bf16[64,1024]{1,0:T(8,128)(2,1)S(1)} %collective-permute-done.9.refs_6_), channel_id=1, source_target_pairs={{0,1},{1,0},{2,3},{3,2},{4,5},{5,4},{6,7},{7,6},{8,9},{9,8},{10,11... | collective-permute-start | bytes 393224 | tf_op jit(solution)/shard_map/ppermute | solution.py:464
  27.7 4.1 %collective-permute-start.14 = (bf16[64,1024]{1,0:T(8,128)(2,1)S(1)}, bf16[64,1024]{1,0:T(8,128)(2,1)S(1)}, u32[]{:S(2)}, u32[]{:S(2)}) collective-permute-start(bf16[64,1024]{1,0:T(8,128)(2,1)S(1)} %collective-permute-done.10.refs_7_), channel_id=1, source_target_pairs={{0,1},{1,0},{2,3},{3,2},{4,5},{5,4},{6,7},{7,6},{8,9},{9,8},{10,11... | collective-permute-start | bytes 393224 | tf_op jit(solution)/shard_map/ppermute | solution.py:464
  27.8 4.1 %collective-permute-start.12 = (bf16[64,1024]{1,0:T(8,128)(2,1)S(1)}, bf16[64,1024]{1,0:T(8,128)(2,1)S(1)}, u32[]{:S(2)}, u32[]{:S(2)}) collective-permute-start(bf16[64,1024]{1,0:T(8,128)(2,1)S(1)} %collective-permute-done.8.refs_5_), channel_id=1, source_target_pairs={{0,1},{1,0},{2,3},{3,2},{4,5},{5,4},{6,7},{7,6},{8,9},{9,8},{10,11... | collective-permute-start | bytes 393224 | tf_op jit(solution)/shard_map/ppermute | solution.py:464
